TPU v7x, 256 devices: a whole 4x4x8 slice. The times are simulated.
256 devices in a mesh: kern: 4 (over x_lo, core), tile: 64 (over z, y, x_hi).
Axes of the slice: x: 4 (x_hi: 2, x_lo: 2; x = x_hi * 2 + x_lo), y: 4, z: 8, core: 2. Of those that a mesh axis runs over, the one named last changes fastest.
Arguments:
- mask: int32 [2048, 512], P('tile'), may hold values 0 or 1
- kernels: bfloat16 [24, 2, 64, 64], replicated, may hold values from -0.09375 to 0.09375
- socs_weights: float32 [24], replicated, may hold values from 0.02 to 0.3
- quencher: float32 [2048, 512], P('tile', 'kern'), may hold values from 0.1 to 0.6
Outputs:
- intensity: float32 [2048, 512], P('tile', 'kern')
- acid_final: float32 [2048, 512], P('tile', 'kern')
- base_final: float32 [2048, 512], P('tile', 'kern')
All inputs are finite; a program needn't handle non-finite values. No bound on the sum of `mask` on one device may be relied on, other than what follows from the above.
Results may differ from a plain program's by a relative error of at most 0.0003.
Values sent between devices are 32-bit elements; how exact they have to be, the bound alone decides.
A program may use at most 128 MiB of HBM per device.

v0:
```python
import jax
import jax.numpy as jnp
from jax import lax
from jax.sharding import PartitionSpec as P

STEPS = 8


DIFFUSE_ACID = 0.2
DIFFUSE_BASE = 0.1
QUENCH_RATE = 0.5
EXPOSURE = 0.35


def shifted(value, axis, steps):
    count = lax.axis_size(axis)
    leading, last = (max(0, -steps), min(count, count - steps))
    return lax.ppermute(value, axis, [(source, source + steps) for source in range(leading, last)])


def padded_2(block, sides, width):
    for axis, dim in sides:
        count = lax.axis_size(axis)
        forward = [(i, i + 1) for i in range(count - 1)]
        backward = [(target, source) for source, target in forward]
        low = lax.ppermute(
            lax.slice_in_dim(block, block.shape[dim] - width, None, axis=dim), axis, forward
        )
        high = lax.ppermute(lax.slice_in_dim(block, 0, width, axis=dim), axis, backward)
        block = jnp.concatenate([low, block, high], axis=dim)
    return block


def react(padded):
    middle = padded[:, 1:-1, 1:-1]
    spread = (
        padded[:, :-2, 1:-1]
        + padded[:, 2:, 1:-1]
        + padded[:, 1:-1, :-2]
        + padded[:, 1:-1, 2:]
        - 4.0 * middle
    )
    quenched = QUENCH_RATE * middle[0] * middle[1]
    acid_next = middle[0] + DIFFUSE_ACID * spread[0] - quenched
    base_next = middle[1] + DIFFUSE_BASE * spread[1] - quenched
    return jnp.stack([acid_next, base_next], axis=0)


def band_table(ambit_size):
    tap_ids = lax.iota(jnp.int32, ambit_size)
    input_ids = lax.iota(jnp.int32, 2 * ambit_size)
    output_ids = lax.iota(jnp.int32, ambit_size)
    offsets = input_ids[None, :, None] - output_ids[None, None, :]
    return (offsets == tap_ids[:, None, None]).astype(jnp.bfloat16)


def field_band(mask_rows, kernel_group, ambit_size, edge_rows):
    column_blocks = (mask_rows.shape[1] - ambit_size) // ambit_size
    padded_rows = jnp.pad(mask_rows, ((edge_rows, edge_rows), (0, 0)))
    total_padded = padded_rows.shape[0]
    halves = padded_rows.reshape(total_padded, column_blocks + 1, ambit_size)
    windows = jnp.concatenate([halves[:, :-1], halves[:, 1:]], axis=2)
    band_rows = total_padded - ambit_size
    kernel_count = kernel_group.shape[0]
    selector = band_table(ambit_size)
    accumulated = jnp.zeros((band_rows * column_blocks, kernel_count * 2 * ambit_size), jnp.float32)
    for group_index in range(ambit_size // 8):
        first = group_index * 8
        stacked = jnp.stack(
            [windows[first + offset : first + offset + band_rows] for offset in range(8)], axis=2
        )
        left_side = stacked.reshape(band_rows * column_blocks, 16 * ambit_size)
        taps = kernel_group[:, :, first : first + 8, :]
        banded_taps = jnp.einsum(
            "kprb,bco->rckpo", taps, selector, preferred_element_type=jnp.float32
        ).astype(jnp.bfloat16)
        right_side = banded_taps.reshape(16 * ambit_size, kernel_count * 2 * ambit_size)
        accumulated = accumulated + jnp.dot(
            left_side, right_side, preferred_element_type=jnp.float32
        )
    banded = accumulated.reshape(band_rows, column_blocks, kernel_count, 2, ambit_size)
    banded = jnp.transpose(banded, (2, 3, 0, 1, 4))
    return banded.reshape(kernel_count, 2, band_rows, column_blocks * ambit_size)


def on_device(mask, kernels, socs_weights, quencher):
    ambit_size = kernels.shape[2]
    half_ambit = ambit_size // 2
    kern_count = lax.axis_size("kern")
    kern_index = lax.axis_index("kern")
    local_rows = mask.shape[0]
    padded_mask = jnp.pad(mask.astype(jnp.bfloat16), ((0, 0), (half_ambit, half_ambit)))
    per_group = kernels.shape[0] // kern_count
    own_kernels = lax.dynamic_slice_in_dim(kernels, kern_index * per_group, per_group, 0)
    own_weights = lax.dynamic_slice_in_dim(socs_weights, kern_index * per_group, per_group, 0)
    fields = field_band(padded_mask, own_kernels, ambit_size, ambit_size)
    upper_rim = fields[:, :, :half_ambit]
    lower_rim = fields[:, :, local_rows + half_ambit :]
    centre = fields[:, :, half_ambit : local_rows + half_ambit]
    from_above = shifted(lower_rim, "tile", 1)
    from_below = shifted(upper_rim, "tile", -1)
    centre = centre + from_above
    centre = centre + from_below
    squared = centre[:, 0] * centre[:, 0] + centre[:, 1] * centre[:, 1]
    partial_value = jnp.sum(own_weights[:, None, None] * squared, axis=0)
    intensity = lax.psum_scatter(partial_value, "kern", scatter_dimension=1, tiled=True)
    acid = 1.0 - jnp.exp(-EXPOSURE * intensity)
    resist_state = jnp.stack([acid, quencher], axis=0)
    for step_index in range(STEPS):
        resist_state = react(padded_2(resist_state, (("kern", 2), ("tile", 1)), 1))
    return (intensity, resist_state[0], resist_state[1])


def solution(mesh):
    placed = (P("tile", None), P(), P(), P("tile", "kern"))
    return jax.shard_map(
        on_device,
        mesh=mesh,
        in_specs=placed,
        out_specs=(P("tile", "kern"), P("tile", "kern"), P("tile", "kern")),
        check_vma=False,
    )
```

profile of v0, /device:TPU:129, one launch (start us, length us, event | category | flops | bytes accessed | tf_op | source)
XLA Modules:
  0.0 354.1 jit_solution(12195451275094378345)
XLA Ops:
  22.2 3.9 %copy.340 = bf16[96,8,8,128]{3,2,1,0:T(8,128)(2,1)} copy(bf16[96,8,8,128]{0,3,1,2:T(8,128)(2,1)} %copy-done.8) | data formatting | bytes 3145728 | tf_op jit(solution)/shard_map/stack | solution.py:69
  28.9 3.9 %copy.342 = bf16[96,8,8,128]{3,2,1,0:T(8,128)(2,1)} copy(bf16[96,8,8,128]{0,3,1,2:T(8,128)(2,1)} %copy-done.9) | data formatting | bytes 3145728 | tf_op jit(solution)/shard_map/stack | solution.py:69
  34.9 3.9 %copy.338 = bf16[96,8,8,128]{3,2,1,0:T(8,128)(2,1)} copy(bf16[96,8,8,128]{0,3,1,2:T(8,128)(2,1)} %copy-done.7) | data formatting | bytes 3145728 | tf_op jit(solution)/shard_map/stack | solution.py:69
  40.9 3.9 %copy.336 = bf16[96,8,8,128]{3,2,1,0:T(8,128)(2,1)} copy(bf16[96,8,8,128]{0,3,1,2:T(8,128)(2,1)} %copy-done.6) | data formatting | bytes 3145728 | tf_op jit(solution)/shard_map/stack | solution.py:69
  47.0 3.9 %copy.334 = bf16[96,8,8,128]{3,2,1,0:T(8,128)(2,1)} copy(bf16[96,8,8,128]{0,3,1,2:T(8,128)(2,1)} %copy-done.5) | data formatting | bytes 3145728 | tf_op jit(solution)/shard_map/stack | solution.py:69
  53.1 3.9 %copy.332 = bf16[96,8,8,128]{3,2,1,0:T(8,128)(2,1)} copy(bf16[96,8,8,128]{0,3,1,2:T(8,128)(2,1)} %copy-done.4) | data formatting | bytes 3145728 | tf_op jit(solution)/shard_map/stack | solution.py:69
  59.2 3.9 %copy.330 = bf16[96,8,8,128]{3,2,1,0:T(8,128)(2,1)} copy(bf16[96,8,8,128]{0,3,1,2:T(8,128)(2,1)} %copy-done.10) | data formatting | bytes 3145728 | tf_op jit(solution)/shard_map/stack | solution.py:69
  65.2 3.9 %copy.328 = bf16[96,8,8,128]{3,2,1,0:T(8,128)(2,1)} copy(bf16[96,8,8,128]{0,3,1,2:T(8,128)(2,1)} %copy-done.11) | data formatting | bytes 3145728 | tf_op jit(solution)/shard_map/stack | solution.py:69
  85.6 4.4 %reshape.131 = f32[96,8,6,2,64]{4,3,2,1,0:T(2,128)} reshape(f32[768,768]{1,0:T(8,128)S(1)} %add_add_fusion) | data formatting | bytes 4718592 | tf_op jit(solution)/shard_map/reshape | solution.py:81
  90.0 5.5 %copy.344 = f32[6,2,96,8,64]{2,4,3,1,0:T(8,128)S(1)} copy(f32[6,2,96,8,64]{4,1,0,3,2:T(2,128)} %bitcast.563) | data formatting | bytes 4718592 | tf_op jit(solution)/shard_map/transpose | solution.py:82
  95.5 5.6 %fusion.425 = (f32[6,2,32,512]{2,3,1,0:T(8,128)}, f32[6,2,32,512]{2,3,1,0:T(8,128)}, f32[6,2,32,512]{2,3,1,0:T(8,128)}) fusion(f32[6,2,96,512]{2,3,1,0:T(8,128)S(1)} %bitcast.562), kind=kLoop, calls=%fused_computation.691 | loop fusion | bytes 4718592 | tf_op jit(solution)/shard_map/slice | solution.py:98
  101.2 3.1 copy.346
  104.3 4.9 %collective-permute-start = (f32[6,2,32,512]{3,2,1,0:T(8,128)}, f32[6,2,32,512]{3,2,1,0:T(8,128)}, u32[]{:S(2)}, u32[]{:S(2)}) collective-permute-start(f32[6,2,32,512]{3,2,1,0:T(8,128)} %copy.346), channel_id=1, source_target_pairs={{0,1},{1,2},{2,3},{3,4},{4,5},{5,6},{6,7},{7,8},{8,9},{9,10},{10,1... | collective-permute-start | bytes 2359304 | tf_op jit(solution)/shard_map/ppermute | solution.py:18
  109.2 3.1 copy.347
  112.3 6.5 %collective-permute-start.1 = (f32[6,2,32,512]{3,2,1,0:T(8,128)}, f32[6,2,32,512]{3,2,1,0:T(8,128)}, u32[]{:S(2)}, u32[]{:S(2)}) collective-permute-start(f32[6,2,32,512]{3,2,1,0:T(8,128)} %copy.347), channel_id=1, source_target_pairs={{1,0},{2,1},{3,2},{4,3},{5,4},{6,5},{7,6},{8,7},{9,8},{10,9},{11,1... | collective-permute-start | bytes 2359304 | tf_op jit(solution)/shard_map/ppermute | solution.py:18
  121.0 21.5 %collective-permute-done = f32[6,2,32,512]{3,2,1,0:T(8,128)} collective-permute-done((f32[6,2,32,512]{3,2,1,0:T(8,128)}, f32[6,2,32,512]{3,2,1,0:T(8,128)}, u32[]{:S(2)}, u32[]{:S(2)}) %collective-permute-start) | collective-permute-done | bytes 786464 | tf_op jit(solution)/shard_map/ppermute | solution.py:18
  147.5 22.5 %reduce-scatter.2.cloned.1.call-done = f32[32,128]{0,1:T(8,128)} async-done(((f32[32,512]{0,1:T(8,128)}), f32[32,128]{0,1:T(8,128)}) %reduce-scatter.2.cloned.1.call-update) | async-done | bytes 16400 | tf_op jit(solution)/shard_map/reduce_scatter | solution.py:106
  175.1 2.7 collective-permute-done.3
  178.0 4.6 %collective-permute-start.4 = (f32[2,1,130]{1,2,0:T(8,128)S(1)}, f32[2,1,130]{1,2,0:T(8,128)S(1)}, u32[]{:S(2)}, u32[]{:S(2)}) collective-permute-start(f32[2,1,130]{1,2,0:T(8,128)S(1)} %get-tuple-element.91), channel_id=1, source_target_pairs={{0,1},{1,2},{2,3},{3,4},{4,5},{5,6},{6,7},{7,8},{8,9},{9,10},{10,1... | collective-permute-start | bytes 3128 | tf_op jit(solution)/shard_map/ppermute | solution.py:26
  182.6 6.4 %collective-permute-start.5 = (f32[2,1,130]{1,2,0:T(8,128)S(1)}, f32[2,1,130]{1,2,0:T(8,128)S(1)}, u32[]{:S(2)}, u32[]{:S(2)}) collective-permute-start(f32[2,1,130]{1,2,0:T(8,128)S(1)} %get-tuple-element.92), channel_id=1, source_target_pairs={{1,0},{2,1},{3,2},{4,3},{5,4},{6,5},{7,6},{8,7},{9,8},{10,9},{11,1... | collective-permute-start | bytes 3128 | tf_op jit(solution)/shard_map/ppermute | solution.py:29
  197.2 2.9 collective-permute-done.7
  200.2 3.8 %collective-permute-start.8 = (f32[2,1,130]{1,2,0:T(8,128)S(1)}, f32[2,1,130]{1,2,0:T(8,128)S(1)}, u32[]{:S(2)}, u32[]{:S(2)}) collective-permute-start(f32[2,1,130]{1,2,0:T(8,128)S(1)} %get-tuple-element.89), channel_id=1, source_target_pairs={{0,1},{1,2},{2,3},{3,4},{4,5},{5,6},{6,7},{7,8},{8,9},{9,10},{10,1... | collective-permute-start | bytes 3128 | tf_op jit(solution)/shard_map/ppermute | solution.py:26
  204.0 8.5 %collective-permute-start.9 = (f32[2,1,130]{1,2,0:T(8,128)S(1)}, f32[2,1,130]{1,2,0:T(8,128)S(1)}, u32[]{:S(2)}, u32[]{:S(2)}) collective-permute-start(f32[2,1,130]{1,2,0:T(8,128)S(1)} %get-tuple-element.90), channel_id=1, source_target_pairs={{1,0},{2,1},{3,2},{4,3},{5,4},{6,5},{7,6},{8,7},{9,8},{10,9},{11,1... | collective-permute-start | bytes 3128 | tf_op jit(solution)/shard_map/ppermute | solution.py:29
  224.0 10.5 %collective-permute-start.13 = (f32[2,1,130]{1,2,0:T(8,128)S(1)}, f32[2,1,130]{1,2,0:T(8,128)S(1)}, u32[]{:S(2)}, u32[]{:S(2)}) collective-permute-start(f32[2,1,130]{1,2,0:T(8,128)S(1)} %get-tuple-element.88), channel_id=1, source_target_pairs={{1,0},{2,1},{3,2},{4,3},{5,4},{6,5},{7,6},{8,7},{9,8},{10,9},{11,1... | collective-permute-start | bytes 3128 | tf_op jit(solution)/shard_map/ppermute | solution.py:29
  245.8 10.4 %collective-permute-start.17 = (f32[2,1,130]{1,2,0:T(8,128)S(1)}, f32[2,1,130]{1,2,0:T(8,128)S(1)}, u32[]{:S(2)}, u32[]{:S(2)}) collective-permute-start(f32[2,1,130]{1,2,0:T(8,128)S(1)} %get-tuple-element.86), channel_id=1, source_target_pairs={{1,0},{2,1},{3,2},{4,3},{5,4},{6,5},{7,6},{8,7},{9,8},{10,9},{11,1... | collective-permute-start | bytes 3128 | tf_op jit(solution)/shard_map/ppermute | solution.py:29
  262.9 2.7 collective-permute-done.19
  267.6 10.4 %collective-permute-start.21 = (f32[2,1,130]{1,2,0:T(8,128)S(1)}, f32[2,1,130]{1,2,0:T(8,128)S(1)}, u32[]{:S(2)}, u32[]{:S(2)}) collective-permute-start(f32[2,1,130]{1,2,0:T(8,128)S(1)} %get-tuple-element.84), channel_id=1, source_target_pairs={{1,0},{2,1},{3,2},{4,3},{5,4},{6,5},{7,6},{8,7},{9,8},{10,9},{11,1... | collective-permute-start | bytes 3128 | tf_op jit(solution)/shard_map/ppermute | solution.py:29
  284.7 2.7 collective-permute-done.23
  289.4 10.4 %collective-permute-start.25 = (f32[2,1,130]{1,2,0:T(8,128)S(1)}, f32[2,1,130]{1,2,0:T(8,128)S(1)}, u32[]{:S(2)}, u32[]{:S(2)}) collective-permute-start(f32[2,1,130]{1,2,0:T(8,128)S(1)} %get-tuple-element.82), channel_id=1, source_target_pairs={{1,0},{2,1},{3,2},{4,3},{5,4},{6,5},{7,6},{8,7},{9,8},{10,9},{11,1... | collective-permute-start | bytes 3128 | tf_op jit(solution)/shard_map/ppermute | solution.py:29
  311.4 10.4 %collective-permute-start.29 = (f32[2,1,130]{1,2,0:T(8,128)S(1)}, f32[2,1,130]{1,2,0:T(8,128)S(1)}, u32[]{:S(2)}, u32[]{:S(2)}) collective-permute-start(f32[2,1,130]{1,2,0:T(8,128)S(1)} %get-tuple-element.80), channel_id=1, source_target_pairs={{1,0},{2,1},{3,2},{4,3},{5,4},{6,5},{7,6},{8,7},{9,8},{10,9},{11,1... | collective-permute-start | bytes 3128 | tf_op jit(solution)/shard_map/ppermute | solution.py:29
  328.5 2.7 collective-permute-done.31
  333.2 10.4 %collective-permute-start.33 = (f32[2,1,130]{1,2,0:T(8,128)S(1)}, f32[2,1,130]{1,2,0:T(8,128)S(1)}, u32[]{:S(2)}, u32[]{:S(2)}) collective-permute-start(f32[2,1,130]{1,2,0:T(8,128)S(1)} %get-tuple-element.78), channel_id=1, source_target_pairs={{1,0},{2,1},{3,2},{4,3},{5,4},{6,5},{7,6},{8,7},{9,8},{10,9},{11,1... | collective-permute-start | bytes 3128 | tf_op jit(solution)/shard_map/ppermute | solution.py:29
  (224 shorter events, 130.9 us)
Async XLA Ops:
  7.2 162.7 %reduce-scatter.2.cloned.1.call-start = ((), (), s32[]{:S(2)}) async-start(), calls=%async_computation.1 | async-start | bytes 327680 | tf_op jit(solution)/shard_map/reduce_scatter | solution.py:106
  104.3 38.2 %collective-permute-start = (f32[6,2,32,512]{3,2,1,0:T(8,128)}, f32[6,2,32,512]{3,2,1,0:T(8,128)}, u32[]{:S(2)}, u32[]{:S(2)}) collective-permute-start(f32[6,2,32,512]{3,2,1,0:T(8,128)} %copy.346), channel_id=1, source_target_pairs={{0,1},{1,2},{2,3},{3,4},{4,5},{5,6},{6,7},{7,8},{8,9},{9,10},{10,1... | collective-permute-start | bytes 2359304 | tf_op jit(solution)/shard_map/ppermute | solution.py:18
  112.3 32.2 %collective-permute-start.1 = (f32[6,2,32,512]{3,2,1,0:T(8,128)}, f32[6,2,32,512]{3,2,1,0:T(8,128)}, u32[]{:S(2)}, u32[]{:S(2)}) collective-permute-start(f32[6,2,32,512]{3,2,1,0:T(8,128)} %copy.347), channel_id=1, source_target_pairs={{1,0},{2,1},{3,2},{4,3},{5,4},{6,5},{7,6},{8,7},{9,8},{10,9},{11,1... | collective-permute-start | bytes 2359304 | tf_op jit(solution)/shard_map/ppermute | solution.py:18
  170.8 4.3 %collective-permute-start.2 = (f32[2,32,1]{1,2,0:T(1,128)S(1)}, f32[2,32,1]{1,2,0:T(1,128)S(1)}, u32[]{:S(2)}, u32[]{:S(2)}) collective-permute-start(f32[2,32,1]{1,2,0:T(1,128)S(1)} %get-tuple-element.107), channel_id=1, source_target_pairs={{0,64},{64,128},{128,192},{1,65},{65,129},{129,193},{2,66},{66,130... | collective-permute-start | bytes 776 | tf_op jit(solution)/shard_map/ppermute | solution.py:26
  173.0 4.9 %collective-permute-start.3 = (f32[2,32,1]{1,2,0:T(1,128)S(1)}, f32[2,32,1]{1,2,0:T(1,128)S(1)}, u32[]{:S(2)}, u32[]{:S(2)}) collective-permute-start(f32[2,32,1]{1,2,0:T(1,128)S(1)} %get-tuple-element.108), channel_id=1, source_target_pairs={{64,0},{128,64},{192,128},{65,1},{129,65},{193,129},{66,2},{130,66... | collective-permute-start | bytes 776 | tf_op jit(solution)/shard_map/ppermute | solution.py:29
  178.0 11.9 %collective-permute-start.4 = (f32[2,1,130]{1,2,0:T(8,128)S(1)}, f32[2,1,130]{1,2,0:T(8,128)S(1)}, u32[]{:S(2)}, u32[]{:S(2)}) collective-permute-start(f32[2,1,130]{1,2,0:T(8,128)S(1)} %get-tuple-element.91), channel_id=1, source_target_pairs={{0,1},{1,2},{2,3},{3,4},{4,5},{5,6},{6,7},{7,8},{8,9},{9,10},{10,1... | collective-permute-start | bytes 3128 | tf_op jit(solution)/shard_map/ppermute | solution.py:26
  182.6 9.0 %collective-permute-start.5 = (f32[2,1,130]{1,2,0:T(8,128)S(1)}, f32[2,1,130]{1,2,0:T(8,128)S(1)}, u32[]{:S(2)}, u32[]{:S(2)}) collective-permute-start(f32[2,1,130]{1,2,0:T(8,128)S(1)} %get-tuple-element.92), channel_id=1, source_target_pairs={{1,0},{2,1},{3,2},{4,3},{5,4},{6,5},{7,6},{8,7},{9,8},{10,9},{11,1... | collective-permute-start | bytes 3128 | tf_op jit(solution)/shard_map/ppermute | solution.py:29
  192.7 4.5 %collective-permute-start.6 = (f32[2,32,1]{1,2,0:T(1,128)S(1)}, f32[2,32,1]{1,2,0:T(1,128)S(1)}, u32[]{:S(2)}, u32[]{:S(2)}) collective-permute-start(f32[2,32,1]{1,2,0:T(1,128)S(1)} %get-tuple-element.105), channel_id=1, source_target_pairs={{0,64},{64,128},{128,192},{1,65},{65,129},{129,193},{2,66},{66,130... | collective-permute-start | bytes 776 | tf_op jit(solution)/shard_map/ppermute | solution.py:26
  195.2 4.9 %collective-permute-start.7 = (f32[2,32,1]{1,2,0:T(1,128)S(1)}, f32[2,32,1]{1,2,0:T(1,128)S(1)}, u32[]{:S(2)}, u32[]{:S(2)}) collective-permute-start(f32[2,32,1]{1,2,0:T(1,128)S(1)} %get-tuple-element.106), channel_id=1, source_target_pairs={{64,0},{128,64},{192,128},{65,1},{129,65},{193,129},{66,2},{130,66... | collective-permute-start | bytes 776 | tf_op jit(solution)/shard_map/ppermute | solution.py:29
  200.2 13.0 %collective-permute-start.8 = (f32[2,1,130]{1,2,0:T(8,128)S(1)}, f32[2,1,130]{1,2,0:T(8,128)S(1)}, u32[]{:S(2)}, u32[]{:S(2)}) collective-permute-start(f32[2,1,130]{1,2,0:T(8,128)S(1)} %get-tuple-element.89), channel_id=1, source_target_pairs={{0,1},{1,2},{2,3},{3,4},{4,5},{5,6},{6,7},{7,8},{8,9},{9,10},{10,1... | collective-permute-start | bytes 3128 | tf_op jit(solution)/shard_map/ppermute | solution.py:26
  204.0 10.6 %collective-permute-start.9 = (f32[2,1,130]{1,2,0:T(8,128)S(1)}, f32[2,1,130]{1,2,0:T(8,128)S(1)}, u32[]{:S(2)}, u32[]{:S(2)}) collective-permute-start(f32[2,1,130]{1,2,0:T(8,128)S(1)} %get-tuple-element.90), channel_id=1, source_target_pairs={{1,0},{2,1},{3,2},{4,3},{5,4},{6,5},{7,6},{8,7},{9,8},{10,9},{11,1... | collective-permute-start | bytes 3128 | tf_op jit(solution)/shard_map/ppermute | solution.py:29
  214.9 4.3 %collective-permute-start.10 = (f32[2,32,1]{1,2,0:T(1,128)S(1)}, f32[2,32,1]{1,2,0:T(1,128)S(1)}, u32[]{:S(2)}, u32[]{:S(2)}) collective-permute-start(f32[2,32,1]{1,2,0:T(1,128)S(1)} %get-tuple-element.103), channel_id=1, source_target_pairs={{0,64},{64,128},{128,192},{1,65},{65,129},{129,193},{2,66},{66,130... | collective-permute-start | bytes 776 | tf_op jit(solution)/shard_map/ppermute | solution.py:26
  217.0 4.9 %collective-permute-start.11 = (f32[2,32,1]{1,2,0:T(1,128)S(1)}, f32[2,32,1]{1,2,0:T(1,128)S(1)}, u32[]{:S(2)}, u32[]{:S(2)}) collective-permute-start(f32[2,32,1]{1,2,0:T(1,128)S(1)} %get-tuple-element.104), channel_id=1, source_target_pairs={{64,0},{128,64},{192,128},{65,1},{129,65},{193,129},{66,2},{130,66... | collective-permute-start | bytes 776 | tf_op jit(solution)/shard_map/ppermute | solution.py:29
  222.0 13.0 %collective-permute-start.12 = (f32[2,1,130]{1,2,0:T(8,128)S(1)}, f32[2,1,130]{1,2,0:T(8,128)S(1)}, u32[]{:S(2)}, u32[]{:S(2)}) collective-permute-start(f32[2,1,130]{1,2,0:T(8,128)S(1)} %get-tuple-element.87), channel_id=1, source_target_pairs={{0,1},{1,2},{2,3},{3,4},{4,5},{5,6},{6,7},{7,8},{8,9},{9,10},{10,1... | collective-permute-start | bytes 3128 | tf_op jit(solution)/shard_map/ppermute | solution.py:26
  224.0 12.5 %collective-permute-start.13 = (f32[2,1,130]{1,2,0:T(8,128)S(1)}, f32[2,1,130]{1,2,0:T(8,128)S(1)}, u32[]{:S(2)}, u32[]{:S(2)}) collective-permute-start(f32[2,1,130]{1,2,0:T(8,128)S(1)} %get-tuple-element.88), channel_id=1, source_target_pairs={{1,0},{2,1},{3,2},{4,3},{5,4},{6,5},{7,6},{8,7},{9,8},{10,9},{11,1... | collective-permute-start | bytes 3128 | tf_op jit(solution)/shard_map/ppermute | solution.py:29
  236.7 4.3 %collective-permute-start.14 = (f32[2,32,1]{1,2,0:T(1,128)S(1)}, f32[2,32,1]{1,2,0:T(1,128)S(1)}, u32[]{:S(2)}, u32[]{:S(2)}) collective-permute-start(f32[2,32,1]{1,2,0:T(1,128)S(1)} %get-tuple-element.101), channel_id=1, source_target_pairs={{0,64},{64,128},{128,192},{1,65},{65,129},{129,193},{2,66},{66,130... | collective-permute-start | bytes 776 | tf_op jit(solution)/shard_map/ppermute | solution.py:26
  238.8 4.9 %collective-permute-start.15 = (f32[2,32,1]{1,2,0:T(1,128)S(1)}, f32[2,32,1]{1,2,0:T(1,128)S(1)}, u32[]{:S(2)}, u32[]{:S(2)}) collective-permute-start(f32[2,32,1]{1,2,0:T(1,128)S(1)} %get-tuple-element.102), channel_id=1, source_target_pairs={{64,0},{128,64},{192,128},{65,1},{129,65},{193,129},{66,2},{130,66... | collective-permute-start | bytes 776 | tf_op jit(solution)/shard_map/ppermute | solution.py:29
  243.9 12.9 %collective-permute-start.16 = (f32[2,1,130]{1,2,0:T(8,128)S(1)}, f32[2,1,130]{1,2,0:T(8,128)S(1)}, u32[]{:S(2)}, u32[]{:S(2)}) collective-permute-start(f32[2,1,130]{1,2,0:T(8,128)S(1)} %get-tuple-element.85), channel_id=1, source_target_pairs={{0,1},{1,2},{2,3},{3,4},{4,5},{5,6},{6,7},{7,8},{8,9},{9,10},{10,1... | collective-permute-start | bytes 3128 | tf_op jit(solution)/shard_map/ppermute | solution.py:26
  245.8 12.5 %collective-permute-start.17 = (f32[2,1,130]{1,2,0:T(8,128)S(1)}, f32[2,1,130]{1,2,0:T(8,128)S(1)}, u32[]{:S(2)}, u32[]{:S(2)}) collective-permute-start(f32[2,1,130]{1,2,0:T(8,128)S(1)} %get-tuple-element.86), channel_id=1, source_target_pairs={{1,0},{2,1},{3,2},{4,3},{5,4},{6,5},{7,6},{8,7},{9,8},{10,9},{11,1... | collective-permute-start | bytes 3128 | tf_op jit(solution)/shard_map/ppermute | solution.py:29
  260.7 4.9 %collective-permute-start.19 = (f32[2,32,1]{1,2,0:T(1,128)S(1)}, f32[2,32,1]{1,2,0:T(1,128)S(1)}, u32[]{:S(2)}, u32[]{:S(2)}) collective-permute-start(f32[2,32,1]{1,2,0:T(1,128)S(1)} %get-tuple-element.100), channel_id=1, source_target_pairs={{64,0},{128,64},{192,128},{65,1},{129,65},{193,129},{66,2},{130,66... | collective-permute-start | bytes 776 | tf_op jit(solution)/shard_map/ppermute | solution.py:29
  265.7 12.9 %collective-permute-start.20 = (f32[2,1,130]{1,2,0:T(8,128)S(1)}, f32[2,1,130]{1,2,0:T(8,128)S(1)}, u32[]{:S(2)}, u32[]{:S(2)}) collective-permute-start(f32[2,1,130]{1,2,0:T(8,128)S(1)} %get-tuple-element.83), channel_id=1, source_target_pairs={{0,1},{1,2},{2,3},{3,4},{4,5},{5,6},{6,7},{7,8},{8,9},{9,10},{10,1... | collective-permute-start | bytes 3128 | tf_op jit(solution)/shard_map/ppermute | solution.py:26
  267.6 12.5 %collective-permute-start.21 = (f32[2,1,130]{1,2,0:T(8,128)S(1)}, f32[2,1,130]{1,2,0:T(8,128)S(1)}, u32[]{:S(2)}, u32[]{:S(2)}) collective-permute-start(f32[2,1,130]{1,2,0:T(8,128)S(1)} %get-tuple-element.84), channel_id=1, source_target_pairs={{1,0},{2,1},{3,2},{4,3},{5,4},{6,5},{7,6},{8,7},{9,8},{10,9},{11,1... | collective-permute-start | bytes 3128 | tf_op jit(solution)/shard_map/ppermute | solution.py:29
  282.5 4.9 %collective-permute-start.23 = (f32[2,32,1]{1,2,0:T(1,128)S(1)}, f32[2,32,1]{1,2,0:T(1,128)S(1)}, u32[]{:S(2)}, u32[]{:S(2)}) collective-permute-start(f32[2,32,1]{1,2,0:T(1,128)S(1)} %get-tuple-element.98), channel_id=1, source_target_pairs={{64,0},{128,64},{192,128},{65,1},{129,65},{193,129},{66,2},{130,66... | collective-permute-start | bytes 776 | tf_op jit(solution)/shard_map/ppermute | solution.py:29
  287.5 12.9 %collective-permute-start.24 = (f32[2,1,130]{1,2,0:T(8,128)S(1)}, f32[2,1,130]{1,2,0:T(8,128)S(1)}, u32[]{:S(2)}, u32[]{:S(2)}) collective-permute-start(f32[2,1,130]{1,2,0:T(8,128)S(1)} %get-tuple-element.81), channel_id=1, source_target_pairs={{0,1},{1,2},{2,3},{3,4},{4,5},{5,6},{6,7},{7,8},{8,9},{9,10},{10,1... | collective-permute-start | bytes 3128 | tf_op jit(solution)/shard_map/ppermute | solution.py:26
  289.4 12.5 %collective-permute-start.25 = (f32[2,1,130]{1,2,0:T(8,128)S(1)}, f32[2,1,130]{1,2,0:T(8,128)S(1)}, u32[]{:S(2)}, u32[]{:S(2)}) collective-permute-start(f32[2,1,130]{1,2,0:T(8,128)S(1)} %get-tuple-element.82), channel_id=1, source_target_pairs={{1,0},{2,1},{3,2},{4,3},{5,4},{6,5},{7,6},{8,7},{9,8},{10,9},{11,1... | collective-permute-start | bytes 3128 | tf_op jit(solution)/shard_map/ppermute | solution.py:29
  302.2 4.5 %collective-permute-start.26 = (f32[2,32,1]{1,2,0:T(1,128)S(1)}, f32[2,32,1]{1,2,0:T(1,128)S(1)}, u32[]{:S(2)}, u32[]{:S(2)}) collective-permute-start(f32[2,32,1]{1,2,0:T(1,128)S(1)} %get-tuple-element.95), channel_id=1, source_target_pairs={{0,64},{64,128},{128,192},{1,65},{65,129},{129,193},{2,66},{66,130... | collective-permute-start | bytes 776 | tf_op jit(solution)/shard_map/ppermute | solution.py:26
  304.4 4.9 %collective-permute-start.27 = (f32[2,32,1]{1,2,0:T(1,128)S(1)}, f32[2,32,1]{1,2,0:T(1,128)S(1)}, u32[]{:S(2)}, u32[]{:S(2)}) collective-permute-start(f32[2,32,1]{1,2,0:T(1,128)S(1)} %get-tuple-element.96), channel_id=1, source_target_pairs={{64,0},{128,64},{192,128},{65,1},{129,65},{193,129},{66,2},{130,66... | collective-permute-start | bytes 776 | tf_op jit(solution)/shard_map/ppermute | solution.py:29
  309.5 12.9 %collective-permute-start.28 = (f32[2,1,130]{1,2,0:T(8,128)S(1)}, f32[2,1,130]{1,2,0:T(8,128)S(1)}, u32[]{:S(2)}, u32[]{:S(2)}) collective-permute-start(f32[2,1,130]{1,2,0:T(8,128)S(1)} %get-tuple-element.79), channel_id=1, source_target_pairs={{0,1},{1,2},{2,3},{3,4},{4,5},{5,6},{6,7},{7,8},{8,9},{9,10},{10,1... | collective-permute-start | bytes 3128 | tf_op jit(solution)/shard_map/ppermute | solution.py:26
  311.4 12.5 %collective-permute-start.29 = (f32[2,1,130]{1,2,0:T(8,128)S(1)}, f32[2,1,130]{1,2,0:T(8,128)S(1)}, u32[]{:S(2)}, u32[]{:S(2)}) collective-permute-start(f32[2,1,130]{1,2,0:T(8,128)S(1)} %get-tuple-element.80), channel_id=1, source_target_pairs={{1,0},{2,1},{3,2},{4,3},{5,4},{6,5},{7,6},{8,7},{9,8},{10,9},{11,1... | collective-permute-start | bytes 3128 | tf_op jit(solution)/shard_map/ppermute | solution.py:29
  326.3 4.9 %collective-permute-start.31 = (f32[2,32,1]{1,2,0:T(1,128)S(1)}, f32[2,32,1]{1,2,0:T(1,128)S(1)}, u32[]{:S(2)}, u32[]{:S(2)}) collective-permute-start(f32[2,32,1]{1,2,0:T(1,128)S(1)} %get-tuple-element.94), channel_id=1, source_target_pairs={{64,0},{128,64},{192,128},{65,1},{129,65},{193,129},{66,2},{130,66... | collective-permute-start | bytes 776 | tf_op jit(solution)/shard_map/ppermute | solution.py:29
  331.3 13.0 %collective-permute-start.32 = (f32[2,1,130]{1,2,0:T(8,128)S(1)}, f32[2,1,130]{1,2,0:T(8,128)S(1)}, u32[]{:S(2)}, u32[]{:S(2)}) collective-permute-start(f32[2,1,130]{1,2,0:T(8,128)S(1)} %get-tuple-element.77), channel_id=1, source_target_pairs={{0,1},{1,2},{2,3},{3,4},{4,5},{5,6},{6,7},{7,8},{8,9},{9,10},{10,1... | collective-permute-start | bytes 3128 | tf_op jit(solution)/shard_map/ppermute | solution.py:26
  333.2 12.5 %collective-permute-start.33 = (f32[2,1,130]{1,2,0:T(8,128)S(1)}, f32[2,1,130]{1,2,0:T(8,128)S(1)}, u32[]{:S(2)}, u32[]{:S(2)}) collective-permute-start(f32[2,1,130]{1,2,0:T(8,128)S(1)} %get-tuple-element.78), channel_id=1, source_target_pairs={{1,0},{2,1},{3,2},{4,3},{5,4},{6,5},{7,6},{8,7},{9,8},{10,9},{11,1... | collective-permute-start | bytes 3128 | tf_op jit(solution)/shard_map/ppermute | solution.py:29
  (32 other events, 219.3 us)
Sparse Core Ops, SparseCore 0:
  147.5 22.4 reduce-scatter.1
where the time goes:
time: 359 us; the launch traced here: 354 us
  starting transfers between devices  144 us (40%)
  waiting for transfers between devices  84.1 us (23%)
  local copies, waits for them, and re-layouts  78 us (22%)
  other arithmetic  16.5 us (5%)
  matrix products  16.5 us (5%)
  between operations  15.2 us (4%)
    ppermute x16, starting transfers between devices, padded_2(): lax.ppermute(lax.slice_in_dim(block, 0, width, axis=dim), axis, backward)  94.9 us
    ppermute x16, starting transfers between devices, padded_2(): lax.ppermute(lax.slice_in_dim(block, block.shape[dim] - width, None, axis...  37.4 us
    ppermute x16, waiting for transfers between devices, padded_2(): lax.ppermute(lax.slice_in_dim(block, 0, width, axis=dim), axis, backward)  34.1 us
    another operation x8, local copies, waits for them, and re-layouts, field_band(): jnp.stack([windows[first + offset:first + offset + band_rows] for offset...  31.3 us
    ppermute x2, waiting for transfers between devices, shifted(): lax.ppermute(value, axis, [(source, source + steps) for source in range(l...  23.5 us
    reduce_scatter x1, waiting for transfers between devices, on_device(): lax.psum_scatter(partial_value, 'kern', scatter_dimension=1, tiled=True)  22.5 us
    unnamed x65, local copies, waits for them, and re-layouts  12.8 us
    dot_general x8, matrix products, field_band(): jnp.dot(left_side, right_side, preferred_element_type=jnp.float32)  11.9 us
  transfers between devices with their start and end apart: 35, of which 26 were waited for; matrix products, arithmetic and copies ran while one was open for 2% of the time, Pallas kernels for 0%

commit v1 on v0

--- a/solution.py
+++ b/solution.py
@@ -106,8 +106,20 @@
     intensity = lax.psum_scatter(partial_value, "kern", scatter_dimension=1, tiled=True)
     acid = 1.0 - jnp.exp(-EXPOSURE * intensity)
     resist_state = jnp.stack([acid, quencher], axis=0)
+    resist_state = padded_2(resist_state, (("kern", 2), ("tile", 1)), STEPS)
+    rows_total = local_rows * lax.axis_size("tile")
+    cols_total = intensity.shape[1] * kern_count
+    row_origin = lax.axis_index("tile") * local_rows
+    col_origin = kern_index * intensity.shape[1]
     for step_index in range(STEPS):
-        resist_state = react(padded_2(resist_state, (("kern", 2), ("tile", 1)), 1))
+        resist_state = react(resist_state)
+        reach = STEPS - step_index - 1
+        if reach:
+            height, width = resist_state.shape[1], resist_state.shape[2]
+            rows = row_origin - reach + lax.broadcasted_iota(jnp.int32, (height, width), 0)
+            cols = col_origin - reach + lax.broadcasted_iota(jnp.int32, (height, width), 1)
+            inside = (rows >= 0) & (rows < rows_total) & (cols >= 0) & (cols < cols_total)
+            resist_state = jnp.where(inside[None], resist_state, 0.0)
     return (intensity, resist_state[0], resist_state[1])
 
 

time: 359 us -> 204 us (0.57)
  starting transfers between devices: 144 us -> 27 us
  waiting for transfers between devices: 84.1 us -> 48.5 us
    ppermute x16 -> x2, starting transfers between devices: 94.9 us -> 8.51 us  [padded_2(): lax.ppermute(lax.slice_in_dim(block, 0, width, axis=dim), axis, backward)]
    ppermute x16 -> x2, waiting for transfers between devices: 34.1 us -> 3.08 us  [padded_2(): lax.ppermute(lax.slice_in_dim(block, 0, width, axis=dim), axis, backward)]
    ppermute x16 -> x2, starting transfers between devices: 37.4 us -> 6.82 us  [padded_2(): lax.ppermute(lax.slice_in_dim(block, block.shape[dim] - width, None, axis...]
    ppermute x16 -> x2, waiting for transfers between devices: 3.99 us -> 0.01 us  [padded_2(): lax.ppermute(lax.slice_in_dim(block, block.shape[dim] - width, None, axis...]
    unnamed x65 -> x60, local copies, waits for them, and re-layouts: 12.8 us -> 12.1 us
  transfers between devices with their start and end apart: 35 -> 7, of which waited for: 26 -> 4; matrix products, arithmetic and copies ran while one was open for 2% -> 4% of each run, Pallas kernels for 0% -> 0%
where the time goes in v1:
time: 204 us; the launch traced here: 201 us
  local copies, waits for them, and re-layouts  76.4 us (37%)
  waiting for transfers between devices  48.5 us (24%)
  starting transfers between devices  27 us (13%)
  other arithmetic  17.4 us (9%)
  matrix products  16.5 us (8%)
  between operations  15 us (7%)
    another operation x8, local copies, waits for them, and re-layouts, field_band(): jnp.stack([windows[first + offset:first + offset + band_rows] for offset...  31.2 us
    ppermute x2, waiting for transfers between devices, shifted(): lax.ppermute(value, axis, [(source, source + steps) for source in range(l...  22.9 us
    reduce_scatter x1, waiting for transfers between devices, on_device(): lax.psum_scatter(partial_value, 'kern', scatter_dimension=1, tiled=True)  22.5 us
    unnamed x60, local copies, waits for them, and re-layouts  12.1 us
    dot_general x8, matrix products, field_band(): jnp.dot(left_side, right_side, preferred_element_type=jnp.float32)  11.9 us
    ppermute x2, starting transfers between devices, shifted(): lax.ppermute(value, axis, [(source, source + steps) for source in range(l...  11.6 us
    convert_element_type x8, local copies, waits for them, and re-layouts, field_band(): banded_taps = jnp.einsum('kprb,bco->rckpo', taps, selector, preferred_ele...  11.1 us
    slice x2, local copies, waits for them, and re-layouts, on_device(): lower_rim = fields[:, :, local_rows + half_ambit:]  8.61 us
  transfers between devices with their start and end apart: 7, of which 4 were waited for; matrix products, arithmetic and copies ran while one was open for 4% of the time, Pallas kernels for 0%

profile of v1, /device:TPU:129, one launch (start us, length us, event | category | flops | bytes accessed | tf_op | source)
XLA Modules:
  0.0 200.7 jit_solution(14555013139951439851)
XLA Ops:
  22.4 3.9 %copy.88 = bf16[96,8,8,128]{3,2,1,0:T(8,128)(2,1)} copy(bf16[96,8,8,128]{0,3,1,2:T(8,128)(2,1)} %copy-done.8) | data formatting | bytes 3145728 | tf_op jit(solution)/shard_map/stack | solution.py:69
  27.5 1.5 copy.89
  29.0 3.9 %copy.90 = bf16[96,8,8,128]{3,2,1,0:T(8,128)(2,1)} copy(bf16[96,8,8,128]{0,3,1,2:T(8,128)(2,1)} %copy-done.9) | data formatting | bytes 3145728 | tf_op jit(solution)/shard_map/stack | solution.py:69
  33.5 1.6 copy.91
  35.1 3.9 %copy.86 = bf16[96,8,8,128]{3,2,1,0:T(8,128)(2,1)} copy(bf16[96,8,8,128]{0,3,1,2:T(8,128)(2,1)} %copy-done.7) | data formatting | bytes 3145728 | tf_op jit(solution)/shard_map/stack | solution.py:69
  39.6 1.5 copy.87
  41.1 3.9 %copy.84 = bf16[96,8,8,128]{3,2,1,0:T(8,128)(2,1)} copy(bf16[96,8,8,128]{0,3,1,2:T(8,128)(2,1)} %copy-done.6) | data formatting | bytes 3145728 | tf_op jit(solution)/shard_map/stack | solution.py:69
  47.2 3.9 %copy.82 = bf16[96,8,8,128]{3,2,1,0:T(8,128)(2,1)} copy(bf16[96,8,8,128]{0,3,1,2:T(8,128)(2,1)} %copy-done.5) | data formatting | bytes 3145728 | tf_op jit(solution)/shard_map/stack | solution.py:69
  51.7 1.6 copy.83
  53.2 3.9 %copy.80 = bf16[96,8,8,128]{3,2,1,0:T(8,128)(2,1)} copy(bf16[96,8,8,128]{0,3,1,2:T(8,128)(2,1)} %copy-done.4) | data formatting | bytes 3145728 | tf_op jit(solution)/shard_map/stack | solution.py:69
  57.7 1.5 copy.81
  59.2 3.9 %copy.78 = bf16[96,8,8,128]{3,2,1,0:T(8,128)(2,1)} copy(bf16[96,8,8,128]{0,3,1,2:T(8,128)(2,1)} %copy-done.10) | data formatting | bytes 3145728 | tf_op jit(solution)/shard_map/stack | solution.py:69
  65.2 3.9 %copy.76 = bf16[96,8,8,128]{3,2,1,0:T(8,128)(2,1)} copy(bf16[96,8,8,128]{0,3,1,2:T(8,128)(2,1)} %copy-done.11) | data formatting | bytes 3145728 | tf_op jit(solution)/shard_map/stack | solution.py:69
  83.7 1.9 add_add_fusion
  85.7 4.4 %reshape.397 = f32[96,8,6,2,64]{4,3,2,1,0:T(2,128)} reshape(f32[768,768]{1,0:T(8,128)S(1)} %add_add_fusion) | data formatting | bytes 4718592 | tf_op jit(solution)/shard_map/reshape | solution.py:81
  90.1 5.5 %copy.92 = f32[6,2,96,8,64]{2,4,3,1,0:T(8,128)S(1)} copy(f32[6,2,96,8,64]{4,1,0,3,2:T(2,128)} %bitcast.457) | data formatting | bytes 4718592 | tf_op jit(solution)/shard_map/transpose | solution.py:82
  95.6 5.5 %fusion.376 = (f32[6,2,32,512]{2,3,1,0:T(8,128)}, f32[6,2,32,512]{2,3,1,0:T(8,128)}, f32[6,2,32,512]{2,3,1,0:T(8,128)}) fusion(f32[6,2,96,512]{2,3,1,0:T(8,128)S(1)} %bitcast.456), kind=kLoop, calls=%fused_computation.565 | loop fusion | bytes 4718592 | tf_op jit(solution)/shard_map/slice | solution.py:98
  101.1 3.1 %copy.94 = f32[6,2,32,512]{3,2,1,0:T(8,128)} copy(f32[6,2,32,512]{2,3,1,0:T(8,128)} %get-tuple-element.12) | data formatting | bytes 1572864 | tf_op jit(solution)/shard_map/slice | solution.py:98
  104.2 4.9 %collective-permute-start = (f32[6,2,32,512]{3,2,1,0:T(8,128)}, f32[6,2,32,512]{3,2,1,0:T(8,128)}, u32[]{:S(2)}, u32[]{:S(2)}) collective-permute-start(f32[6,2,32,512]{3,2,1,0:T(8,128)} %copy.94), channel_id=1, source_target_pairs={{0,1},{1,2},{2,3},{3,4},{4,5},{5,6},{6,7},{7,8},{8,9},{9,10},{10,1... | collective-permute-start | bytes 2359304 | tf_op jit(solution)/shard_map/ppermute | solution.py:18
  109.1 3.1 %copy.95 = f32[6,2,32,512]{3,2,1,0:T(8,128)} copy(f32[6,2,32,512]{2,3,1,0:T(8,128)} %get-tuple-element.13) | data formatting | bytes 1572864 | tf_op jit(solution)/shard_map/slice | solution.py:97
  112.2 6.7 %collective-permute-start.1 = (f32[6,2,32,512]{3,2,1,0:T(8,128)}, f32[6,2,32,512]{3,2,1,0:T(8,128)}, u32[]{:S(2)}, u32[]{:S(2)}) collective-permute-start(f32[6,2,32,512]{3,2,1,0:T(8,128)} %copy.95), channel_id=1, source_target_pairs={{1,0},{2,1},{3,2},{4,3},{5,4},{6,5},{7,6},{8,7},{9,8},{10,9},{11,1... | collective-permute-start | bytes 2359304 | tf_op jit(solution)/shard_map/ppermute | solution.py:18
  119.3 1.9 copy.101
  121.5 20.9 %collective-permute-done = f32[6,2,32,512]{3,2,1,0:T(8,128)} collective-permute-done((f32[6,2,32,512]{3,2,1,0:T(8,128)}, f32[6,2,32,512]{3,2,1,0:T(8,128)}, u32[]{:S(2)}, u32[]{:S(2)}) %collective-permute-start) | collective-permute-done | bytes 786464 | tf_op jit(solution)/shard_map/ppermute | solution.py:18
  142.4 2.0 %collective-permute-done.1 = f32[6,2,32,512]{3,2,1,0:T(8,128)} collective-permute-done((f32[6,2,32,512]{3,2,1,0:T(8,128)}, f32[6,2,32,512]{3,2,1,0:T(8,128)}, u32[]{:S(2)}, u32[]{:S(2)}) %collective-permute-start.1) | collective-permute-done | bytes 786464 | tf_op jit(solution)/shard_map/ppermute | solution.py:18
  144.4 1.9 add_add_fusion.1
  147.4 22.5 %reduce-scatter.2.cloned.1.call-done = f32[32,128]{0,1:T(8,128)} async-done(((f32[32,512]{0,1:T(8,128)}), f32[32,128]{0,1:T(8,128)}) %reduce-scatter.2.cloned.1.call-update) | async-done | bytes 16400 | tf_op jit(solution)/shard_map/reduce_scatter | solution.py:106
  170.8 2.2 %collective-permute-start.2 = (f32[2,32,8]{2,1,0:T(8,128)S(1)}, f32[2,32,8]{2,1,0:T(8,128)S(1)}, u32[]{:S(2)}, u32[]{:S(2)}) collective-permute-start(f32[2,32,8]{2,1,0:T(8,128)S(1)} %get-tuple-element.73), channel_id=1, source_target_pairs={{0,64},{64,128},{128,192},{1,65},{65,129},{129,193},{2,66},{66,130... | collective-permute-start | bytes 6152 | tf_op jit(solution)/shard_map/ppermute | solution.py:26
  173.0 2.1 %collective-permute-start.3 = (f32[2,32,8]{2,1,0:T(8,128)S(1)}, f32[2,32,8]{2,1,0:T(8,128)S(1)}, u32[]{:S(2)}, u32[]{:S(2)}) collective-permute-start(f32[2,32,8]{2,1,0:T(8,128)S(1)} %get-tuple-element.74), channel_id=1, source_target_pairs={{64,0},{128,64},{192,128},{65,1},{129,65},{193,129},{66,2},{130,66... | collective-permute-start | bytes 6152 | tf_op jit(solution)/shard_map/ppermute | solution.py:29
  175.2 3.1 %collective-permute-done.3 = f32[2,32,8]{2,1,0:T(8,128)S(1)} collective-permute-done((f32[2,32,8]{2,1,0:T(8,128)S(1)}, f32[2,32,8]{2,1,0:T(8,128)S(1)}, u32[]{:S(2)}, u32[]{:S(2)}) %collective-permute-start.3) | collective-permute-done | bytes 2080 | tf_op jit(solution)/shard_map/ppermute | solution.py:29
  178.4 4.6 %collective-permute-start.4 = (f32[2,8,144]{2,1,0:T(8,128)S(1)}, f32[2,8,144]{2,1,0:T(8,128)S(1)}, u32[]{:S(2)}, u32[]{:S(2)}) collective-permute-start(f32[2,8,144]{2,1,0:T(8,128)S(1)} %get-tuple-element.71), channel_id=1, source_target_pairs={{0,1},{1,2},{2,3},{3,4},{4,5},{5,6},{6,7},{7,8},{8,9},{9,10},{10,1... | collective-permute-start | bytes 27656 | tf_op jit(solution)/shard_map/ppermute | solution.py:26
  183.0 6.4 %collective-permute-start.5 = (f32[2,8,144]{2,1,0:T(8,128)S(1)}, f32[2,8,144]{2,1,0:T(8,128)S(1)}, u32[]{:S(2)}, u32[]{:S(2)}) collective-permute-start(f32[2,8,144]{2,1,0:T(8,128)S(1)} %get-tuple-element.72), channel_id=1, source_target_pairs={{1,0},{2,1},{3,2},{4,3},{5,4},{6,5},{7,6},{8,7},{9,8},{10,9},{11,1... | collective-permute-start | bytes 27656 | tf_op jit(solution)/shard_map/ppermute | solution.py:29
  189.5 1.5 copy.98
  (171 shorter events, 42.6 us)
Async XLA Ops:
  7.2 19.2 %copy-start = (bf16[24,2,64,64]{3,2,1,0:T(8,128)(2,1)S(1)}, bf16[24,2,64,64]{3,2,1,0:T(8,128)(2,1)}, u32[]{:S(2)}) copy-start(bf16[24,2,64,64]{3,2,1,0:T(8,128)(2,1)} %param.5) | copy-start | bytes 1179652
  7.2 162.6 %reduce-scatter.2.cloned.1.call-start = ((), (), s32[]{:S(2)}) async-start(), calls=%async_computation.1 | async-start | bytes 327680 | tf_op jit(solution)/shard_map/reduce_scatter | solution.py:106
  12.7 1.9 copy-start.10
  14.6 1.6 copy-start.4
  16.1 1.4 copy-start.5
  17.4 1.6 copy-start.6
  21.0 1.4 copy-start.9
  69.1 1.4 copy-start.12
  69.1 1.9 copy-start.19
  71.0 1.4 copy-start.13
  71.0 1.9 copy-start.20
  72.9 1.4 copy-start.14
  72.9 1.9 copy-start.21
  74.8 1.4 copy-start.15
  74.8 1.9 copy-start.22
  76.7 1.4 copy-start.16
  76.7 1.9 copy-start.23
  78.5 1.4 copy-start.17
  78.5 1.9 copy-start.24
  80.4 1.4 copy-start.18
  80.4 1.9 copy-start.25
  82.3 1.4 copy-start.3
  104.2 15.1 %copy-start.2 = (f32[6,2,32,512]{2,3,1,0:T(8,128)S(1)}, f32[6,2,32,512]{2,3,1,0:T(8,128)}, u32[]{:S(2)}) copy-start(f32[6,2,32,512]{2,3,1,0:T(8,128)} %get-tuple-element.14) | copy-start | bytes 2359300
  104.2 38.2 %collective-permute-start = (f32[6,2,32,512]{3,2,1,0:T(8,128)}, f32[6,2,32,512]{3,2,1,0:T(8,128)}, u32[]{:S(2)}, u32[]{:S(2)}) collective-permute-start(f32[6,2,32,512]{3,2,1,0:T(8,128)} %copy.94), channel_id=1, source_target_pairs={{0,1},{1,2},{2,3},{3,4},{4,5},{5,6},{6,7},{7,8},{8,9},{9,10},{10,1... | collective-permute-start | bytes 2359304 | tf_op jit(solution)/shard_map/ppermute | solution.py:18
  112.2 9.0 %copy-start.27 = (f32[24]{0:T(128)S(1)}, f32[24]{0:T(128)}, u32[]{:S(2)}) copy-start(f32[24]{0:T(128)} %param.6) | copy-start | bytes 292
  112.2 32.2 %collective-permute-start.1 = (f32[6,2,32,512]{3,2,1,0:T(8,128)}, f32[6,2,32,512]{3,2,1,0:T(8,128)}, u32[]{:S(2)}, u32[]{:S(2)}) collective-permute-start(f32[6,2,32,512]{3,2,1,0:T(8,128)} %copy.95), channel_id=1, source_target_pairs={{1,0},{2,1},{3,2},{4,3},{5,4},{6,5},{7,6},{8,7},{9,8},{10,9},{11,1... | collective-permute-start | bytes 2359304 | tf_op jit(solution)/shard_map/ppermute | solution.py:18
  121.5 49.2 %copy-start.26 = (f32[32,128]{1,0:T(8,128)S(1)}, f32[32,128]{1,0:T(8,128)}, u32[]{:S(2)}) copy-start(f32[32,128]{1,0:T(8,128)} %param.7) | copy-start | bytes 49156
  170.8 4.4 %collective-permute-start.2 = (f32[2,32,8]{2,1,0:T(8,128)S(1)}, f32[2,32,8]{2,1,0:T(8,128)S(1)}, u32[]{:S(2)}, u32[]{:S(2)}) collective-permute-start(f32[2,32,8]{2,1,0:T(8,128)S(1)} %get-tuple-element.73), channel_id=1, source_target_pairs={{0,64},{64,128},{128,192},{1,65},{65,129},{129,193},{2,66},{66,130... | collective-permute-start | bytes 6152 | tf_op jit(solution)/shard_map/ppermute | solution.py:26
  173.0 5.2 %collective-permute-start.3 = (f32[2,32,8]{2,1,0:T(8,128)S(1)}, f32[2,32,8]{2,1,0:T(8,128)S(1)}, u32[]{:S(2)}, u32[]{:S(2)}) collective-permute-start(f32[2,32,8]{2,1,0:T(8,128)S(1)} %get-tuple-element.74), channel_id=1, source_target_pairs={{64,0},{128,64},{192,128},{65,1},{129,65},{193,129},{66,2},{130,66... | collective-permute-start | bytes 6152 | tf_op jit(solution)/shard_map/ppermute | solution.py:29
  178.4 12.6 %collective-permute-start.4 = (f32[2,8,144]{2,1,0:T(8,128)S(1)}, f32[2,8,144]{2,1,0:T(8,128)S(1)}, u32[]{:S(2)}, u32[]{:S(2)}) collective-permute-start(f32[2,8,144]{2,1,0:T(8,128)S(1)} %get-tuple-element.71), channel_id=1, source_target_pairs={{0,1},{1,2},{2,3},{3,4},{4,5},{5,6},{6,7},{7,8},{8,9},{9,10},{10,1... | collective-permute-start | bytes 27656 | tf_op jit(solution)/shard_map/ppermute | solution.py:26
  183.0 8.0 %collective-permute-start.5 = (f32[2,8,144]{2,1,0:T(8,128)S(1)}, f32[2,8,144]{2,1,0:T(8,128)S(1)}, u32[]{:S(2)}, u32[]{:S(2)}) collective-permute-start(f32[2,8,144]{2,1,0:T(8,128)S(1)} %get-tuple-element.72), channel_id=1, source_target_pairs={{1,0},{2,1},{3,2},{4,3},{5,4},{6,5},{7,6},{8,7},{9,8},{10,9},{11,1... | collective-permute-start | bytes 27656 | tf_op jit(solution)/shard_map/ppermute | solution.py:29
  191.8 2.0 %copy-start.1 = (bf16[24,2,64,64]{3,2,1,0:T(8,128)(2,1)S(1)}, bf16[24,2,64,64]{3,2,1,0:T(8,128)(2,1)}, u32[]{:S(2)}) copy-start(bf16[24,2,64,64]{3,2,1,0:T(8,128)(2,1)} %param.5) | copy-start | bytes 1179652
  (3 other events, 4.1 us)
Sparse Core Ops, SparseCore 0:
  147.4 22.3 reduce-scatter.1

commit v2 on v0

v2 whole, which is shorter than its diff:
```python
import functools

import jax
import jax.numpy as jnp
from jax import lax
from jax.experimental import pallas as pl
from jax.experimental.pallas import tpu as pltpu
from jax.sharding import PartitionSpec as P

STEPS = 8


DIFFUSE_ACID = 0.2
DIFFUSE_BASE = 0.1
QUENCH_RATE = 0.5
EXPOSURE = 0.35

BLOCKS = 8
TAP_GROUP = 8


def shifted(value, axis, steps):
    count = lax.axis_size(axis)
    leading, last = (max(0, -steps), min(count, count - steps))
    return lax.ppermute(value, axis, [(source, source + steps) for source in range(leading, last)])


def padded_2(block, sides, width):
    for axis, dim in sides:
        count = lax.axis_size(axis)
        forward = [(i, i + 1) for i in range(count - 1)]
        backward = [(target, source) for source, target in forward]
        low = lax.ppermute(
            lax.slice_in_dim(block, block.shape[dim] - width, None, axis=dim), axis, forward
        )
        high = lax.ppermute(lax.slice_in_dim(block, 0, width, axis=dim), axis, backward)
        block = jnp.concatenate([low, block, high], axis=dim)
    return block


def react(padded):
    middle = padded[:, 1:-1, 1:-1]
    spread = (
        padded[:, :-2, 1:-1]
        + padded[:, 2:, 1:-1]
        + padded[:, 1:-1, :-2]
        + padded[:, 1:-1, 2:]
        - 4.0 * middle
    )
    quenched = QUENCH_RATE * middle[0] * middle[1]
    acid_next = middle[0] + DIFFUSE_ACID * spread[0] - quenched
    base_next = middle[1] + DIFFUSE_BASE * spread[1] - quenched
    return jnp.stack([acid_next, base_next], axis=0)


def toeplitz_taps(kernels, window, width):
    ambit = kernels.shape[-1]
    tap_ids = lax.iota(jnp.int32, ambit)
    input_ids = lax.iota(jnp.int32, window)
    output_ids = lax.iota(jnp.int32, width)
    offsets = input_ids[None, :, None] - output_ids[None, None, :]
    selector = (offsets == tap_ids[:, None, None]).astype(jnp.bfloat16)
    taps = jnp.einsum(
        "kpab,bco->ackpo", kernels, selector, preferred_element_type=jnp.float32
    ).astype(jnp.bfloat16)
    return taps.reshape(kernels.shape[2] * window, -1)


def field_kernel(x_ref, t_ref, o_ref, *, out_rows, window):
    step = pl.program_id(0)

    @pl.when(step == 0)
    def _():
        o_ref[...] = jnp.zeros_like(o_ref)

    pieces = []
    for offset in range(TAP_GROUP):
        tap = step * TAP_GROUP + offset
        start = pl.multiple_of(tap * BLOCKS, BLOCKS)
        pieces.append(x_ref[pl.ds(start, out_rows * BLOCKS), :].astype(jnp.bfloat16))
    left = jnp.concatenate(pieces, axis=1)
    o_ref[...] += jnp.dot(left, t_ref[...], preferred_element_type=jnp.float32)


def fields_of(windows, taps, out_rows, window, ambit):
    width_n = taps.shape[1]
    m_rows = out_rows * BLOCKS
    groups = ambit // TAP_GROUP

    return pl.pallas_call(
        functools.partial(field_kernel, out_rows=out_rows, window=window),
        out_shape=jax.ShapeDtypeStruct((m_rows, width_n), jnp.float32),
        grid=(groups,),
        in_specs=[
            pl.BlockSpec(windows.shape, lambda g: (0, 0)),
            pl.BlockSpec((TAP_GROUP * window, width_n), lambda g: (g, 0)),
        ],
        out_specs=pl.BlockSpec((m_rows, width_n), lambda g: (0, 0)),
        compiler_params=pltpu.CompilerParams(vmem_limit_bytes=48 * 1024 * 1024),
        cost_estimate=pl.CostEstimate(
            flops=2 * m_rows * ambit * window * width_n,
            transcendentals=0,
            bytes_accessed=taps.size * 2 + m_rows * width_n * 4,
        ),
    )(windows, taps)


def on_device(mask, kernels, socs_weights, quencher):
    ambit = kernels.shape[2]
    half_ambit = ambit // 2
    kern_count = lax.axis_size("kern")
    kern_index = lax.axis_index("kern")
    tile_index = lax.axis_index("tile")
    local_rows = mask.shape[0]
    local_cols = quencher.shape[1]
    halo = STEPS
    out_rows = local_rows + 2 * halo
    out_cols = local_cols + 2 * halo
    width = out_cols // BLOCKS
    window = 128

    base = padded_2(quencher[None], (("kern", 2), ("tile", 1)), halo)[0]

    reach = halo + half_ambit - local_rows
    up2 = shifted(mask[local_rows - reach :], "tile", 2)
    up1 = shifted(mask, "tile", 1)
    down1 = shifted(mask, "tile", -1)
    down2 = shifted(mask[:reach], "tile", -2)
    rows = jnp.concatenate([up2, up1, mask, down1, down2], axis=0).astype(jnp.float32)
    lead = halo + half_ambit
    span = width * (BLOCKS - 1) + window
    total_cols = mask.shape[1]
    padded = jnp.pad(rows, ((0, 0), (lead, span + local_cols * kern_count - total_cols)))
    cols = lax.dynamic_slice_in_dim(padded, kern_index * local_cols, span, axis=1)
    windows = jnp.stack(
        [cols[:, width * block : width * block + window] for block in range(BLOCKS)], axis=1
    )
    windows = windows.reshape(-1, window)

    taps = toeplitz_taps(kernels, window, width)
    fields = fields_of(windows, taps, out_rows, window, ambit)
    fields = fields.reshape(out_rows, BLOCKS, kernels.shape[0], 2, width)
    squared = fields[:, :, :, 0] ** 2 + fields[:, :, :, 1] ** 2
    intensity_ext = jnp.sum(squared * socs_weights[None, None, :, None], axis=2)
    intensity_ext = intensity_ext.reshape(out_rows, out_cols)
    intensity = intensity_ext[halo : halo + local_rows, halo : halo + local_cols]

    rows_total = local_rows * lax.axis_size("tile")
    cols_total = local_cols * kern_count
    row_origin = tile_index * local_rows
    col_origin = kern_index * local_cols

    def inside(reach_now, height, width_now):
        r = row_origin - reach_now + lax.broadcasted_iota(jnp.int32, (height, width_now), 0)
        c = col_origin - reach_now + lax.broadcasted_iota(jnp.int32, (height, width_now), 1)
        return (r >= 0) & (r < rows_total) & (c >= 0) & (c < cols_total)

    acid = 1.0 - jnp.exp(-EXPOSURE * intensity_ext)
    acid = jnp.where(inside(halo, out_rows, out_cols), acid, 0.0)
    resist_state = jnp.stack([acid, base], axis=0)
    for step_index in range(STEPS):
        resist_state = react(resist_state)
        reach_now = STEPS - step_index - 1
        if reach_now:
            keep = inside(reach_now, resist_state.shape[1], resist_state.shape[2])
            resist_state = jnp.where(keep[None], resist_state, 0.0)
    return (intensity, resist_state[0], resist_state[1])


def solution(mesh):
    placed = (P("tile", None), P(), P(), P("tile", "kern"))
    return jax.shard_map(
        on_device,
        mesh=mesh,
        in_specs=placed,
        out_specs=(P("tile", "kern"), P("tile", "kern"), P("tile", "kern")),
        check_vma=False,
    )
```

time: 359 us -> 138 us (0.38)
  starting transfers between devices: 144 us -> 37.3 us
  waiting for transfers between devices: 84.1 us -> 0.02 us
  between operations: 15.2 us -> 1.29 us
  local copies, waits for them, and re-layouts: 78 us -> 64.3 us
  Pallas kernels: 0 us -> 11.4 us
  matrix products: 16.5 us -> 7.12 us
    ppermute x16 -> x2, starting transfers between devices: 94.9 us -> 11.2 us  [padded_2(): lax.ppermute(lax.slice_in_dim(block, 0, width, axis=dim), axis, backward)]
    ppermute x16 -> x2, waiting for transfers between devices: 34.1 us -> 0.01 us  [padded_2(): lax.ppermute(lax.slice_in_dim(block, 0, width, axis=dim), axis, backward)]
    reshape x1 -> x3, local copies, waits for them, and re-layouts: 4.4 us -> 36.3 us  [the longest x1 19.4 us: toeplitz_taps(): return taps.reshape(kernels.shape[2] * window, -1)]
    ppermute x16 -> x2, starting transfers between devices: 37.4 us -> 6.15 us  [padded_2(): lax.ppermute(lax.slice_in_dim(block, block.shape[dim] - width, None, axis...]
    another operation x8 -> x2, local copies, waits for them, and re-layouts: 31.3 us -> 0.24 us  [on_device(): jnp.stack([cols[:, width * block:width * block + window] for block in ran...]
    ppermute x2 -> x4, waiting for transfers between devices: 23.5 us -> 0.01 us  [shifted(): lax.ppermute(value, axis, [(source, source + steps) for source in range(l...]
    reduce_scatter x1 -> x0, waiting for transfers between devices: 22.5 us -> none  [on_device(): lax.psum_scatter(partial_value, 'kern', scatter_dimension=1, tiled=True)]
    pallas_call x0 -> x1, Pallas kernels: none -> 11.4 us  [fields_of(): pl.pallas_call(functools.partial(field_kernel, out_rows=out_rows, window=...]
  transfers between devices with their start and end apart: 35 -> 8, of which waited for: 26 -> 0; matrix products, arithmetic and copies ran while one was open for 2% -> 59% of each run, Pallas kernels for 0% -> 8%
where the time goes in v2:
time: 138 us; the launch traced here: 136 us
  local copies, waits for them, and re-layouts  64.3 us (47%)
  starting transfers between devices  37.3 us (27%)
  other arithmetic  14.2 us (10%)
  Pallas kernels  11.4 us (8%)
  matrix products  7.12 us (5%)
    ppermute x4, starting transfers between devices, shifted(): lax.ppermute(value, axis, [(source, source + steps) for source in range(l...  20 us
    reshape x1, local copies, waits for them, and re-layouts, toeplitz_taps(): return taps.reshape(kernels.shape[2] * window, -1)  19.4 us
    unnamed x24, local copies, waits for them, and re-layouts  17.4 us
    reshape x1, local copies, waits for them, and re-layouts, on_device(): fields = fields.reshape(out_rows, BLOCKS, kernels.shape[0], 2, width)  16.8 us
    pallas_call x1, Pallas kernels, fields_of(): pl.pallas_call(functools.partial(field_kernel, out_rows=out_rows, window=...  11.4 us
    ppermute x2, starting transfers between devices, padded_2(): lax.ppermute(lax.slice_in_dim(block, 0, width, axis=dim), axis, backward)  11.2 us
    add x1, other arithmetic, on_device(): squared = fields[:, :, :, 0] ** 2 + fields[:, :, :, 1] ** 2  9.24 us
    convert_element_type x1, local copies, waits for them, and re-layouts, toeplitz_taps(): taps = jnp.einsum('kpab,bco->ackpo', kernels, selector, preferred_element...  7.61 us
  transfers between devices with their start and end apart: 8, of which 0 were waited for; matrix products, arithmetic and copies ran while one was open for 59% of the time, Pallas kernels for 8%

profile of v2, /device:TPU:129, one launch (start us, length us, event | category | flops | bytes accessed | tf_op | source)
XLA Modules:
  0.0 135.7 jit_solution(2776163617707274726)
XLA Ops:
  0.6 4.8 %collective-permute-start.1 = (s32[32,512]{1,0:T(8,128)}, s32[32,512]{1,0:T(8,128)S(1)}, u32[]{:S(2)}, u32[]{:S(2)}) collective-permute-start(s32[32,512]{1,0:T(8,128)} %param.4), channel_id=1, source_target_pairs={{0,1},{1,2},{2,3},{3,4},{4,5},{5,6},{6,7},{7,8},{8,9},{9,10},{10,1... | collective-permute-start | bytes 196616 | tf_op jit(solution)/shard_map/ppermute | solution.py:25
  5.4 6.4 %collective-permute-start.2 = (s32[32,512]{1,0:T(8,128)}, s32[32,512]{1,0:T(8,128)S(1)}, u32[]{:S(2)}, u32[]{:S(2)}) collective-permute-start(s32[32,512]{1,0:T(8,128)} %param.4), channel_id=1, source_target_pairs={{1,0},{2,1},{3,2},{4,3},{5,4},{6,5},{7,6},{8,7},{9,8},{10,9},{11,1... | collective-permute-start | bytes 196616 | tf_op jit(solution)/shard_map/ppermute | solution.py:25
  11.8 0.8 fusion.79
  12.6 1.9 %collective-permute-start = (s32[8,512]{1,0:T(8,128)S(1)}, s32[8,512]{1,0:T(8,128)S(1)}, u32[]{:S(2)}, u32[]{:S(2)}) collective-permute-start(s32[8,512]{1,0:T(8,128)S(1)} %get-tuple-element.29), channel_id=1, source_target_pairs={{0,2},{1,3},{2,4},{3,5},{4,6},{5,7},{6,8},{7,9},{8,10},{9,11},{10,... | collective-permute-start | bytes 49160 | tf_op jit(solution)/shard_map/ppermute | solution.py:25
  14.5 0.9 fusion.81
  15.4 4.2 %collective-permute-start.4 = (f32[1,32,8]{2,1,0:T(8,128)S(1)}, f32[1,32,8]{2,1,0:T(8,128)S(1)}, u32[]{:S(2)}, u32[]{:S(2)}) collective-permute-start(f32[1,32,8]{2,1,0:T(8,128)S(1)} %get-tuple-element.32), channel_id=1, source_target_pairs={{0,64},{64,128},{128,192},{1,65},{65,129},{129,193},{2,66},{66,130... | collective-permute-start | bytes 3080 | tf_op jit(solution)/shard_map/ppermute | solution.py:33
  19.6 1.9 %collective-permute-start.5 = (f32[1,32,8]{2,1,0:T(8,128)S(1)}, f32[1,32,8]{2,1,0:T(8,128)S(1)}, u32[]{:S(2)}, u32[]{:S(2)}) collective-permute-start(f32[1,32,8]{2,1,0:T(8,128)S(1)} %get-tuple-element.33), channel_id=1, source_target_pairs={{64,0},{128,64},{192,128},{65,1},{129,65},{193,129},{66,2},{130,66... | collective-permute-start | bytes 3080 | tf_op jit(solution)/shard_map/ppermute | solution.py:36
  21.8 7.1 %convert_bitcast_fusion = bf16[64,128,24,2,18]{1,0,3,2,4:T(8,128)(2,1)} fusion(bf16[24,2,64,64]{3,2,1,0:T(8,128)(2,1)S(1)} %copy-done, s32[128,18]{0,1:T(8,128)S(1)} %iota_subtract_fusion), kind=kOutput, calls=%fused_computation.1 | convolution fusion | flops 913195008 | bytes 14558208 | tf_op jit(solution)/shard_map/kpab,bco->ackpo/dot_general | solution.py:63
  29.7 7.6 %copy.28 = bf16[64,128,24,2,18]{1,0,4,3,2:T(8,128)(2,1)S(1)} copy(bf16[64,128,24,2,18]{1,0,3,2,4:T(8,128)(2,1)} %convert_bitcast_fusion) | data formatting | bytes 28311552 | tf_op jit(solution)/shard_map/convert_element_type | solution.py:65
  37.3 15.3 %copy.45 = bf16[108,8,64,128]{3,1,2,0:T(8,128)(2,1)} copy(bf16[108,8,64,128]{3,2,1,0:T(8,128)(2,1)S(1)} %bitcast.61) | data formatting | bytes 28311552
  52.6 19.4 %copy.29.t_ref = bf16[8192,864]{1,0:T(8,128)(2,1)} copy(bf16[8192,864]{0,1:T(8,128)(2,1)} %bitcast.62) | data formatting | bytes 28311552 | tf_op jit(solution)/shard_map/reshape | solution.py:66
  72.0 7.0 %collective-permute-start.3 = (s32[8,512]{1,0:T(8,128)S(1)}, s32[8,512]{1,0:T(8,128)S(1)}, u32[]{:S(2)}, u32[]{:S(2)}) collective-permute-start(s32[8,512]{1,0:T(8,128)S(1)} %get-tuple-element.28), channel_id=1, source_target_pairs={{2,0},{3,1},{4,2},{5,3},{6,4},{7,5},{8,6},{9,7},{10,8},{11,9},{12,... | collective-permute-start | bytes 49160 | tf_op jit(solution)/shard_map/ppermute | solution.py:25
  79.3 1.9 %collective-permute-start.6 = (f32[1,8,144]{1,2,0:T(8,128)S(1)}, f32[1,8,144]{1,2,0:T(8,128)S(1)}, u32[]{:S(2)}, u32[]{:S(2)}) collective-permute-start(f32[1,8,144]{1,2,0:T(8,128)S(1)} %copy.33), channel_id=1, source_target_pairs={{0,1},{1,2},{2,3},{3,4},{4,5},{5,6},{6,7},{7,8},{8,9},{9,10},{10,1... | collective-permute-start | bytes 13832 | tf_op jit(solution)/shard_map/ppermute | solution.py:33
  81.3 9.3 %collective-permute-start.7 = (f32[1,8,144]{1,2,0:T(8,128)S(1)}, f32[1,8,144]{1,2,0:T(8,128)S(1)}, u32[]{:S(2)}, u32[]{:S(2)}) collective-permute-start(f32[1,8,144]{1,2,0:T(8,128)S(1)} %copy.34), channel_id=1, source_target_pairs={{1,0},{2,1},{3,2},{4,3},{5,4},{6,5},{7,6},{8,7},{9,8},{10,9},{11,1... | collective-permute-start | bytes 13832 | tf_op jit(solution)/shard_map/ppermute | solution.py:36
  91.5 0.2 copy.46
  91.6 11.4 %shard_map.67 = f32[384,864]{1,0:T(8,128)S(1)} custom-call(f32[896,128]{1,0:T(8,128)S(1)} %bitcast.60, bf16[8192,864]{1,0:T(8,128)(2,1)} %copy.29.t_ref), custom_call_target="tpu_custom_call" | custom-call | flops 5435817984 | bytes 15482880 | tf_op jit(solution)/shard_map/pallas_call | solution.py:90
  103.0 16.8 %reshape.427 = f32[48,8,24,2,18]{4,3,2,1,0:T(2,128)} reshape(f32[384,864]{1,0:T(8,128)S(1)} %shard_map.67) | data formatting | bytes 2654208 | tf_op jit(solution)/shard_map/reshape | solution.py:142
  119.8 9.2 %fusion = f32[48,8,24,1,18]{4,3,2,1,0:T(1,128)S(1)} fusion(f32[48,8,24,2,18]{4,3,2,1,0:T(2,128)} %reshape.427), kind=kLoop, calls=%fused_computation.3 | loop fusion | flops 497664 | bytes 1990656 | tf_op jit(solution)/shard_map/add | solution.py:143
  129.1 1.0 multiply_reduce_fusion
  130.1 0.1 copy.31
  130.7 0.2 fusion.7
  131.0 0.2 fusion.24
  131.1 0.2 fusion.6
  131.5 0.2 fusion.5
  131.9 0.2 fusion.11
  132.2 0.2 fusion.10
  132.6 0.2 fusion.9
  132.9 0.2 fusion.8
  133.3 0.2 fusion.12
  133.6 0.7 copy.37
  134.3 0.7 copy.38
  135.0 0.7 slice.392
  (81 shorter events, 3.4 us)
Async XLA Ops:
  0.6 21.2 %copy-start = (bf16[24,2,64,64]{3,2,1,0:T(8,128)(2,1)S(1)}, bf16[24,2,64,64]{3,2,1,0:T(8,128)(2,1)}, u32[]{:S(2)}) copy-start(bf16[24,2,64,64]{3,2,1,0:T(8,128)(2,1)} %param.5) | copy-start | bytes 1179652
  0.6 89.9 %collective-permute-start.1 = (s32[32,512]{1,0:T(8,128)}, s32[32,512]{1,0:T(8,128)S(1)}, u32[]{:S(2)}, u32[]{:S(2)}) collective-permute-start(s32[32,512]{1,0:T(8,128)} %param.4), channel_id=1, source_target_pairs={{0,1},{1,2},{2,3},{3,4},{4,5},{5,6},{6,7},{7,8},{8,9},{9,10},{10,1... | collective-permute-start | bytes 196616 | tf_op jit(solution)/shard_map/ppermute | solution.py:25
  5.4 85.2 %collective-permute-start.2 = (s32[32,512]{1,0:T(8,128)}, s32[32,512]{1,0:T(8,128)S(1)}, u32[]{:S(2)}, u32[]{:S(2)}) collective-permute-start(s32[32,512]{1,0:T(8,128)} %param.4), channel_id=1, source_target_pairs={{1,0},{2,1},{3,2},{4,3},{5,4},{6,5},{7,6},{8,7},{9,8},{10,9},{11,1... | collective-permute-start | bytes 196616 | tf_op jit(solution)/shard_map/ppermute | solution.py:25
  12.6 68.7 %collective-permute-start = (s32[8,512]{1,0:T(8,128)S(1)}, s32[8,512]{1,0:T(8,128)S(1)}, u32[]{:S(2)}, u32[]{:S(2)}) collective-permute-start(s32[8,512]{1,0:T(8,128)S(1)} %get-tuple-element.29), channel_id=1, source_target_pairs={{0,2},{1,3},{2,4},{3,5},{4,6},{5,7},{6,8},{7,9},{8,10},{9,11},{10,... | collective-permute-start | bytes 49160 | tf_op jit(solution)/shard_map/ppermute | solution.py:25
  15.4 56.6 %collective-permute-start.4 = (f32[1,32,8]{2,1,0:T(8,128)S(1)}, f32[1,32,8]{2,1,0:T(8,128)S(1)}, u32[]{:S(2)}, u32[]{:S(2)}) collective-permute-start(f32[1,32,8]{2,1,0:T(8,128)S(1)} %get-tuple-element.32), channel_id=1, source_target_pairs={{0,64},{64,128},{128,192},{1,65},{65,129},{129,193},{2,66},{66,130... | collective-permute-start | bytes 3080 | tf_op jit(solution)/shard_map/ppermute | solution.py:33
  19.6 59.4 %collective-permute-start.5 = (f32[1,32,8]{2,1,0:T(8,128)S(1)}, f32[1,32,8]{2,1,0:T(8,128)S(1)}, u32[]{:S(2)}, u32[]{:S(2)}) collective-permute-start(f32[1,32,8]{2,1,0:T(8,128)S(1)} %get-tuple-element.33), channel_id=1, source_target_pairs={{64,0},{128,64},{192,128},{65,1},{129,65},{193,129},{66,2},{130,66... | collective-permute-start | bytes 3080 | tf_op jit(solution)/shard_map/ppermute | solution.py:36
  52.6 26.3 %copy-start.2 = (f32[32,128]{1,0:T(8,128)S(1)}, f32[32,128]{1,0:T(8,128)}, u32[]{:S(2)}) copy-start(f32[32,128]{1,0:T(8,128)} %param.7) | copy-start | bytes 49156
  52.6 38.0 %copy-start.3 = (s32[32,512]{1,0:T(8,128)S(1)}, s32[32,512]{1,0:T(8,128)}, u32[]{:S(2)}) copy-start(s32[32,512]{1,0:T(8,128)} %param.4) | copy-start | bytes 196612
  72.0 18.7 %collective-permute-start.3 = (s32[8,512]{1,0:T(8,128)S(1)}, s32[8,512]{1,0:T(8,128)S(1)}, u32[]{:S(2)}, u32[]{:S(2)}) collective-permute-start(s32[8,512]{1,0:T(8,128)S(1)} %get-tuple-element.28), channel_id=1, source_target_pairs={{2,0},{3,1},{4,2},{5,3},{6,4},{7,5},{8,6},{9,7},{10,8},{11,9},{12,... | collective-permute-start | bytes 49160 | tf_op jit(solution)/shard_map/ppermute | solution.py:25
  79.3 51.3 %collective-permute-start.6 = (f32[1,8,144]{1,2,0:T(8,128)S(1)}, f32[1,8,144]{1,2,0:T(8,128)S(1)}, u32[]{:S(2)}, u32[]{:S(2)}) collective-permute-start(f32[1,8,144]{1,2,0:T(8,128)S(1)} %copy.33), channel_id=1, source_target_pairs={{0,1},{1,2},{2,3},{3,4},{4,5},{5,6},{6,7},{7,8},{8,9},{9,10},{10,1... | collective-permute-start | bytes 13832 | tf_op jit(solution)/shard_map/ppermute | solution.py:33
  81.3 49.3 %collective-permute-start.7 = (f32[1,8,144]{1,2,0:T(8,128)S(1)}, f32[1,8,144]{1,2,0:T(8,128)S(1)}, u32[]{:S(2)}, u32[]{:S(2)}) collective-permute-start(f32[1,8,144]{1,2,0:T(8,128)S(1)} %copy.34), channel_id=1, source_target_pairs={{1,0},{2,1},{3,2},{4,3},{5,4},{6,5},{7,6},{8,7},{9,8},{10,9},{11,1... | collective-permute-start | bytes 13832 | tf_op jit(solution)/shard_map/ppermute | solution.py:36
  119.8 9.3 %copy-start.4 = (f32[24]{0:T(128)S(1)}, f32[24]{0:T(128)}, u32[]{:S(2)}) copy-start(f32[24]{0:T(128)} %param.6) | copy-start | bytes 292
  131.5 4.2 %copy-start.1 = (bf16[24,2,64,64]{3,2,1,0:T(8,128)(2,1)S(1)}, bf16[24,2,64,64]{3,2,1,0:T(8,128)(2,1)}, u32[]{:S(2)}) copy-start(bf16[24,2,64,64]{3,2,1,0:T(8,128)(2,1)} %param.5) | copy-start | bytes 1179652

commit v3 on v2

--- a/solution.py
+++ b/solution.py
@@ -53,56 +53,86 @@
     return jnp.stack([acid_next, base_next], axis=0)
 
 
-def toeplitz_taps(kernels, window, width):
-    ambit = kernels.shape[-1]
+def toeplitz_selector(ambit, window, width):
     tap_ids = lax.iota(jnp.int32, ambit)
     input_ids = lax.iota(jnp.int32, window)
     output_ids = lax.iota(jnp.int32, width)
-    offsets = input_ids[None, :, None] - output_ids[None, None, :]
+    offsets = input_ids[None, None, :] - output_ids[None, :, None]
     selector = (offsets == tap_ids[:, None, None]).astype(jnp.bfloat16)
-    taps = jnp.einsum(
-        "kpab,bco->ackpo", kernels, selector, preferred_element_type=jnp.float32
-    ).astype(jnp.bfloat16)
-    return taps.reshape(kernels.shape[2] * window, -1)
-
-
-def field_kernel(x_ref, t_ref, o_ref, *, out_rows, window):
+    return selector.reshape(ambit, width * window)
+
+
+def field_kernel(x_ref, k_ref, sel_ref, w_ref, s_ref, o_ref, acc_ref, *, out_rows, pairs, window):
     step = pl.program_id(0)
+    width = sel_ref.shape[1] // window
 
     @pl.when(step == 0)
     def _():
-        o_ref[...] = jnp.zeros_like(o_ref)
-
+        acc_ref[...] = jnp.zeros_like(acc_ref)
+
+    kernel_rows = k_ref[pl.ds(pl.multiple_of(step * TAP_GROUP * pairs, pairs), TAP_GROUP * pairs), :]
+    taps = jnp.dot(kernel_rows, sel_ref[...], preferred_element_type=jnp.float32).astype(
+        jnp.bfloat16
+    )
     pieces = []
+    columns = []
     for offset in range(TAP_GROUP):
         tap = step * TAP_GROUP + offset
         start = pl.multiple_of(tap * BLOCKS, BLOCKS)
         pieces.append(x_ref[pl.ds(start, out_rows * BLOCKS), :].astype(jnp.bfloat16))
+        columns.append(
+            jnp.concatenate(
+                [
+                    taps[offset * pairs : (offset + 1) * pairs, o * window : (o + 1) * window]
+                    for o in range(width)
+                ],
+                axis=0,
+            )
+        )
     left = jnp.concatenate(pieces, axis=1)
-    o_ref[...] += jnp.dot(left, t_ref[...], preferred_element_type=jnp.float32)
-
-
-def fields_of(windows, taps, out_rows, window, ambit):
-    width_n = taps.shape[1]
+    right = jnp.concatenate(columns, axis=1)
+    acc_ref[...] += lax.dot_general(
+        left, right, (((1,), (1,)), ((), ())), preferred_element_type=jnp.float32
+    )
+
+    @pl.when(step == pl.num_programs(0) - 1)
+    def _():
+        field = acc_ref[...]
+        weighted = field * field * w_ref[...]
+        o_ref[...] = jnp.dot(
+            weighted, s_ref[...], precision=lax.Precision.HIGHEST,
+            preferred_element_type=jnp.float32,
+        )
+
+
+def intensity_of(windows, kernel_rows, selector, lane_weights, summer, out_rows, ambit):
+    window = windows.shape[1]
+    width = summer.shape[1]
+    pairs = kernel_rows.shape[0] // ambit
+    width_n = pairs * width
     m_rows = out_rows * BLOCKS
     groups = ambit // TAP_GROUP
 
     return pl.pallas_call(
-        functools.partial(field_kernel, out_rows=out_rows, window=window),
-        out_shape=jax.ShapeDtypeStruct((m_rows, width_n), jnp.float32),
+        functools.partial(field_kernel, out_rows=out_rows, pairs=pairs, window=window),
+        out_shape=jax.ShapeDtypeStruct((m_rows, width), jnp.float32),
         grid=(groups,),
         in_specs=[
             pl.BlockSpec(windows.shape, lambda g: (0, 0)),
-            pl.BlockSpec((TAP_GROUP * window, width_n), lambda g: (g, 0)),
+            pl.BlockSpec(kernel_rows.shape, lambda g: (0, 0)),
+            pl.BlockSpec(selector.shape, lambda g: (0, 0)),
+            pl.BlockSpec(lane_weights.shape, lambda g: (0, 0)),
+            pl.BlockSpec(summer.shape, lambda g: (0, 0)),
         ],
-        out_specs=pl.BlockSpec((m_rows, width_n), lambda g: (0, 0)),
+        out_specs=pl.BlockSpec((m_rows, width), lambda g: (0, 0)),
+        scratch_shapes=[pltpu.VMEM((m_rows, width_n), jnp.float32)],
         compiler_params=pltpu.CompilerParams(vmem_limit_bytes=48 * 1024 * 1024),
         cost_estimate=pl.CostEstimate(
             flops=2 * m_rows * ambit * window * width_n,
             transcendentals=0,
-            bytes_accessed=taps.size * 2 + m_rows * width_n * 4,
+            bytes_accessed=windows.size * 4 + kernel_rows.size * 2,
         ),
-    )(windows, taps)
+    )(windows, kernel_rows, selector, lane_weights, summer)
 
 
 def on_device(mask, kernels, socs_weights, quencher):
@@ -137,11 +167,18 @@
     )
     windows = windows.reshape(-1, window)
 
-    taps = toeplitz_taps(kernels, window, width)
-    fields = fields_of(windows, taps, out_rows, window, ambit)
-    fields = fields.reshape(out_rows, BLOCKS, kernels.shape[0], 2, width)
-    squared = fields[:, :, :, 0] ** 2 + fields[:, :, :, 1] ** 2
-    intensity_ext = jnp.sum(squared * socs_weights[None, None, :, None], axis=2)
+    pairs = kernels.shape[0] * kernels.shape[1]
+    kernel_rows = jnp.transpose(kernels, (2, 0, 1, 3)).reshape(ambit * pairs, ambit)
+    selector = toeplitz_selector(ambit, window, width)
+    lane_weights = jnp.broadcast_to(
+        socs_weights[None, :, None], (width, kernels.shape[0], kernels.shape[1])
+    ).reshape(1, width * pairs)
+    summer = (
+        lax.iota(jnp.int32, width * pairs)[:, None] // pairs == lax.iota(jnp.int32, width)[None, :]
+    ).astype(jnp.float32)
+    intensity_ext = intensity_of(
+        windows, kernel_rows, selector, lane_weights, summer, out_rows, ambit
+    )
     intensity_ext = intensity_ext.reshape(out_rows, out_cols)
     intensity = intensity_ext[halo : halo + local_rows, halo : halo + local_cols]
 

time: 138 us -> 56.9 us (0.41); the launches traced: 136 us -> 56.2 us
  local copies, waits for them, and re-layouts: 64.3 us -> 5.35 us
  other arithmetic: 14.2 us -> 3.92 us
  matrix products: 7.12 us -> 0 us
  starting transfers between devices: 37.3 us -> 32.9 us
  Pallas kernels: 11.4 us -> 12.8 us
    reshape x2 -> x1, local copies, waits for them, and re-layouts: 36.2 us -> 0.16 us  [on_device(): lane_weights = jnp.broadcast_to(socs_weights[None, :, None], (width, kern...]
    unnamed x24 -> x19, local copies, waits for them, and re-layouts: 17.4 us -> 1.51 us
    add x1 -> x0, other arithmetic: 9.24 us -> none  [on_device(): squared = fields[:, :, :, 0] ** 2 + fields[:, :, :, 1] ** 2]
    convert_element_type x1 -> x0, local copies, waits for them, and re-layouts: 7.61 us -> none  [toeplitz_taps(): taps = jnp.einsum('kpab,bco->ackpo', kernels, selector, preferred_element...]
    dot_general x1 -> x0, matrix products: 7.12 us -> none  [toeplitz_taps(): jnp.einsum('kpab,bco->ackpo', kernels, selector, preferred_element_type=j...]
    ppermute x2, starting transfers between devices: 11.2 us -> 5.04 us  [padded_2(): lax.ppermute(lax.slice_in_dim(block, 0, width, axis=dim), axis, backward)]
    ppermute x2, starting transfers between devices: 6.15 us -> 7.88 us  [padded_2(): lax.ppermute(lax.slice_in_dim(block, block.shape[dim] - width, None, axis...]
    pallas_call x1, Pallas kernels: 11.4 us -> 12.8 us  [intensity_of(): pl.pallas_call(functools.partial(field_kernel, out_rows=out_rows, pairs=p...]
  transfers between devices with their start and end apart: 8 -> 8, of which waited for: 0 -> 0; matrix products, arithmetic and copies ran while one was open for 59% -> 10% of each run, Pallas kernels for 8% -> 23%
where the time goes in v3:
time: 56.9 us; the launch traced here: 56.2 us
  starting transfers between devices  32.9 us (58%)
  Pallas kernels  12.8 us (22%)
  local copies, waits for them, and re-layouts  5.35 us (9%)
  other arithmetic  3.92 us (7%)
  between operations  1.21 us (2%)
    ppermute x4, starting transfers between devices, shifted(): lax.ppermute(value, axis, [(source, source + steps) for source in range(l...  20 us
    pallas_call x1, Pallas kernels, intensity_of(): pl.pallas_call(functools.partial(field_kernel, out_rows=out_rows, pairs=p...  12.8 us
    ppermute x2, starting transfers between devices, padded_2(): lax.ppermute(lax.slice_in_dim(block, block.shape[dim] - width, None, axis...  7.88 us
    ppermute x2, starting transfers between devices, padded_2(): lax.ppermute(lax.slice_in_dim(block, 0, width, axis=dim), axis, backward)  5.04 us
    unnamed x19, local copies, waits for them, and re-layouts  1.51 us
    sub x8, other arithmetic, react(): padded[:, :-2, 1:-1] + padded[:, 2:, 1:-1] + padded[:, 1:-1, :-2]  1.21 us
  transfers between devices with their start and end apart: 8, of which 0 were waited for; matrix products, arithmetic and copies ran while one was open for 10% of the time, Pallas kernels for 23%

profile of v3, /device:TPU:129, one launch (start us, length us, event | category | flops | bytes accessed | tf_op | source)
XLA Modules:
  0.0 56.2 jit_solution(10696309102422843560)
XLA Ops:
  0.6 4.8 %collective-permute-start.1 = (s32[32,512]{1,0:T(8,128)}, s32[32,512]{1,0:T(8,128)S(1)}, u32[]{:S(2)}, u32[]{:S(2)}) collective-permute-start(s32[32,512]{1,0:T(8,128)} %param.4), channel_id=1, source_target_pairs={{0,1},{1,2},{2,3},{3,4},{4,5},{5,6},{6,7},{7,8},{8,9},{9,10},{10,1... | collective-permute-start | bytes 196616 | tf_op jit(solution)/shard_map/ppermute | solution.py:25
  5.4 6.4 %collective-permute-start.2 = (s32[32,512]{1,0:T(8,128)}, s32[32,512]{1,0:T(8,128)S(1)}, u32[]{:S(2)}, u32[]{:S(2)}) collective-permute-start(s32[32,512]{1,0:T(8,128)} %param.4), channel_id=1, source_target_pairs={{1,0},{2,1},{3,2},{4,3},{5,4},{6,5},{7,6},{8,7},{9,8},{10,9},{11,1... | collective-permute-start | bytes 196616 | tf_op jit(solution)/shard_map/ppermute | solution.py:25
  11.8 0.8 %fusion.79 = (s32[8,512]{1,0:T(8,128)S(1)}, s32[8,512]{1,0:T(8,128)S(1)}) fusion(s32[32,512]{1,0:T(8,128)} %param.4), kind=kLoop, calls=%fused_computation.196 | loop fusion | bytes 65536 | tf_op jit(solution)/shard_map/slice | solution.py:158
  12.6 1.9 %collective-permute-start = (s32[8,512]{1,0:T(8,128)S(1)}, s32[8,512]{1,0:T(8,128)S(1)}, u32[]{:S(2)}, u32[]{:S(2)}) collective-permute-start(s32[8,512]{1,0:T(8,128)S(1)} %get-tuple-element.20), channel_id=1, source_target_pairs={{0,2},{1,3},{2,4},{3,5},{4,6},{5,7},{6,8},{7,9},{8,10},{9,11},{10,... | collective-permute-start | bytes 49160 | tf_op jit(solution)/shard_map/ppermute | solution.py:25
  14.5 0.9 %fusion.80 = (f32[1,32,8]{2,1,0:T(8,128)S(1)}, f32[1,32,8]{2,1,0:T(8,128)S(1)}) fusion(f32[1,32,128]{2,1,0:T(8,128)} %bitcast.47), kind=kLoop, calls=%fused_computation.197 | loop fusion | bytes 4096 | tf_op jit(solution)/shard_map/slice | solution.py:34
  15.4 3.1 %collective-permute-start.5 = (f32[1,32,8]{2,1,0:T(8,128)S(1)}, f32[1,32,8]{2,1,0:T(8,128)S(1)}, u32[]{:S(2)}, u32[]{:S(2)}) collective-permute-start(f32[1,32,8]{2,1,0:T(8,128)S(1)} %get-tuple-element.24), channel_id=1, source_target_pairs={{64,0},{128,64},{192,128},{65,1},{129,65},{193,129},{66,2},{130,66... | collective-permute-start | bytes 3080 | tf_op jit(solution)/shard_map/ppermute | solution.py:36
  18.5 3.0 %collective-permute-start.4 = (f32[1,32,8]{2,1,0:T(8,128)S(1)}, f32[1,32,8]{2,1,0:T(8,128)S(1)}, u32[]{:S(2)}, u32[]{:S(2)}) collective-permute-start(f32[1,32,8]{2,1,0:T(8,128)S(1)} %get-tuple-element.23), channel_id=1, source_target_pairs={{0,64},{64,128},{128,192},{1,65},{65,129},{129,193},{2,66},{66,130... | collective-permute-start | bytes 3080 | tf_op jit(solution)/shard_map/ppermute | solution.py:33
  21.6 0.2 fusion.1.s_ref
  22.6 0.8 %copy.10 = bf16[64,24,2,64]{3,2,1,0:T(2,128)(2,1)S(1)} copy(bf16[64,24,2,64]{3,0,2,1:T(8,128)(2,1)S(1)} %bitcast.46) | data formatting | bytes 786432 | tf_op jit(solution)/shard_map/transpose | solution.py:171
  23.6 0.2 reshape.451.w_ref
  23.8 7.0 %collective-permute-start.3 = (s32[8,512]{1,0:T(8,128)S(1)}, s32[8,512]{1,0:T(8,128)S(1)}, u32[]{:S(2)}, u32[]{:S(2)}) collective-permute-start(s32[8,512]{1,0:T(8,128)S(1)} %get-tuple-element.19), channel_id=1, source_target_pairs={{2,0},{3,1},{4,2},{5,3},{6,4},{7,5},{8,6},{9,7},{10,8},{11,9},{12,... | collective-permute-start | bytes 49160 | tf_op jit(solution)/shard_map/ppermute | solution.py:25
  30.8 1.9 %collective-permute-start.7 = (f32[1,8,144]{2,1,0:T(8,128)S(1)}, f32[1,8,144]{2,1,0:T(8,128)S(1)}, u32[]{:S(2)}, u32[]{:S(2)}) collective-permute-start(f32[1,8,144]{2,1,0:T(8,128)S(1)} %get-tuple-element.22), channel_id=1, source_target_pairs={{1,0},{2,1},{3,2},{4,3},{5,4},{6,5},{7,6},{8,7},{9,8},{10,9},{11,1... | collective-permute-start | bytes 13832 | tf_op jit(solution)/shard_map/ppermute | solution.py:36
  32.7 4.9 %collective-permute-start.6 = (f32[1,8,144]{2,1,0:T(8,128)S(1)}, f32[1,8,144]{2,1,0:T(8,128)S(1)}, u32[]{:S(2)}, u32[]{:S(2)}) collective-permute-start(f32[1,8,144]{2,1,0:T(8,128)S(1)} %get-tuple-element.21), channel_id=1, source_target_pairs={{0,1},{1,2},{2,3},{3,4},{4,5},{5,6},{6,7},{7,8},{8,9},{9,10},{10,1... | collective-permute-start | bytes 13832 | tf_op jit(solution)/shard_map/ppermute | solution.py:33
  37.7 0.8 %copy-done.2 = s32[32,512]{1,0:T(8,128)S(1)} copy-done((s32[32,512]{1,0:T(8,128)S(1)}, s32[32,512]{1,0:T(8,128)}, u32[]{:S(2)}) %copy-start.2) | copy-done | bytes 65560
  39.0 0.1 fusion.22
  39.3 0.2 copy.12
  39.5 12.8 %shard_map.67 = f32[384,18]{1,0:T(8,128)S(1)} custom-call(f32[896,128]{1,0:T(8,128)S(1)} %bitcast.45, bf16[3072,64]{1,0:T(8,128)(2,1)S(1)} %bitcast.44, bf16[64,2304]{1,0:T(8,128)(2,1)S(1)} %fusion.sel_ref, f32[1,864]{1,0:T(1,128)S(1)} %reshape.451.w_ref, f32[864,18]{1,0:T(8,128)S(1)} %fusion.1.s_ref), custom_call_target="tpu_custom_call" | custom-call | flops 5435817984 | bytes 851968 | tf_op jit(solution)/shard_map/pallas_call | solution.py:116
  52.3 0.1 sub.206
  52.5 0.1 reshape.452
  52.6 0.7 %slice.382 = f32[32,128]{1,0:T(8,128)} slice(f32[48,144]{1,0:T(8,128)S(1)} %reshape.452), slice={[8:40], [8:136]} | slice | bytes 32768 | tf_op jit(solution)/shard_map/slice | solution.py:183
  53.4 0.2 fusion.4
  53.6 0.1 fusion.36
  53.7 0.2 fusion.3
  53.9 0.1 fusion.32
  54.0 0.2 fusion.2
  54.2 0.1 fusion.28
  54.3 0.2 fusion.8
  54.6 0.2 fusion.7
  54.9 0.2 fusion.6
  55.1 0.2 fusion.5
  55.4 0.1 fusion.53
  55.5 0.7 %fusion.56 = (f32[32,128]{1,0:T(8,128)}, f32[32,128]{1,0:T(8,128)}) fusion(f32[2,32,128]{2,1,0:T(8,128)S(1)} %fusion.53, f32[2,34,130]{2,1,0:T(8,128)S(1)} %maximum_select_fusion.6), kind=kLoop, calls=%fused_computation.147 | loop fusion | flops 32768 | bytes 98304 | tf_op jit(solution)/shard_map/sub | solution.py:52
  (70 shorter events, 2.4 us)
Async XLA Ops:
  0.6 22.0 %copy-start = (bf16[24,2,64,64]{3,2,1,0:T(8,128)(2,1)S(1)}, bf16[24,2,64,64]{3,2,1,0:T(8,128)(2,1)}, u32[]{:S(2)}) copy-start(bf16[24,2,64,64]{3,2,1,0:T(8,128)(2,1)} %param.5) | copy-start | bytes 1179652
  0.6 37.0 %collective-permute-start.1 = (s32[32,512]{1,0:T(8,128)}, s32[32,512]{1,0:T(8,128)S(1)}, u32[]{:S(2)}, u32[]{:S(2)}) collective-permute-start(s32[32,512]{1,0:T(8,128)} %param.4), channel_id=1, source_target_pairs={{0,1},{1,2},{2,3},{3,4},{4,5},{5,6},{6,7},{7,8},{8,9},{9,10},{10,1... | collective-permute-start | bytes 196616 | tf_op jit(solution)/shard_map/ppermute | solution.py:25
  5.4 33.1 %collective-permute-start.2 = (s32[32,512]{1,0:T(8,128)}, s32[32,512]{1,0:T(8,128)S(1)}, u32[]{:S(2)}, u32[]{:S(2)}) collective-permute-start(s32[32,512]{1,0:T(8,128)} %param.4), channel_id=1, source_target_pairs={{1,0},{2,1},{3,2},{4,3},{5,4},{6,5},{7,6},{8,7},{9,8},{10,9},{11,1... | collective-permute-start | bytes 196616 | tf_op jit(solution)/shard_map/ppermute | solution.py:25
  12.6 20.2 %collective-permute-start = (s32[8,512]{1,0:T(8,128)S(1)}, s32[8,512]{1,0:T(8,128)S(1)}, u32[]{:S(2)}, u32[]{:S(2)}) collective-permute-start(s32[8,512]{1,0:T(8,128)S(1)} %get-tuple-element.20), channel_id=1, source_target_pairs={{0,2},{1,3},{2,4},{3,5},{4,6},{5,7},{6,8},{7,9},{8,10},{9,11},{10,... | collective-permute-start | bytes 49160 | tf_op jit(solution)/shard_map/ppermute | solution.py:25
  15.4 8.4 %collective-permute-start.5 = (f32[1,32,8]{2,1,0:T(8,128)S(1)}, f32[1,32,8]{2,1,0:T(8,128)S(1)}, u32[]{:S(2)}, u32[]{:S(2)}) collective-permute-start(f32[1,32,8]{2,1,0:T(8,128)S(1)} %get-tuple-element.24), channel_id=1, source_target_pairs={{64,0},{128,64},{192,128},{65,1},{129,65},{193,129},{66,2},{130,66... | collective-permute-start | bytes 3080 | tf_op jit(solution)/shard_map/ppermute | solution.py:36
  18.5 12.2 %collective-permute-start.4 = (f32[1,32,8]{2,1,0:T(8,128)S(1)}, f32[1,32,8]{2,1,0:T(8,128)S(1)}, u32[]{:S(2)}, u32[]{:S(2)}) collective-permute-start(f32[1,32,8]{2,1,0:T(8,128)S(1)} %get-tuple-element.23), channel_id=1, source_target_pairs={{0,64},{64,128},{128,192},{1,65},{65,129},{129,193},{2,66},{66,130... | collective-permute-start | bytes 3080 | tf_op jit(solution)/shard_map/ppermute | solution.py:33
  22.6 0.8 %copy-start.3 = (f32[24]{0:T(128)S(1)}, f32[24]{0:T(128)}, u32[]{:S(2)}) copy-start(f32[24]{0:T(128)} %param.6) | copy-start | bytes 292
  23.6 7.2 %copy-start.1 = (f32[32,128]{1,0:T(8,128)S(1)}, f32[32,128]{1,0:T(8,128)}, u32[]{:S(2)}) copy-start(f32[32,128]{1,0:T(8,128)} %param.7) | copy-start | bytes 49156
  23.8 14.8 %collective-permute-start.3 = (s32[8,512]{1,0:T(8,128)S(1)}, s32[8,512]{1,0:T(8,128)S(1)}, u32[]{:S(2)}, u32[]{:S(2)}) collective-permute-start(s32[8,512]{1,0:T(8,128)S(1)} %get-tuple-element.19), channel_id=1, source_target_pairs={{2,0},{3,1},{4,2},{5,3},{6,4},{7,5},{8,6},{9,7},{10,8},{11,9},{12,... | collective-permute-start | bytes 49160 | tf_op jit(solution)/shard_map/ppermute | solution.py:25
  30.8 22.5 %collective-permute-start.7 = (f32[1,8,144]{2,1,0:T(8,128)S(1)}, f32[1,8,144]{2,1,0:T(8,128)S(1)}, u32[]{:S(2)}, u32[]{:S(2)}) collective-permute-start(f32[1,8,144]{2,1,0:T(8,128)S(1)} %get-tuple-element.22), channel_id=1, source_target_pairs={{1,0},{2,1},{3,2},{4,3},{5,4},{6,5},{7,6},{8,7},{9,8},{10,9},{11,1... | collective-permute-start | bytes 13832 | tf_op jit(solution)/shard_map/ppermute | solution.py:36
  32.7 20.6 %collective-permute-start.6 = (f32[1,8,144]{2,1,0:T(8,128)S(1)}, f32[1,8,144]{2,1,0:T(8,128)S(1)}, u32[]{:S(2)}, u32[]{:S(2)}) collective-permute-start(f32[1,8,144]{2,1,0:T(8,128)S(1)} %get-tuple-element.21), channel_id=1, source_target_pairs={{0,1},{1,2},{2,3},{3,4},{4,5},{5,6},{6,7},{7,8},{8,9},{9,10},{10,1... | collective-permute-start | bytes 13832 | tf_op jit(solution)/shard_map/ppermute | solution.py:33
  37.6 0.8 %copy-start.2 = (s32[32,512]{1,0:T(8,128)S(1)}, s32[32,512]{1,0:T(8,128)}, u32[]{:S(2)}) copy-start(s32[32,512]{1,0:T(8,128)} %param.4) | copy-start | bytes 196612

commit v4 on v3

--- a/solution.py
+++ b/solution.py
@@ -135,6 +135,100 @@
     )(windows, kernel_rows, selector, lane_weights, summer)
 
 
+MASK_FROM = ((-1, 0), (1, 0), (-2, 0), (2, 0))
+QUENCH_FROM = ((-1, -1), (-1, 0), (-1, 1), (0, -1), (0, 1), (1, -1), (1, 0), (1, 1))
+
+
+def exchange_kernel(mask_ref, q_ref, mask_out, q_out, mask_slots, q_slots, send_sems, recv_sems):
+    tile = lax.axis_index("tile")
+    kern = lax.axis_index("kern")
+    tiles = lax.axis_size("tile")
+    kerns = lax.axis_size("kern")
+
+    def exists(dt, dq):
+        return (tile + dt >= 0) & (tile + dt < tiles) & (kern + dq >= 0) & (kern + dq < kerns)
+
+    def device(dt, dq):
+        return {"tile": tile + dt, "kern": kern + dq}
+
+    barrier = pltpu.get_barrier_semaphore()
+    partners = sorted(set(MASK_FROM) | set(QUENCH_FROM))
+    count = jnp.int32(0)
+    for dt, dq in partners:
+        here = exists(dt, dq)
+
+        @pl.when(here)
+        def _():
+            pl.semaphore_signal(
+                barrier, 1, device_id=device(dt, dq), device_id_type=pl.DeviceIdType.MESH
+            )
+
+        count = count + here.astype(jnp.int32)
+    pl.semaphore_wait(barrier, count)
+
+    plan = [(mask_ref, mask_slots, slot, offset) for slot, offset in enumerate(MASK_FROM)]
+    plan += [(q_ref, q_slots, slot, offset) for slot, offset in enumerate(QUENCH_FROM)]
+    copies = []
+    for index, (source, slots, slot, (dt, dq)) in enumerate(plan):
+        copy = pltpu.make_async_remote_copy(
+            src_ref=source,
+            dst_ref=slots.at[slot],
+            send_sem=send_sems.at[index],
+            recv_sem=recv_sems.at[index],
+            device_id=device(-dt, -dq),
+            device_id_type=pl.DeviceIdType.MESH,
+        )
+
+        @pl.when(exists(-dt, -dq))
+        def _():
+            copy.start()
+
+        copies.append(copy)
+    for copy, (source, slots, slot, (dt, dq)) in zip(copies, plan):
+
+        @pl.when(exists(-dt, -dq))
+        def _():
+            copy.wait_send()
+
+        @pl.when(exists(dt, dq))
+        def _():
+            copy.wait_recv()
+
+    for out, slots, offsets in ((mask_out, mask_slots, MASK_FROM), (q_out, q_slots, QUENCH_FROM)):
+        for slot, (dt, dq) in enumerate(offsets):
+            here = exists(dt, dq)
+
+            @pl.when(here)
+            def _():
+                out[slot] = slots[slot]
+
+            @pl.when(jnp.logical_not(here))
+            def _():
+                out[slot] = jnp.zeros(out.shape[1:], out.dtype)
+
+
+def exchange(mask, quencher):
+    mask_shape = (len(MASK_FROM),) + mask.shape
+    q_shape = (len(QUENCH_FROM),) + quencher.shape
+    vmem = pl.BlockSpec(memory_space=pltpu.VMEM)
+    return pl.pallas_call(
+        exchange_kernel,
+        out_shape=(
+            jax.ShapeDtypeStruct(mask_shape, mask.dtype),
+            jax.ShapeDtypeStruct(q_shape, quencher.dtype),
+        ),
+        in_specs=[vmem, vmem],
+        out_specs=(vmem, vmem),
+        scratch_shapes=[
+            pltpu.VMEM(mask_shape, mask.dtype),
+            pltpu.VMEM(q_shape, quencher.dtype),
+            pltpu.SemaphoreType.DMA((len(MASK_FROM) + len(QUENCH_FROM),)),
+            pltpu.SemaphoreType.DMA((len(MASK_FROM) + len(QUENCH_FROM),)),
+        ],
+        compiler_params=pltpu.CompilerParams(collective_id=0, has_side_effects=True),
+    )(mask, quencher)
+
+
 def on_device(mask, kernels, socs_weights, quencher):
     ambit = kernels.shape[2]
     half_ambit = ambit // 2
@@ -149,14 +243,21 @@
     width = out_cols // BLOCKS
     window = 128
 
-    base = padded_2(quencher[None], (("kern", 2), ("tile", 1)), halo)[0]
+    mask_from, q_from = exchange(mask, quencher)
+    top = jnp.concatenate(
+        [q_from[0][-halo:, -halo:], q_from[1][-halo:], q_from[2][-halo:, :halo]], axis=1
+    )
+    middle = jnp.concatenate([q_from[3][:, -halo:], quencher, q_from[4][:, :halo]], axis=1)
+    bottom = jnp.concatenate(
+        [q_from[5][:halo, -halo:], q_from[6][:halo], q_from[7][:halo, :halo]], axis=1
+    )
+    base = jnp.concatenate([top, middle, bottom], axis=0)
 
     reach = halo + half_ambit - local_rows
-    up2 = shifted(mask[local_rows - reach :], "tile", 2)
-    up1 = shifted(mask, "tile", 1)
-    down1 = shifted(mask, "tile", -1)
-    down2 = shifted(mask[:reach], "tile", -2)
-    rows = jnp.concatenate([up2, up1, mask, down1, down2], axis=0).astype(jnp.float32)
+    rows = jnp.concatenate(
+        [mask_from[2][local_rows - reach :], mask_from[0], mask, mask_from[1], mask_from[3][:reach]],
+        axis=0,
+    ).astype(jnp.float32)
     lead = halo + half_ambit
     span = width * (BLOCKS - 1) + window
     total_cols = mask.shape[1]

time: 56.9 us -> 40.7 us (0.72)
  starting transfers between devices: 32.9 us -> 0 us
  Pallas kernels: 12.8 us -> 27.8 us
  local copies, waits for them, and re-layouts: 5.35 us -> 7.5 us
    ppermute x8 -> x0, starting transfers between devices: 32.9 us -> none  [the longest x4 20 us: shifted(): lax.ppermute(value, axis, [(source, source + steps) for source in range(l...]
    pallas_call x0 -> x1, Pallas kernels: none -> 15.1 us  [exchange(): pl.pallas_call(exchange_kernel, out_shape=(jax.ShapeDtypeStruct(mask_shap...]
    unnamed x19 -> x21, local copies, waits for them, and re-layouts: 1.51 us -> 3.56 us
    squeeze x0 -> x1, local copies, waits for them, and re-layouts: none -> 0.81 us  [on_device(): q_from[0][-halo:, -halo:]]
    slice x2 -> x6, local copies, waits for them, and re-layouts: 1.64 us -> 0.93 us  [the longest x1 0.71 us: on_device(): q_from[1][-halo:]]
  transfers between devices with their start and end apart: 8 -> 0, of which waited for: 0 -> 0; matrix products, arithmetic and copies ran while one was open for 10% -> 0% of each run, Pallas kernels for 23% -> 0%
where the time goes in v4:
time: 40.7 us; the launch traced here: 40.3 us
  Pallas kernels  27.8 us (68%)
  local copies, waits for them, and re-layouts  7.5 us (18%)
  other arithmetic  3.83 us (9%)
  between operations  1.09 us (3%)
    pallas_call x1, Pallas kernels, exchange(): pl.pallas_call(exchange_kernel, out_shape=(jax.ShapeDtypeStruct(mask_shap...  15.1 us
    pallas_call x1, Pallas kernels, intensity_of(): pl.pallas_call(functools.partial(field_kernel, out_rows=out_rows, pairs=p...  12.7 us
    unnamed x21, local copies, waits for them, and re-layouts  3.56 us
    sub x8, other arithmetic, react(): padded[:, :-2, 1:-1] + padded[:, 2:, 1:-1] + padded[:, 1:-1, :-2]  1.21 us

profile of v4, /device:TPU:129, one launch (start us, length us, event | category | flops | bytes accessed | tf_op | source)
XLA Modules:
  0.0 40.3 jit_solution(7898896374434628775)
XLA Ops:
  1.5 0.6 %copy-done.4 = f32[24]{0:T(128)S(1)} copy-done((f32[24]{0:T(128)S(1)}, f32[24]{0:T(128)}, u32[]{:S(2)}) %copy-start.4) | copy-done | bytes 120
  2.2 0.2 reshape.455.w_ref
  2.4 15.1 %shard_map.67 = (s32[4,32,512]{2,1,0:T(8,128)}, f32[8,32,128]{2,1,0:T(8,128)}) custom-call(s32[32,512]{1,0:T(8,128)} %mask_ref.1, f32[32,128]{1,0:T(8,128)} %q_ref.1), custom_call_target="tpu_custom_call" | custom-call | tf_op jit(solution)/shard_map/pallas_call | solution.py:214
  17.6 0.7 %slice_bitcast_fusion.7 = (f32[8,128]{1,0:T(8,128)S(1)}, f32[8,128]{1,0:T(8,128)S(1)}) fusion(f32[8,32,128]{2,1,0:T(8,128)} %get-tuple-element.6), kind=kLoop, calls=%fused_computation.176 | loop fusion | bytes 16384 | tf_op jit(solution)/shard_map/slice | solution.py:248
  18.3 0.8 %slice_bitcast_fusion.5 = (f32[32,128]{1,0:T(8,128)S(1)}, f32[32,128]{1,0:T(8,128)S(1)}, f32[32,128]{1,0:T(8,128)S(1)}, f32[32,128]{1,0:T(8,128)S(1)}, f32[32,128]{1,0:T(8,128)S(1)}, /*index=5*/f32[32,128]{1,0:T(8,128)S(1)}) fusion(f32[8,32,128]{2,1,0:T(8,128)} %get-tuple-element.6), kind=kLoop, calls=%fused_computation.167 | loop fusion | bytes 196608 | tf_op jit(solution)/shard_map/squeeze | solution.py:248
  19.3 0.6 %copy-done.3 = f32[32,128]{1,0:T(8,128)S(1)} copy-done((f32[32,128]{1,0:T(8,128)S(1)}, f32[32,128]{1,0:T(8,128)}, u32[]{:S(2)}) %copy-start.3) | copy-done | bytes 16408
  20.1 0.8 %copy-done.1 = s32[32,512]{1,0:T(8,128)S(1)} copy-done((s32[32,512]{1,0:T(8,128)S(1)}, s32[32,512]{1,0:T(8,128)}, u32[]{:S(2)}) %copy-start.1) | copy-done | bytes 65560
  21.0 0.2 fusion.1.s_ref
  21.2 0.1 fusion.22
  21.3 0.1 fusion.24
  21.4 0.1 fusion.26
  21.5 0.1 fusion.28
  21.7 0.1 fusion.32
  21.9 0.2 copy.12
  22.1 0.8 %copy-done = bf16[24,2,64,64]{3,2,1,0:T(8,128)(2,1)S(1)} copy-done((bf16[24,2,64,64]{3,2,1,0:T(8,128)(2,1)S(1)}, bf16[24,2,64,64]{3,2,1,0:T(8,128)(2,1)}, u32[]{:S(2)}) %copy-start) | copy-done | bytes 393240
  22.9 0.8 %copy.10 = bf16[64,24,2,64]{3,2,1,0:T(2,128)(2,1)S(1)} copy(bf16[64,24,2,64]{3,0,2,1:T(8,128)(2,1)S(1)} %bitcast.72) | data formatting | bytes 786432 | tf_op jit(solution)/shard_map/transpose | solution.py:272
  23.7 12.7 %shard_map.68 = f32[384,18]{1,0:T(8,128)S(1)} custom-call(f32[896,128]{1,0:T(8,128)S(1)} %bitcast.71, bf16[3072,64]{1,0:T(8,128)(2,1)S(1)} %bitcast.70, bf16[64,2304]{1,0:T(8,128)(2,1)S(1)} %fusion.sel_ref, f32[1,864]{1,0:T(1,128)S(1)} %reshape.455.w_ref, f32[864,18]{1,0:T(8,128)S(1)} %fusion.1.s_ref), custom_call_target="tpu_custom_call" | custom-call | flops 5435817984 | bytes 851968 | tf_op jit(solution)/shard_map/pallas_call | solution.py:116
  36.4 0.1 reshape.456
  36.5 0.7 %slice.454 = f32[32,128]{1,0:T(8,128)} slice(f32[48,144]{1,0:T(8,128)S(1)} %reshape.456), slice={[8:40], [8:136]} | slice | bytes 32768 | tf_op jit(solution)/shard_map/slice | solution.py:284
  37.3 0.1 sub.206
  37.5 0.2 fusion.4
  37.6 0.1 fusion.44
  37.8 0.2 fusion.11
  37.9 0.1 fusion.40
  38.1 0.2 fusion.10
  38.2 0.1 fusion.36
  38.4 0.2 fusion.16
  38.6 0.2 fusion.15
  38.9 0.2 fusion.14
  39.2 0.2 fusion.13
  39.5 0.1 fusion.61
  39.6 0.7 %fusion.64 = (f32[32,128]{1,0:T(8,128)}, f32[32,128]{1,0:T(8,128)}) fusion(f32[2,32,128]{2,1,0:T(8,128)S(1)} %fusion.61, f32[2,34,130]{2,1,0:T(8,128)S(1)} %maximum_select_fusion.6), kind=kLoop, calls=%fused_computation.156 | loop fusion | flops 32768 | bytes 98304 | tf_op jit(solution)/shard_map/sub | solution.py:52
  (61 shorter events, 2.1 us)
Async XLA Ops:
  1.5 0.7 %copy-start.4 = (f32[24]{0:T(128)S(1)}, f32[24]{0:T(128)}, u32[]{:S(2)}) copy-start(f32[24]{0:T(128)} %param.6) | copy-start | bytes 292
  17.5 2.5 %copy-start.2 = (s32[4,32,512]{2,1,0:T(8,128)S(1)}, s32[4,32,512]{2,1,0:T(8,128)}, u32[]{:S(2)}) copy-start(s32[4,32,512]{2,1,0:T(8,128)} %get-tuple-element.5) | copy-start | bytes 786436
  19.2 0.7 %copy-start.3 = (f32[32,128]{1,0:T(8,128)S(1)}, f32[32,128]{1,0:T(8,128)}, u32[]{:S(2)}) copy-start(f32[32,128]{1,0:T(8,128)} %q_ref.1) | copy-start | bytes 49156
  20.1 0.8 %copy-start.1 = (s32[32,512]{1,0:T(8,128)S(1)}, s32[32,512]{1,0:T(8,128)}, u32[]{:S(2)}) copy-start(s32[32,512]{1,0:T(8,128)} %mask_ref.1) | copy-start | bytes 196612
  21.7 1.1 %copy-start = (bf16[24,2,64,64]{3,2,1,0:T(8,128)(2,1)S(1)}, bf16[24,2,64,64]{3,2,1,0:T(8,128)(2,1)}, u32[]{:S(2)}) copy-start(bf16[24,2,64,64]{3,2,1,0:T(8,128)(2,1)} %param.5) | copy-start | bytes 1179652

commit v5 on v4

--- a/solution.py
+++ b/solution.py
@@ -62,7 +62,19 @@
     return selector.reshape(ambit, width * window)
 
 
-def field_kernel(x_ref, k_ref, sel_ref, w_ref, s_ref, o_ref, acc_ref, *, out_rows, pairs, window):
+def spread_of(value):
+    rows, lanes = value.shape
+    up = pltpu.roll(value, 1, 0)
+    down = pltpu.roll(value, rows - 1, 0)
+    left = pltpu.roll(value, 1, 1)
+    right = pltpu.roll(value, lanes - 1, 1)
+    return up + down + left + right - 4.0 * value
+
+
+def field_kernel(
+    x_ref, k_ref, sel_ref, w_ref, s_ref, keep_ref, base_ref,
+    i_out, a_out, b_out, acc_ref, red_ref, *, out_rows, pairs, window, halo,
+):
     step = pl.program_id(0)
     width = sel_ref.shape[1] // window
 
@@ -97,42 +109,67 @@
 
     @pl.when(step == pl.num_programs(0) - 1)
     def _():
+        lanes = keep_ref.shape[1]
         field = acc_ref[...]
         weighted = field * field * w_ref[...]
-        o_ref[...] = jnp.dot(
+        red_ref[...] = jnp.dot(
             weighted, s_ref[...], precision=lax.Precision.HIGHEST,
             preferred_element_type=jnp.float32,
         )
-
-
-def intensity_of(windows, kernel_rows, selector, lane_weights, summer, out_rows, ambit):
+        intensity = jnp.zeros((out_rows, lanes), jnp.float32)
+        for block in range(BLOCKS):
+            part = red_ref[pl.ds(block, out_rows, stride=BLOCKS), :]
+            part = jnp.concatenate([part, jnp.zeros_like(part)], axis=1)
+            intensity = intensity + pltpu.roll(part, width * block, 1) if block else part
+        keep = keep_ref[...] > 0.5
+        acid = jnp.where(keep, 1.0 - jnp.exp(-EXPOSURE * intensity), 0.0)
+        base = base_ref[...]
+        for _ in range(STEPS):
+            quenched = QUENCH_RATE * acid * base
+            acid_next = acid + DIFFUSE_ACID * spread_of(acid) - quenched
+            base_next = base + DIFFUSE_BASE * spread_of(base) - quenched
+            acid = jnp.where(keep, acid_next, 0.0)
+            base = jnp.where(keep, base_next, 0.0)
+        rows, cols = i_out.shape
+        for out, value in ((i_out, intensity), (a_out, acid), (b_out, base)):
+            out[...] = pltpu.roll(value, lanes - halo, 1)[halo : halo + rows, :cols]
+
+
+def resist_of(windows, kernel_rows, selector, lane_weights, summer, keep, base, out_rows, ambit, halo, local):
     window = windows.shape[1]
-    width = summer.shape[1]
+    width = selector.shape[1] // window
     pairs = kernel_rows.shape[0] // ambit
     width_n = pairs * width
     m_rows = out_rows * BLOCKS
     groups = ambit // TAP_GROUP
+    whole = lambda g: (0, 0)
+    out = jax.ShapeDtypeStruct(local, jnp.float32)
 
     return pl.pallas_call(
-        functools.partial(field_kernel, out_rows=out_rows, pairs=pairs, window=window),
-        out_shape=jax.ShapeDtypeStruct((m_rows, width), jnp.float32),
+        functools.partial(field_kernel, out_rows=out_rows, pairs=pairs, window=window, halo=halo),
+        out_shape=(out, out, out),
         grid=(groups,),
         in_specs=[
-            pl.BlockSpec(windows.shape, lambda g: (0, 0)),
-            pl.BlockSpec(kernel_rows.shape, lambda g: (0, 0)),
-            pl.BlockSpec(selector.shape, lambda g: (0, 0)),
-            pl.BlockSpec(lane_weights.shape, lambda g: (0, 0)),
-            pl.BlockSpec(summer.shape, lambda g: (0, 0)),
+            pl.BlockSpec(windows.shape, whole),
+            pl.BlockSpec(kernel_rows.shape, whole),
+            pl.BlockSpec(selector.shape, whole),
+            pl.BlockSpec(lane_weights.shape, whole),
+            pl.BlockSpec(summer.shape, whole),
+            pl.BlockSpec(keep.shape, whole),
+            pl.BlockSpec(base.shape, whole),
         ],
-        out_specs=pl.BlockSpec((m_rows, width), lambda g: (0, 0)),
-        scratch_shapes=[pltpu.VMEM((m_rows, width_n), jnp.float32)],
+        out_specs=(pl.BlockSpec(local, whole),) * 3,
+        scratch_shapes=[
+            pltpu.VMEM((m_rows, width_n), jnp.float32),
+            pltpu.VMEM((m_rows, summer.shape[1]), jnp.float32),
+        ],
         compiler_params=pltpu.CompilerParams(vmem_limit_bytes=48 * 1024 * 1024),
         cost_estimate=pl.CostEstimate(
             flops=2 * m_rows * ambit * window * width_n,
             transcendentals=0,
             bytes_accessed=windows.size * 4 + kernel_rows.size * 2,
         ),
-    )(windows, kernel_rows, selector, lane_weights, summer)
+    )(windows, kernel_rows, selector, lane_weights, summer, keep, base)
 
 
 MASK_FROM = ((-1, 0), (1, 0), (-2, 0), (2, 0))
@@ -274,35 +311,22 @@
     lane_weights = jnp.broadcast_to(
         socs_weights[None, :, None], (width, kernels.shape[0], kernels.shape[1])
     ).reshape(1, width * pairs)
+    lanes = 2 * window
     summer = (
-        lax.iota(jnp.int32, width * pairs)[:, None] // pairs == lax.iota(jnp.int32, width)[None, :]
+        lax.iota(jnp.int32, width * pairs)[:, None] // pairs == lax.iota(jnp.int32, window)[None, :]
     ).astype(jnp.float32)
-    intensity_ext = intensity_of(
-        windows, kernel_rows, selector, lane_weights, summer, out_rows, ambit
-    )
-    intensity_ext = intensity_ext.reshape(out_rows, out_cols)
-    intensity = intensity_ext[halo : halo + local_rows, halo : halo + local_cols]
 
     rows_total = local_rows * lax.axis_size("tile")
     cols_total = local_cols * kern_count
-    row_origin = tile_index * local_rows
-    col_origin = kern_index * local_cols
-
-    def inside(reach_now, height, width_now):
-        r = row_origin - reach_now + lax.broadcasted_iota(jnp.int32, (height, width_now), 0)
-        c = col_origin - reach_now + lax.broadcasted_iota(jnp.int32, (height, width_now), 1)
-        return (r >= 0) & (r < rows_total) & (c >= 0) & (c < cols_total)
-
-    acid = 1.0 - jnp.exp(-EXPOSURE * intensity_ext)
-    acid = jnp.where(inside(halo, out_rows, out_cols), acid, 0.0)
-    resist_state = jnp.stack([acid, base], axis=0)
-    for step_index in range(STEPS):
-        resist_state = react(resist_state)
-        reach_now = STEPS - step_index - 1
-        if reach_now:
-            keep = inside(reach_now, resist_state.shape[1], resist_state.shape[2])
-            resist_state = jnp.where(keep[None], resist_state, 0.0)
-    return (intensity, resist_state[0], resist_state[1])
+    r = tile_index * local_rows - halo + lax.broadcasted_iota(jnp.int32, (out_rows, lanes), 0)
+    c = kern_index * local_cols - halo + lax.broadcasted_iota(jnp.int32, (out_rows, lanes), 1)
+    keep = (r >= 0) & (r < rows_total) & (c >= 0) & (c < cols_total)
+    keep = (keep & (c < kern_index * local_cols - halo + out_cols)).astype(jnp.float32)
+    base = jnp.pad(base, ((0, 0), (0, lanes - out_cols)))
+    return resist_of(
+        windows, kernel_rows, selector, lane_weights, summer, keep, base,
+        out_rows, ambit, halo, (local_rows, local_cols),
+    )
 
 
 def solution(mesh):

time: 40.7 us -> 37.5 us (0.921)
  other arithmetic: 3.83 us -> 0.46 us
  Pallas kernels: 27.8 us -> 29.3 us
  local copies, waits for them, and re-layouts: 7.5 us -> 6.55 us
    sub x17 -> x0, other arithmetic: 2.59 us -> none  [the longest x8 1.21 us: react(): padded[:, :-2, 1:-1] + padded[:, 2:, 1:-1] + padded[:, 1:-1, :-2]]
    pallas_call x1, Pallas kernels: 12.7 us -> 14.2 us  [resist_of(): pl.pallas_call(functools.partial(field_kernel, out_rows=out_rows, pairs=p...]
    slice x1 -> x0, local copies, waits for them, and re-layouts: 0.68 us -> none  [on_device(): intensity = intensity_ext[halo:halo + local_rows, halo:halo + local_cols]]
    and x15 -> x1, other arithmetic: 0.63 us -> 0.01 us  [on_device(): keep = (r >= 0) & (r < rows_total) & (c >= 0) & (c < cols_total)]
where the time goes in v5:
time: 37.5 us; the launch traced here: 37.1 us
  Pallas kernels  29.3 us (78%)
  local copies, waits for them, and re-layouts  6.55 us (17%)
  between operations  0.83 us (2%)
  other arithmetic  0.46 us (1%)
    pallas_call x1, Pallas kernels, exchange(): pl.pallas_call(exchange_kernel, out_shape=(jax.ShapeDtypeStruct(mask_shap...  15.1 us
    pallas_call x1, Pallas kernels, resist_of(): pl.pallas_call(functools.partial(field_kernel, out_rows=out_rows, pairs=p...  14.2 us
    unnamed x21, local copies, waits for them, and re-layouts  3.49 us
    squeeze x1, local copies, waits for them, and re-layouts, on_device(): q_from[0][-halo:, -halo:]  0.81 us
    transpose x1, local copies, waits for them, and re-layouts, on_device(): jnp.transpose(kernels, (2, 0, 1, 3)).reshape(ambit * pairs, ambit)  0.81 us

profile of v5, /device:TPU:129, one launch (start us, length us, event | category | flops | bytes accessed | tf_op | source)
XLA Modules:
  0.0 37.1 jit_solution(5624629989488740474)
XLA Ops:
  0.7 0.0 copy-start.4
  0.7 0.1 and_convert_fusion.keep_ref
  0.8 0.6 %copy-done.4 = f32[24]{0:T(128)S(1)} copy-done((f32[24]{0:T(128)S(1)}, f32[24]{0:T(128)}, u32[]{:S(2)}) %copy-start.4) | copy-done | bytes 120
  1.4 0.1 broadcast_in_dim.2
  1.5 0.2 reshape.64.w_ref
  1.6 0.1 fusion.sel_ref
  1.7 15.1 %shard_map.67 = (s32[4,32,512]{2,1,0:T(8,128)}, f32[8,32,128]{2,1,0:T(8,128)}) custom-call(s32[32,512]{1,0:T(8,128)} %mask_ref.1, f32[32,128]{1,0:T(8,128)} %q_ref.1), custom_call_target="tpu_custom_call" | custom-call | tf_op jit(solution)/shard_map/pallas_call | solution.py:251
  16.8 0.0 copy-start.2
  16.8 0.7 %slice_bitcast_fusion.7 = (f32[8,128]{1,0:T(8,128)S(1)}, f32[8,128]{1,0:T(8,128)S(1)}) fusion(f32[8,32,128]{2,1,0:T(8,128)} %get-tuple-element.6), kind=kLoop, calls=%fused_computation.58 | loop fusion | bytes 16384 | tf_op jit(solution)/shard_map/slice | solution.py:285
  17.5 0.8 %slice_bitcast_fusion.5 = (f32[32,128]{1,0:T(8,128)S(1)}, f32[32,128]{1,0:T(8,128)S(1)}, f32[32,128]{1,0:T(8,128)S(1)}, f32[32,128]{1,0:T(8,128)S(1)}, f32[32,128]{1,0:T(8,128)S(1)}, /*index=5*/f32[32,128]{1,0:T(8,128)S(1)}) fusion(f32[8,32,128]{2,1,0:T(8,128)} %get-tuple-element.6), kind=kLoop, calls=%fused_computation.49 | loop fusion | bytes 196608 | tf_op jit(solution)/shard_map/squeeze | solution.py:285
  18.3 0.1 slice.128
  18.4 0.1 slice.132
  18.5 0.1 slice.130
  18.5 0.6 %copy-done.3 = f32[32,128]{1,0:T(8,128)S(1)} copy-done((f32[32,128]{1,0:T(8,128)S(1)}, f32[32,128]{1,0:T(8,128)}, u32[]{:S(2)}) %copy-start.3) | copy-done | bytes 16408
  19.2 0.1 fusion.18.base_ref
  19.3 0.0 copy-done.2
  19.3 0.0 copy-start.1
  19.3 0.8 %copy-done.1 = s32[32,512]{1,0:T(8,128)S(1)} copy-done((s32[32,512]{1,0:T(8,128)S(1)}, s32[32,512]{1,0:T(8,128)}, u32[]{:S(2)}) %copy-start.1) | copy-done | bytes 65560
  20.2 0.2 fusion.1.s_ref
  20.4 0.1 fusion.5
  20.5 0.1 fusion.7
  20.6 0.1 fusion.9
  20.7 0.1 fusion.11
  20.8 0.1 fusion.13
  20.9 0.1 fusion.15
  21.0 0.0 copy-start
  21.0 0.1 fusion.17
  21.1 0.1 fusion.3
  21.2 0.2 copy.12
  21.3 0.8 %copy-done = bf16[24,2,64,64]{3,2,1,0:T(8,128)(2,1)S(1)} copy-done((bf16[24,2,64,64]{3,2,1,0:T(8,128)(2,1)S(1)}, bf16[24,2,64,64]{3,2,1,0:T(8,128)(2,1)}, u32[]{:S(2)}) %copy-start) | copy-done | bytes 393240
  22.1 0.8 %copy.10 = bf16[64,24,2,64]{3,2,1,0:T(2,128)(2,1)S(1)} copy(bf16[64,24,2,64]{3,0,2,1:T(8,128)(2,1)S(1)} %bitcast.66) | data formatting | bytes 786432 | tf_op jit(solution)/shard_map/transpose | solution.py:309
  22.9 14.2 %shard_map.68 = (f32[32,128]{1,0:T(8,128)}, f32[32,128]{1,0:T(8,128)}, f32[32,128]{1,0:T(8,128)}) custom-call(f32[896,128]{1,0:T(8,128)S(1)} %bitcast.65, bf16[3072,64]{1,0:T(8,128)(2,1)S(1)} %bitcast.64, bf16[64,2304]{1,0:T(8,128)(2,1)S(1)} %fusion.sel_ref, f32[1,864]{1,0:T(1,128)S(1)} %reshape.64.w_ref, f32[864,128]{1,0:T(8,128)S(1)} %fusion.1.s_ref, ...), custom_call_target="tpu_custom_call" | custom-call | flops 5435817984 | bytes 851968 | tf_op jit(solution)/shard_map/pallas_call | solution.py:148
  (14 shorter events, 0.1 us)
Async XLA Ops:
  0.7 0.7 %copy-start.4 = (f32[24]{0:T(128)S(1)}, f32[24]{0:T(128)}, u32[]{:S(2)}) copy-start(f32[24]{0:T(128)} %param.6) | copy-start | bytes 292
  16.8 2.5 %copy-start.2 = (s32[4,32,512]{2,1,0:T(8,128)S(1)}, s32[4,32,512]{2,1,0:T(8,128)}, u32[]{:S(2)}) copy-start(s32[4,32,512]{2,1,0:T(8,128)} %get-tuple-element.5) | copy-start | bytes 786436
  18.5 0.7 %copy-start.3 = (f32[32,128]{1,0:T(8,128)S(1)}, f32[32,128]{1,0:T(8,128)}, u32[]{:S(2)}) copy-start(f32[32,128]{1,0:T(8,128)} %q_ref.1) | copy-start | bytes 49156
  19.3 0.8 %copy-start.1 = (s32[32,512]{1,0:T(8,128)S(1)}, s32[32,512]{1,0:T(8,128)}, u32[]{:S(2)}) copy-start(s32[32,512]{1,0:T(8,128)} %mask_ref.1) | copy-start | bytes 196612
  21.0 1.1 %copy-start = (bf16[24,2,64,64]{3,2,1,0:T(8,128)(2,1)S(1)}, bf16[24,2,64,64]{3,2,1,0:T(8,128)(2,1)}, u32[]{:S(2)}) copy-start(bf16[24,2,64,64]{3,2,1,0:T(8,128)(2,1)} %param.5) | copy-start | bytes 1179652

commit v6 on v5

--- a/solution.py
+++ b/solution.py
@@ -16,6 +16,7 @@
 EXPOSURE = 0.35
 
 BLOCKS = 8
+HALO = STEPS
 TAP_GROUP = 8
 
 
@@ -203,13 +204,23 @@
         count = count + here.astype(jnp.int32)
     pl.semaphore_wait(barrier, count)
 
-    plan = [(mask_ref, mask_slots, slot, offset) for slot, offset in enumerate(MASK_FROM)]
-    plan += [(q_ref, q_slots, slot, offset) for slot, offset in enumerate(QUENCH_FROM)]
+    def rows_for(source, dt, whole):
+        height = source.shape[0]
+        if abs(dt) == 1 and whole:
+            return 0, height
+        return (height - HALO, HALO) if dt < 0 else (0, HALO)
+
+    plan = [(mask_ref, mask_slots, slot, offset, True) for slot, offset in enumerate(MASK_FROM)]
+    plan += [(q_ref, q_slots, slot, offset, False) for slot, offset in enumerate(QUENCH_FROM)]
     copies = []
-    for index, (source, slots, slot, (dt, dq)) in enumerate(plan):
+    for index, (source, slots, slot, (dt, dq), whole) in enumerate(plan):
+        if dt == 0:
+            first, count = 0, source.shape[0]
+        else:
+            first, count = rows_for(source, dt, whole)
         copy = pltpu.make_async_remote_copy(
-            src_ref=source,
-            dst_ref=slots.at[slot],
+            src_ref=source.at[pl.ds(first, count)],
+            dst_ref=slots.at[slot, pl.ds(first, count)],
             send_sem=send_sems.at[index],
             recv_sem=recv_sems.at[index],
             device_id=device(-dt, -dq),
@@ -220,28 +231,24 @@
         def _():
             copy.start()
 
-        copies.append(copy)
-    for copy, (source, slots, slot, (dt, dq)) in zip(copies, plan):
+        copies.append((copy, first, count))
+    for (copy, first, count), (source, slots, slot, (dt, dq), whole) in zip(copies, plan):
 
         @pl.when(exists(-dt, -dq))
         def _():
             copy.wait_send()
 
-        @pl.when(exists(dt, dq))
+        out = mask_out if slots is mask_slots else q_out
+        here = exists(dt, dq)
+
+        @pl.when(here)
         def _():
             copy.wait_recv()
-
-    for out, slots, offsets in ((mask_out, mask_slots, MASK_FROM), (q_out, q_slots, QUENCH_FROM)):
-        for slot, (dt, dq) in enumerate(offsets):
-            here = exists(dt, dq)
-
-            @pl.when(here)
-            def _():
-                out[slot] = slots[slot]
-
-            @pl.when(jnp.logical_not(here))
-            def _():
-                out[slot] = jnp.zeros(out.shape[1:], out.dtype)
+            out[slot, pl.ds(first, count)] = slots[slot, pl.ds(first, count)]
+
+        @pl.when(jnp.logical_not(here))
+        def _():
+            out[slot] = jnp.zeros(out.shape[1:], out.dtype)
 
 
 def exchange(mask, quencher):

time: 37.5 us -> 35.7 us (0.952)
  Pallas kernels: 29.3 us -> 27.5 us
    pallas_call x1, Pallas kernels: 15.1 us -> 13.3 us  [exchange(): pl.pallas_call(exchange_kernel, out_shape=(jax.ShapeDtypeStruct(mask_shap...]
where the time goes in v6:
time: 35.7 us; the launch traced here: 35.4 us
  Pallas kernels  27.5 us (77%)
  local copies, waits for them, and re-layouts  6.55 us (18%)
  between operations  0.83 us (2%)
  other arithmetic  0.46 us (1%)
    pallas_call x1, Pallas kernels, resist_of(): pl.pallas_call(functools.partial(field_kernel, out_rows=out_rows, pairs=p...  14.2 us
    pallas_call x1, Pallas kernels, exchange(): pl.pallas_call(exchange_kernel, out_shape=(jax.ShapeDtypeStruct(mask_shap...  13.3 us
    unnamed x21, local copies, waits for them, and re-layouts  3.49 us
    squeeze x1, local copies, waits for them, and re-layouts, on_device(): q_from[0][-halo:, -halo:]  0.81 us
    transpose x1, local copies, waits for them, and re-layouts, on_device(): jnp.transpose(kernels, (2, 0, 1, 3)).reshape(ambit * pairs, ambit)  0.81 us
    slice x1, local copies, waits for them, and re-layouts, on_device(): q_from[1][-halo:]  0.73 us

profile of v6, /device:TPU:129, one launch (start us, length us, event | category | flops | bytes accessed | tf_op | source)
XLA Modules:
  0.0 35.4 jit_solution(9917150384598946984)
XLA Ops:
  0.7 0.0 copy-start.4
  0.7 0.1 and_convert_fusion.keep_ref
  0.8 0.6 %copy-done.4 = f32[24]{0:T(128)S(1)} copy-done((f32[24]{0:T(128)S(1)}, f32[24]{0:T(128)}, u32[]{:S(2)}) %copy-start.4) | copy-done | bytes 120
  1.4 0.1 broadcast_in_dim.2
  1.5 0.2 reshape.64.w_ref
  1.6 0.1 fusion.sel_ref
  1.7 13.3 %shard_map.67 = (s32[4,32,512]{2,1,0:T(8,128)}, f32[8,32,128]{2,1,0:T(8,128)}) custom-call(s32[32,512]{1,0:T(8,128)} %mask_ref.1, f32[32,128]{1,0:T(8,128)} %q_ref.1), custom_call_target="tpu_custom_call" | custom-call | tf_op jit(solution)/shard_map/pallas_call | solution.py:258
  15.0 0.0 copy-start.2
  15.0 0.7 %slice_bitcast_fusion.7 = (f32[8,128]{1,0:T(8,128)S(1)}, f32[8,128]{1,0:T(8,128)S(1)}) fusion(f32[8,32,128]{2,1,0:T(8,128)} %get-tuple-element.6), kind=kLoop, calls=%fused_computation.58 | loop fusion | bytes 16384 | tf_op jit(solution)/shard_map/slice | solution.py:292
  15.7 0.8 %slice_bitcast_fusion.5 = (f32[32,128]{1,0:T(8,128)S(1)}, f32[32,128]{1,0:T(8,128)S(1)}, f32[32,128]{1,0:T(8,128)S(1)}, f32[32,128]{1,0:T(8,128)S(1)}, f32[32,128]{1,0:T(8,128)S(1)}, /*index=5*/f32[32,128]{1,0:T(8,128)S(1)}) fusion(f32[8,32,128]{2,1,0:T(8,128)} %get-tuple-element.6), kind=kLoop, calls=%fused_computation.49 | loop fusion | bytes 196608 | tf_op jit(solution)/shard_map/squeeze | solution.py:292
  16.5 0.1 slice.128
  16.6 0.1 slice.132
  16.7 0.1 slice.130
  16.8 0.6 %copy-done.3 = f32[32,128]{1,0:T(8,128)S(1)} copy-done((f32[32,128]{1,0:T(8,128)S(1)}, f32[32,128]{1,0:T(8,128)}, u32[]{:S(2)}) %copy-start.3) | copy-done | bytes 16408
  17.4 0.1 fusion.18.base_ref
  17.5 0.0 copy-done.2
  17.5 0.0 copy-start.1
  17.5 0.8 %copy-done.1 = s32[32,512]{1,0:T(8,128)S(1)} copy-done((s32[32,512]{1,0:T(8,128)S(1)}, s32[32,512]{1,0:T(8,128)}, u32[]{:S(2)}) %copy-start.1) | copy-done | bytes 65560
  18.4 0.2 fusion.1.s_ref
  18.6 0.1 fusion.5
  18.7 0.1 fusion.7
  18.8 0.1 fusion.9
  18.9 0.1 fusion.11
  19.0 0.1 fusion.13
  19.1 0.1 fusion.15
  19.2 0.0 copy-start
  19.2 0.1 fusion.17
  19.3 0.1 fusion.3
  19.4 0.2 copy.12
  19.6 0.8 %copy-done = bf16[24,2,64,64]{3,2,1,0:T(8,128)(2,1)S(1)} copy-done((bf16[24,2,64,64]{3,2,1,0:T(8,128)(2,1)S(1)}, bf16[24,2,64,64]{3,2,1,0:T(8,128)(2,1)}, u32[]{:S(2)}) %copy-start) | copy-done | bytes 393240
  20.3 0.8 %copy.10 = bf16[64,24,2,64]{3,2,1,0:T(2,128)(2,1)S(1)} copy(bf16[64,24,2,64]{3,0,2,1:T(8,128)(2,1)S(1)} %bitcast.66) | data formatting | bytes 786432 | tf_op jit(solution)/shard_map/transpose | solution.py:316
  21.1 14.2 %shard_map.68 = (f32[32,128]{1,0:T(8,128)}, f32[32,128]{1,0:T(8,128)}, f32[32,128]{1,0:T(8,128)}) custom-call(f32[896,128]{1,0:T(8,128)S(1)} %bitcast.65, bf16[3072,64]{1,0:T(8,128)(2,1)S(1)} %bitcast.64, bf16[64,2304]{1,0:T(8,128)(2,1)S(1)} %fusion.sel_ref, f32[1,864]{1,0:T(1,128)S(1)} %reshape.64.w_ref, f32[864,128]{1,0:T(8,128)S(1)} %fusion.1.s_ref, ...), custom_call_target="tpu_custom_call" | custom-call | flops 5435817984 | bytes 851968 | tf_op jit(solution)/shard_map/pallas_call | solution.py:149
  (14 shorter events, 0.1 us)
Async XLA Ops:
  0.7 0.7 %copy-start.4 = (f32[24]{0:T(128)S(1)}, f32[24]{0:T(128)}, u32[]{:S(2)}) copy-start(f32[24]{0:T(128)} %param.6) | copy-start | bytes 292
  15.0 2.5 %copy-start.2 = (s32[4,32,512]{2,1,0:T(8,128)S(1)}, s32[4,32,512]{2,1,0:T(8,128)}, u32[]{:S(2)}) copy-start(s32[4,32,512]{2,1,0:T(8,128)} %get-tuple-element.5) | copy-start | bytes 786436
  16.7 0.7 %copy-start.3 = (f32[32,128]{1,0:T(8,128)S(1)}, f32[32,128]{1,0:T(8,128)}, u32[]{:S(2)}) copy-start(f32[32,128]{1,0:T(8,128)} %q_ref.1) | copy-start | bytes 49156
  17.5 0.8 %copy-start.1 = (s32[32,512]{1,0:T(8,128)S(1)}, s32[32,512]{1,0:T(8,128)}, u32[]{:S(2)}) copy-start(s32[32,512]{1,0:T(8,128)} %mask_ref.1) | copy-start | bytes 196612
  19.2 1.1 %copy-start = (bf16[24,2,64,64]{3,2,1,0:T(8,128)(2,1)S(1)}, bf16[24,2,64,64]{3,2,1,0:T(8,128)(2,1)}, u32[]{:S(2)}) copy-start(bf16[24,2,64,64]{3,2,1,0:T(8,128)(2,1)} %param.5) | copy-start | bytes 1179652

commit v7 on v6

--- a/solution.py
+++ b/solution.py
@@ -273,6 +273,196 @@
     )(mask, quencher)
 
 
+def fused_kernel(
+    mask_ref, q_ref, k_ref, sel_ref, w_ref, s_ref, keep_ref,
+    i_out, a_out, b_out,
+    mask_slots, q_slots, send_sems, recv_sems, taps_ref, win_ref, acc_ref, red_ref,
+    *, pairs, window, halo,
+):
+    tile = lax.axis_index("tile")
+    kern = lax.axis_index("kern")
+    tiles = lax.axis_size("tile")
+    kerns = lax.axis_size("kern")
+    local_rows, local_cols = q_ref.shape
+    out_rows = local_rows + 2 * halo
+    out_cols = local_cols + 2 * halo
+    width = sel_ref.shape[1] // window
+    lanes = keep_ref.shape[1]
+    groups = k_ref.shape[0] // (TAP_GROUP * pairs)
+    span = TAP_GROUP * window
+
+    def exists(dt, dq):
+        return (tile + dt >= 0) & (tile + dt < tiles) & (kern + dq >= 0) & (kern + dq < kerns)
+
+    def device(dt, dq):
+        return {"tile": tile + dt, "kern": kern + dq}
+
+    barrier = pltpu.get_barrier_semaphore()
+    partners = sorted(set(MASK_FROM) | set(QUENCH_FROM))
+    count = jnp.int32(0)
+    for dt, dq in partners:
+        here = exists(dt, dq)
+
+        @pl.when(here)
+        def _():
+            pl.semaphore_signal(
+                barrier, 1, device_id=device(dt, dq), device_id_type=pl.DeviceIdType.MESH
+            )
+
+        count = count + here.astype(jnp.int32)
+    pl.semaphore_wait(barrier, count)
+
+    def rows_for(source, dt, whole):
+        height = source.shape[0]
+        if dt == 0 or (abs(dt) == 1 and whole):
+            return 0, height
+        return (height - HALO, HALO) if dt < 0 else (0, HALO)
+
+    plan = [(mask_ref, mask_slots, slot, offset, True) for slot, offset in enumerate(MASK_FROM)]
+    plan += [(q_ref, q_slots, slot, offset, False) for slot, offset in enumerate(QUENCH_FROM)]
+    copies = []
+    for index, (source, slots, slot, (dt, dq), whole) in enumerate(plan):
+        first, rows = rows_for(source, dt, whole)
+        copy = pltpu.make_async_remote_copy(
+            src_ref=source.at[pl.ds(first, rows)],
+            dst_ref=slots.at[slot, pl.ds(first, rows)],
+            send_sem=send_sems.at[index],
+            recv_sem=recv_sems.at[index],
+            device_id=device(-dt, -dq),
+            device_id_type=pl.DeviceIdType.MESH,
+        )
+
+        @pl.when(exists(-dt, -dq))
+        def _():
+            copy.start()
+
+        copies.append(copy)
+
+    def build(group, carry):
+        first = pl.multiple_of(group * TAP_GROUP * pairs, TAP_GROUP * pairs)
+        product = jnp.dot(
+            k_ref[pl.ds(first, TAP_GROUP * pairs), :], sel_ref[...],
+            preferred_element_type=jnp.float32,
+        ).astype(jnp.bfloat16)
+        columns = [
+            jnp.concatenate(
+                [
+                    product[j * pairs : (j + 1) * pairs, o * window : (o + 1) * window]
+                    for o in range(width)
+                ],
+                axis=0,
+            )
+            for j in range(TAP_GROUP)
+        ]
+        taps_ref[:, pl.ds(pl.multiple_of(group * span, span), span)] = jnp.concatenate(
+            columns, axis=1
+        )
+        return carry
+
+    lax.fori_loop(0, groups, build, 0)
+
+    for copy, (source, slots, slot, (dt, dq), whole) in zip(copies, plan):
+
+        @pl.when(exists(-dt, -dq))
+        def _():
+            copy.wait_send()
+
+        @pl.when(exists(dt, dq))
+        def _():
+            copy.wait_recv()
+
+    def slot_rows(slots, slot, first, rows):
+        dt, dq = (MASK_FROM if slots is mask_slots else QUENCH_FROM)[slot]
+        value = slots[slot, pl.ds(first, rows), :]
+        return jnp.where(exists(dt, dq), value, jnp.zeros_like(value))
+
+    reach = HALO
+    rows = jnp.concatenate(
+        [
+            slot_rows(mask_slots, 2, local_rows - reach, reach),
+            slot_rows(mask_slots, 0, 0, local_rows),
+            mask_ref[...],
+            slot_rows(mask_slots, 1, 0, local_rows),
+            slot_rows(mask_slots, 3, 0, reach),
+        ],
+        axis=0,
+    ).astype(jnp.float32)
+    total = rows.shape[1] + 128
+    rows = jnp.concatenate([rows, jnp.zeros((rows.shape[0], 128), jnp.float32)], axis=1)
+    lead = (win_ref.shape[0] // BLOCKS - out_rows) // 2 + halo
+    for block in range(BLOCKS):
+        start = kern * local_cols - lead + width * block
+        part = pltpu.roll(rows, lax.rem(total - start, total), 1)[:, :window]
+        win_ref[pl.ds(block, rows.shape[0], stride=BLOCKS), :] = part
+
+    def band(left, middle, right):
+        lane = lax.broadcasted_iota(jnp.int32, (middle.shape[0], lanes), 1)
+
+        def widen(value):
+            return jnp.concatenate(
+                [value, jnp.zeros((value.shape[0], lanes - value.shape[1]), value.dtype)], axis=1
+            )
+
+        outer = lanes - (local_cols - halo)
+        return jnp.where(
+            lane < halo,
+            pltpu.roll(widen(left), outer, 1),
+            jnp.where(
+                lane < halo + local_cols,
+                pltpu.roll(widen(middle), halo, 1),
+                jnp.where(lane < out_cols, pltpu.roll(widen(right), outer, 1), 0.0),
+            ),
+        )
+
+    low = local_rows - halo
+    base = jnp.concatenate(
+        [
+            band(*(slot_rows(q_slots, s, low, halo) for s in (0, 1, 2))),
+            band(slot_rows(q_slots, 3, 0, local_rows), q_ref[...], slot_rows(q_slots, 4, 0, local_rows)),
+            band(*(slot_rows(q_slots, s, 0, halo) for s in (5, 6, 7))),
+        ],
+        axis=0,
+    )
+
+    acc_ref[...] = jnp.zeros_like(acc_ref)
+
+    def accumulate(group, carry):
+        pieces = []
+        for offset in range(TAP_GROUP):
+            start = pl.multiple_of((group * TAP_GROUP + offset) * BLOCKS, BLOCKS)
+            pieces.append(win_ref[pl.ds(start, out_rows * BLOCKS), :].astype(jnp.bfloat16))
+        left = jnp.concatenate(pieces, axis=1)
+        right = taps_ref[:, pl.ds(pl.multiple_of(group * span, span), span)]
+        acc_ref[...] += lax.dot_general(
+            left, right, (((1,), (1,)), ((), ())), preferred_element_type=jnp.float32
+        )
+        return carry
+
+    lax.fori_loop(0, groups, accumulate, 0)
+
+    field = acc_ref[...]
+    weighted = field * field * w_ref[...]
+    red_ref[...] = jnp.dot(
+        weighted, s_ref[...], precision=lax.Precision.HIGHEST,
+        preferred_element_type=jnp.float32,
+    )
+    intensity = jnp.zeros((out_rows, lanes), jnp.float32)
+    for block in range(BLOCKS):
+        part = red_ref[pl.ds(block, out_rows, stride=BLOCKS), :]
+        part = jnp.concatenate([part, jnp.zeros_like(part)], axis=1)
+        intensity = intensity + pltpu.roll(part, width * block, 1) if block else part
+    keep = keep_ref[...] > 0.5
+    acid = jnp.where(keep, 1.0 - jnp.exp(-EXPOSURE * intensity), 0.0)
+    for _ in range(STEPS):
+        quenched = QUENCH_RATE * acid * base
+        acid_next = acid + DIFFUSE_ACID * spread_of(acid) - quenched
+        base_next = base + DIFFUSE_BASE * spread_of(base) - quenched
+        acid = jnp.where(keep, acid_next, 0.0)
+        base = jnp.where(keep, base_next, 0.0)
+    for out, value in ((i_out, intensity), (a_out, acid), (b_out, base)):
+        out[...] = pltpu.roll(value, lanes - halo, 1)[halo : halo + local_rows, :local_cols]
+
+
 def on_device(mask, kernels, socs_weights, quencher):
     ambit = kernels.shape[2]
     half_ambit = ambit // 2
@@ -281,36 +471,13 @@
     tile_index = lax.axis_index("tile")
     local_rows = mask.shape[0]
     local_cols = quencher.shape[1]
-    halo = STEPS
+    halo = HALO
     out_rows = local_rows + 2 * halo
     out_cols = local_cols + 2 * halo
     width = out_cols // BLOCKS
     window = 128
-
-    mask_from, q_from = exchange(mask, quencher)
-    top = jnp.concatenate(
-        [q_from[0][-halo:, -halo:], q_from[1][-halo:], q_from[2][-halo:, :halo]], axis=1
-    )
-    middle = jnp.concatenate([q_from[3][:, -halo:], quencher, q_from[4][:, :halo]], axis=1)
-    bottom = jnp.concatenate(
-        [q_from[5][:halo, -halo:], q_from[6][:halo], q_from[7][:halo, :halo]], axis=1
-    )
-    base = jnp.concatenate([top, middle, bottom], axis=0)
-
-    reach = halo + half_ambit - local_rows
-    rows = jnp.concatenate(
-        [mask_from[2][local_rows - reach :], mask_from[0], mask, mask_from[1], mask_from[3][:reach]],
-        axis=0,
-    ).astype(jnp.float32)
-    lead = halo + half_ambit
-    span = width * (BLOCKS - 1) + window
-    total_cols = mask.shape[1]
-    padded = jnp.pad(rows, ((0, 0), (lead, span + local_cols * kern_count - total_cols)))
-    cols = lax.dynamic_slice_in_dim(padded, kern_index * local_cols, span, axis=1)
-    windows = jnp.stack(
-        [cols[:, width * block : width * block + window] for block in range(BLOCKS)], axis=1
-    )
-    windows = windows.reshape(-1, window)
+    lanes = 2 * window
+    window_rows = out_rows + ambit
 
     pairs = kernels.shape[0] * kernels.shape[1]
     kernel_rows = jnp.transpose(kernels, (2, 0, 1, 3)).reshape(ambit * pairs, ambit)
@@ -318,22 +485,44 @@
     lane_weights = jnp.broadcast_to(
         socs_weights[None, :, None], (width, kernels.shape[0], kernels.shape[1])
     ).reshape(1, width * pairs)
-    lanes = 2 * window
     summer = (
         lax.iota(jnp.int32, width * pairs)[:, None] // pairs == lax.iota(jnp.int32, window)[None, :]
     ).astype(jnp.float32)
-
     rows_total = local_rows * lax.axis_size("tile")
     cols_total = local_cols * kern_count
     r = tile_index * local_rows - halo + lax.broadcasted_iota(jnp.int32, (out_rows, lanes), 0)
     c = kern_index * local_cols - halo + lax.broadcasted_iota(jnp.int32, (out_rows, lanes), 1)
     keep = (r >= 0) & (r < rows_total) & (c >= 0) & (c < cols_total)
     keep = (keep & (c < kern_index * local_cols - halo + out_cols)).astype(jnp.float32)
-    base = jnp.pad(base, ((0, 0), (0, lanes - out_cols)))
-    return resist_of(
-        windows, kernel_rows, selector, lane_weights, summer, keep, base,
-        out_rows, ambit, halo, (local_rows, local_cols),
-    )
+
+    vmem = pl.BlockSpec(memory_space=pltpu.VMEM)
+    out = jax.ShapeDtypeStruct((local_rows, local_cols), jnp.float32)
+    copies = len(MASK_FROM) + len(QUENCH_FROM)
+    m_rows = out_rows * BLOCKS
+    return pl.pallas_call(
+        functools.partial(fused_kernel, pairs=pairs, window=window, halo=halo),
+        out_shape=(out, out, out),
+        in_specs=[vmem] * 7,
+        out_specs=(vmem, vmem, vmem),
+        scratch_shapes=[
+            pltpu.VMEM((len(MASK_FROM),) + mask.shape, mask.dtype),
+            pltpu.VMEM((len(QUENCH_FROM),) + quencher.shape, quencher.dtype),
+            pltpu.SemaphoreType.DMA((copies,)),
+            pltpu.SemaphoreType.DMA((copies,)),
+            pltpu.VMEM((width * pairs, ambit * window), jnp.bfloat16),
+            pltpu.VMEM((window_rows * BLOCKS, window), jnp.float32),
+            pltpu.VMEM((m_rows, width * pairs), jnp.float32),
+            pltpu.VMEM((m_rows, window), jnp.float32),
+        ],
+        compiler_params=pltpu.CompilerParams(
+            collective_id=0, has_side_effects=True, vmem_limit_bytes=56 * 1024 * 1024
+        ),
+        cost_estimate=pl.CostEstimate(
+            flops=2 * m_rows * ambit * window * width * pairs,
+            transcendentals=0,
+            bytes_accessed=kernel_rows.size * 2 + mask.size * 4 * 5,
+        ),
+    )(mask, quencher, kernel_rows, selector, lane_weights, summer, keep)
 
 
 def solution(mesh):

time: 35.7 us -> 33.9 us (0.950)
  Pallas kernels: 27.5 us -> 24.6 us
  other arithmetic: 0.46 us -> 2.47 us
  local copies, waits for them, and re-layouts: 6.55 us -> 5.84 us
    pallas_call x2 -> x1, Pallas kernels: 27.5 us -> 24.6 us  [on_device(): pl.pallas_call(functools.partial(fused_kernel, pairs=pairs, window=window...]
    slice x6 -> x0, local copies, waits for them, and re-layouts: 0.95 us -> none  [the longest x1 0.73 us: on_device(): q_from[1][-halo:]]
    transpose x1, local copies, waits for them, and re-layouts: 0.81 us -> 1.7 us  [on_device(): jnp.transpose(kernels, (2, 0, 1, 3)).reshape(ambit * pairs, ambit)]
    unnamed x21 -> x9, local copies, waits for them, and re-layouts: 3.49 us -> 2.67 us
    squeeze x1 -> x0, local copies, waits for them, and re-layouts: 0.81 us -> none  [on_device(): q_from[0][-halo:, -halo:]]
    convert_element_type x1, other arithmetic: 0.18 us -> 0.96 us  [on_device(): summer = (lax.iota(jnp.int32, width * pairs)[:, None] // pairs == lax.iot...]
    convert_element_type x1, other arithmetic: 0.05 us -> 0.78 us  [toeplitz_selector(): selector = (offsets == tap_ids[:, None, None]).astype(jnp.bfloat16)]
    broadcast_in_dim x1, local copies, waits for them, and re-layouts: 0.08 us -> 0.74 us  [on_device(): jnp.broadcast_to(socs_weights[None, :, None], (width, kernels.shape[0], k...]
where the time goes in v7:
time: 33.9 us; the launch traced here: 33.6 us
  Pallas kernels  24.6 us (73%)
  local copies, waits for them, and re-layouts  5.84 us (17%)
  other arithmetic  2.47 us (7%)
  between operations  0.7 us (2%)
    pallas_call x1, Pallas kernels, on_device(): pl.pallas_call(functools.partial(fused_kernel, pairs=pairs, window=window...  24.6 us
    unnamed x9, local copies, waits for them, and re-layouts  2.67 us
    transpose x1, local copies, waits for them, and re-layouts, on_device(): jnp.transpose(kernels, (2, 0, 1, 3)).reshape(ambit * pairs, ambit)  1.7 us
    convert_element_type x1, other arithmetic, on_device(): summer = (lax.iota(jnp.int32, width * pairs)[:, None] // pairs == lax.iot...  0.96 us
    convert_element_type x1, other arithmetic, toeplitz_selector(): selector = (offsets == tap_ids[:, None, None]).astype(jnp.bfloat16)  0.78 us
    reshape x1, local copies, waits for them, and re-layouts, on_device(): lane_weights = jnp.broadcast_to(socs_weights[None, :, None], (width, kern...  0.74 us
    broadcast_in_dim x1, local copies, waits for them, and re-layouts, on_device(): jnp.broadcast_to(socs_weights[None, :, None], (width, kernels.shape[0], k...  0.74 us
    convert_element_type x1, other arithmetic, on_device(): (keep & (c < kern_index * local_cols - halo + out_cols)).astype(jnp.float32)  0.69 us

profile of v7, /device:TPU:129, one launch (start us, length us, event | category | flops | bytes accessed | tf_op | source)
XLA Modules:
  0.0 33.6 jit_solution(354756015926395593)
XLA Ops:
  0.6 0.0 copy-start
  0.7 0.7 %and_convert_fusion.keep_ref = f32[48,256]{1,0:T(8,128)} fusion(pred[256]{0:T(512)(128)(4,1)S(1)} %get-tuple-element.3, pred[256]{0:T(512)(128)(4,1)S(1)} %get-tuple-element.4, pred[256]{0:T(512)(128)(4,1)S(1)} %fusion.7, pred[48]{0:T(512)(128)(4,1)S(1)} %compare_and_fusion), kind=kLoop, calls=%fused_computation.4 | loop fusion | flops 49152 | bytes 49968 | tf_op jit(solution)/shard_map/convert_element_type | solution.py:496
  1.4 0.7 %broadcast_in_dim.2 = f32[18,24,2]{2,1,0:T(8,128)S(1)} broadcast(f32[24]{0:T(128)} %param.6), dimensions={1} | broadcast | bytes 3552 | tf_op jit(solution)/shard_map/broadcast_in_dim | solution.py:485
  2.2 0.7 %reshape.56.w_ref = f32[1,864]{1,0:T(1,128)} reshape(f32[18,24,2]{2,1,0:T(8,128)S(1)} %broadcast_in_dim.2) | data formatting | bytes 6912 | tf_op jit(solution)/shard_map/reshape | solution.py:487
  2.9 0.8 %fusion.sel_ref = bf16[64,2304]{1,0:T(8,128)(2,1)} fusion(s32[2304]{0:T(1024)S(1)} %subtract_bitcast_fusion), kind=kLoop, calls=%fused_computation.1 | loop fusion | flops 294912 | bytes 304128 | tf_op jit(solution)/shard_map/convert_element_type | solution.py:62
  3.7 1.0 %fusion.1.s_ref = f32[864,128]{1,0:T(8,128)} fusion(s32[864]{0:T(1024)S(1)} %add_select_fusion), kind=kLoop, calls=%fused_computation.3 | loop fusion | flops 221184 | bytes 445824 | tf_op jit(solution)/shard_map/convert_element_type | solution.py:490
  4.6 0.0 copy-done
  4.6 1.7 %copy.8 = bf16[64,24,2,64]{3,2,1,0:T(2,128)(2,1)} copy(bf16[64,24,2,64]{3,0,2,1:T(8,128)(2,1)S(1)} %bitcast.4) | data formatting | bytes 786432 | tf_op jit(solution)/shard_map/transpose | solution.py:483
  6.3 24.6 %shard_map.67 = (f32[32,128]{1,0:T(8,128)}, f32[32,128]{1,0:T(8,128)}, f32[32,128]{1,0:T(8,128)}) custom-call(s32[32,512]{1,0:T(8,128)} %mask_ref.1, f32[32,128]{1,0:T(8,128)} %q_ref.1, bf16[3072,64]{1,0:T(8,128)(2,1)} %bitcast.5, bf16[64,2304]{1,0:T(8,128)(2,1)} %fusion.sel_ref, f32[1,864]{1,0:T(1,128)} %reshape.56.w_ref, f32[864,128]{1,0:T(8,128)} %fusion.1.s_ref, ...), custom_call_target="tpu_custom_call" | custom-call | flops 5435817984 | bytes 720896 | tf_op jit(solution)/shard_map/pallas_call | solution.py:502
  30.9 0.0 copy-start.2
  30.9 1.3 %copy.12 = f32[32,128]{1,0:T(8,128)} copy(f32[32,128]{1,0:T(8,128)} %get-tuple-element.8) | data formatting | bytes 32768
  32.2 0.0 copy-done.2
  32.2 0.0 copy-start.1
  32.2 0.6 %copy.13 = f32[32,128]{1,0:T(8,128)} copy(f32[32,128]{1,0:T(8,128)S(1)} %copy-done.2) | data formatting | bytes 32768
  32.8 0.1 copy-done.1
  33.0 0.6 %copy.14 = f32[32,128]{1,0:T(8,128)} copy(f32[32,128]{1,0:T(8,128)S(1)} %copy-done.1) | data formatting | bytes 32768
  (5 shorter events, 0.0 us)
Async XLA Ops:
  0.6 4.0 %copy-start = (bf16[24,2,64,64]{3,2,1,0:T(8,128)(2,1)S(1)}, bf16[24,2,64,64]{3,2,1,0:T(8,128)(2,1)}, u32[]{:S(2)}) copy-start(bf16[24,2,64,64]{3,2,1,0:T(8,128)(2,1)} %param.5) | copy-start | bytes 1179652
  30.9 1.3 %copy-start.2 = (f32[32,128]{1,0:T(8,128)S(1)}, f32[32,128]{1,0:T(8,128)}, u32[]{:S(2)}) copy-start(f32[32,128]{1,0:T(8,128)} %get-tuple-element.9) | copy-start | bytes 49156
  32.2 0.7 %copy-start.1 = (f32[32,128]{1,0:T(8,128)S(1)}, f32[32,128]{1,0:T(8,128)}, u32[]{:S(2)}) copy-start(f32[32,128]{1,0:T(8,128)} %get-tuple-element.10) | copy-start | bytes 49156

commit v8 on v7

--- a/solution.py
+++ b/solution.py
@@ -274,10 +274,10 @@
 
 
 def fused_kernel(
-    mask_ref, q_ref, k_ref, sel_ref, w_ref, s_ref, keep_ref,
+    mask_ref, q_ref, k_ref, w_smem,
     i_out, a_out, b_out,
     mask_slots, q_slots, send_sems, recv_sems, taps_ref, win_ref, acc_ref, red_ref,
-    *, pairs, window, halo,
+    *, pairs, window, halo, width,
 ):
     tile = lax.axis_index("tile")
     kern = lax.axis_index("kern")
@@ -286,10 +286,11 @@
     local_rows, local_cols = q_ref.shape
     out_rows = local_rows + 2 * halo
     out_cols = local_cols + 2 * halo
-    width = sel_ref.shape[1] // window
-    lanes = keep_ref.shape[1]
+    lanes = 2 * window
+    ambit = k_ref.shape[1]
     groups = k_ref.shape[0] // (TAP_GROUP * pairs)
     span = TAP_GROUP * window
+    width_n = width * pairs
 
     def exists(dt, dq):
         return (tile + dt >= 0) & (tile + dt < tiles) & (kern + dq >= 0) & (kern + dq < kerns)
@@ -338,10 +339,14 @@
 
         copies.append(copy)
 
+    sel_lane = lax.broadcasted_iota(jnp.int32, (ambit, width * window), 1)
+    sel_row = lax.broadcasted_iota(jnp.int32, (ambit, width * window), 0)
+    selector = (sel_lane % window - sel_lane // window == sel_row).astype(jnp.bfloat16)
+
     def build(group, carry):
         first = pl.multiple_of(group * TAP_GROUP * pairs, TAP_GROUP * pairs)
         product = jnp.dot(
-            k_ref[pl.ds(first, TAP_GROUP * pairs), :], sel_ref[...],
+            k_ref[pl.ds(first, TAP_GROUP * pairs), :], selector,
             preferred_element_type=jnp.float32,
         ).astype(jnp.bfloat16)
         columns = [
@@ -440,10 +445,18 @@
 
     lax.fori_loop(0, groups, accumulate, 0)
 
+    kernel_of_lane = lax.broadcasted_iota(jnp.int32, (1, width_n), 1) % pairs // 2
+    lane_weights = jnp.zeros((1, width_n), jnp.float32)
+    for k in range(pairs // 2):
+        lane_weights = jnp.where(kernel_of_lane == k, w_smem[k], lane_weights)
+    summer = (
+        lax.broadcasted_iota(jnp.int32, (width_n, window), 0) // pairs
+        == lax.broadcasted_iota(jnp.int32, (width_n, window), 1)
+    ).astype(jnp.float32)
     field = acc_ref[...]
-    weighted = field * field * w_ref[...]
+    weighted = field * field * lane_weights
     red_ref[...] = jnp.dot(
-        weighted, s_ref[...], precision=lax.Precision.HIGHEST,
+        weighted, summer, precision=lax.Precision.HIGHEST,
         preferred_element_type=jnp.float32,
     )
     intensity = jnp.zeros((out_rows, lanes), jnp.float32)
@@ -451,7 +464,10 @@
         part = red_ref[pl.ds(block, out_rows, stride=BLOCKS), :]
         part = jnp.concatenate([part, jnp.zeros_like(part)], axis=1)
         intensity = intensity + pltpu.roll(part, width * block, 1) if block else part
-    keep = keep_ref[...] > 0.5
+    r = tile * local_rows - halo + lax.broadcasted_iota(jnp.int32, (out_rows, lanes), 0)
+    c = kern * local_cols - halo + lax.broadcasted_iota(jnp.int32, (out_rows, lanes), 1)
+    keep = (r >= 0) & (r < tiles * local_rows) & (c >= 0) & (c < kerns * local_cols)
+    keep = keep & (c < kern * local_cols - halo + out_cols)
     acid = jnp.where(keep, 1.0 - jnp.exp(-EXPOSURE * intensity), 0.0)
     for _ in range(STEPS):
         quenched = QUENCH_RATE * acid * base
@@ -481,28 +497,15 @@
 
     pairs = kernels.shape[0] * kernels.shape[1]
     kernel_rows = jnp.transpose(kernels, (2, 0, 1, 3)).reshape(ambit * pairs, ambit)
-    selector = toeplitz_selector(ambit, window, width)
-    lane_weights = jnp.broadcast_to(
-        socs_weights[None, :, None], (width, kernels.shape[0], kernels.shape[1])
-    ).reshape(1, width * pairs)
-    summer = (
-        lax.iota(jnp.int32, width * pairs)[:, None] // pairs == lax.iota(jnp.int32, window)[None, :]
-    ).astype(jnp.float32)
-    rows_total = local_rows * lax.axis_size("tile")
-    cols_total = local_cols * kern_count
-    r = tile_index * local_rows - halo + lax.broadcasted_iota(jnp.int32, (out_rows, lanes), 0)
-    c = kern_index * local_cols - halo + lax.broadcasted_iota(jnp.int32, (out_rows, lanes), 1)
-    keep = (r >= 0) & (r < rows_total) & (c >= 0) & (c < cols_total)
-    keep = (keep & (c < kern_index * local_cols - halo + out_cols)).astype(jnp.float32)
 
     vmem = pl.BlockSpec(memory_space=pltpu.VMEM)
     out = jax.ShapeDtypeStruct((local_rows, local_cols), jnp.float32)
     copies = len(MASK_FROM) + len(QUENCH_FROM)
     m_rows = out_rows * BLOCKS
     return pl.pallas_call(
-        functools.partial(fused_kernel, pairs=pairs, window=window, halo=halo),
+        functools.partial(fused_kernel, pairs=pairs, window=window, halo=halo, width=width),
         out_shape=(out, out, out),
-        in_specs=[vmem] * 7,
+        in_specs=[vmem] * 3 + [pl.BlockSpec(memory_space=pltpu.SMEM)],
         out_specs=(vmem, vmem, vmem),
         scratch_shapes=[
             pltpu.VMEM((len(MASK_FROM),) + mask.shape, mask.dtype),
@@ -522,7 +525,7 @@
             transcendentals=0,
             bytes_accessed=kernel_rows.size * 2 + mask.size * 4 * 5,
         ),
-    )(mask, quencher, kernel_rows, selector, lane_weights, summer, keep)
+    )(mask, quencher, kernel_rows, socs_weights)
 
 
 def solution(mesh):

time: 33.9 us -> 31 us (0.914)
  other arithmetic: 2.47 us -> 0 us
  local copies, waits for them, and re-layouts: 5.84 us -> 5.5 us
    convert_element_type x3 -> x0, other arithmetic: 2.43 us -> none  [the longest x1 0.96 us: on_device(): summer = (lax.iota(jnp.int32, width * pairs)[:, None] // pairs == lax.iot...]
    transpose x1, local copies, waits for them, and re-layouts: 1.7 us -> 2.84 us  [on_device(): jnp.transpose(kernels, (2, 0, 1, 3)).reshape(ambit * pairs, ambit)]
    reshape x1 -> x0, local copies, waits for them, and re-layouts: 0.74 us -> none  [on_device(): lane_weights = jnp.broadcast_to(socs_weights[None, :, None], (width, kern...]
    broadcast_in_dim x1 -> x0, local copies, waits for them, and re-layouts: 0.74 us -> none  [on_device(): jnp.broadcast_to(socs_weights[None, :, None], (width, kernels.shape[0], k...]
    unnamed x9 -> x7, local copies, waits for them, and re-layouts: 2.67 us -> 2.66 us
where the time goes in v8:
time: 31 us; the launch traced here: 30.6 us
  Pallas kernels  24.5 us (79%)
  local copies, waits for them, and re-layouts  5.5 us (18%)
  between operations  0.65 us (2%)
    pallas_call x1, Pallas kernels, on_device(): pl.pallas_call(functools.partial(fused_kernel, pairs=pairs, window=window...  24.5 us
    transpose x1, local copies, waits for them, and re-layouts, on_device(): jnp.transpose(kernels, (2, 0, 1, 3)).reshape(ambit * pairs, ambit)  2.84 us
    unnamed x7, local copies, waits for them, and re-layouts  2.66 us

profile of v8, /device:TPU:129, one launch (start us, length us, event | category | flops | bytes accessed | tf_op | source)
XLA Modules:
  0.0 30.6 jit_solution(2767739587679025502)
XLA Ops:
  0.6 2.8 %copy.7 = bf16[64,24,2,64]{3,2,1,0:T(2,128)(2,1)} copy(bf16[64,24,2,64]{3,0,2,1:T(8,128)(2,1)} %bitcast.2) | data formatting | bytes 786432 | tf_op jit(solution)/shard_map/transpose | solution.py:499
  3.5 24.5 %shard_map.67 = (f32[32,128]{1,0:T(8,128)}, f32[32,128]{1,0:T(8,128)}, f32[32,128]{1,0:T(8,128)}) custom-call(s32[32,512]{1,0:T(8,128)} %mask_ref.1, f32[32,128]{1,0:T(8,128)} %q_ref.1, bf16[3072,64]{1,0:T(8,128)(2,1)} %bitcast.3, f32[24]{0:T(128)} %w_smem.1), custom_call_target="tpu_custom_call" | custom-call | flops 5435817984 | bytes 720896 | tf_op jit(solution)/shard_map/pallas_call | solution.py:505
  28.0 0.0 copy-start.1
  28.0 1.3 %copy.11 = f32[32,128]{1,0:T(8,128)} copy(f32[32,128]{1,0:T(8,128)} %get-tuple-element.6) | data formatting | bytes 32768
  29.3 0.0 copy-done.1
  29.3 0.0 copy-start
  29.3 0.6 %copy.12 = f32[32,128]{1,0:T(8,128)} copy(f32[32,128]{1,0:T(8,128)S(1)} %copy-done.1) | data formatting | bytes 32768
  29.9 0.1 copy-done
  30.0 0.6 %copy.13 = f32[32,128]{1,0:T(8,128)} copy(f32[32,128]{1,0:T(8,128)S(1)} %copy-done) | data formatting | bytes 32768
Async XLA Ops:
  28.0 1.3 %copy-start.1 = (f32[32,128]{1,0:T(8,128)S(1)}, f32[32,128]{1,0:T(8,128)}, u32[]{:S(2)}) copy-start(f32[32,128]{1,0:T(8,128)} %get-tuple-element.7) | copy-start | bytes 49156
  29.3 0.7 %copy-start = (f32[32,128]{1,0:T(8,128)S(1)}, f32[32,128]{1,0:T(8,128)}, u32[]{:S(2)}) copy-start(f32[32,128]{1,0:T(8,128)} %get-tuple-element.8) | copy-start | bytes 49156

commit v9 on v8

--- a/solution.py
+++ b/solution.py
@@ -276,7 +276,7 @@
 def fused_kernel(
     mask_ref, q_ref, k_ref, w_smem,
     i_out, a_out, b_out,
-    mask_slots, q_slots, send_sems, recv_sems, taps_ref, win_ref, acc_ref, red_ref,
+    mask_slots, q_slots, send_sems, recv_sems, taps_ref, win_ref, acc_ref, red_ref, rows_ref,
     *, pairs, window, halo, width,
 ):
     tile = lax.axis_index("tile")
@@ -288,7 +288,7 @@
     out_cols = local_cols + 2 * halo
     lanes = 2 * window
     ambit = k_ref.shape[1]
-    groups = k_ref.shape[0] // (TAP_GROUP * pairs)
+    groups = ambit // TAP_GROUP
     span = TAP_GROUP * window
     width_n = width * pairs
 
@@ -343,11 +343,18 @@
     sel_row = lax.broadcasted_iota(jnp.int32, (ambit, width * window), 0)
     selector = (sel_lane % window - sel_lane // window == sel_row).astype(jnp.bfloat16)
 
+    rows_ref[...] = k_ref[...].astype(jnp.float32)
+
     def build(group, carry):
-        first = pl.multiple_of(group * TAP_GROUP * pairs, TAP_GROUP * pairs)
+        kernel_rows = jnp.concatenate(
+            [
+                rows_ref[pl.ds(group * TAP_GROUP + j, pairs, stride=ambit), :]
+                for j in range(TAP_GROUP)
+            ],
+            axis=0,
+        ).astype(jnp.bfloat16)
         product = jnp.dot(
-            k_ref[pl.ds(first, TAP_GROUP * pairs), :], selector,
-            preferred_element_type=jnp.float32,
+            kernel_rows, selector, preferred_element_type=jnp.float32
         ).astype(jnp.bfloat16)
         columns = [
             jnp.concatenate(
@@ -496,7 +503,7 @@
     window_rows = out_rows + ambit
 
     pairs = kernels.shape[0] * kernels.shape[1]
-    kernel_rows = jnp.transpose(kernels, (2, 0, 1, 3)).reshape(ambit * pairs, ambit)
+    kernel_rows = kernels.reshape(pairs * ambit, ambit)
 
     vmem = pl.BlockSpec(memory_space=pltpu.VMEM)
     out = jax.ShapeDtypeStruct((local_rows, local_cols), jnp.float32)
@@ -516,6 +523,7 @@
             pltpu.VMEM((window_rows * BLOCKS, window), jnp.float32),
             pltpu.VMEM((m_rows, width * pairs), jnp.float32),
             pltpu.VMEM((m_rows, window), jnp.float32),
+            pltpu.VMEM((pairs * ambit, ambit), jnp.float32),
         ],
         compiler_params=pltpu.CompilerParams(
             collective_id=0, has_side_effects=True, vmem_limit_bytes=56 * 1024 * 1024

time: 31 us -> 28.7 us (0.926)
  the two profiles are of different devices: /device:TPU:129 before, /device:TPU:161 now
where the time goes in v9:
time: 28.7 us; the launch traced here: 28.5 us
  Pallas kernels  25.1 us (87%)
  local copies, waits for them, and re-layouts  2.66 us (9%)
  between operations  0.65 us (2%)
    pallas_call x1, Pallas kernels, on_device(): pl.pallas_call(functools.partial(fused_kernel, pairs=pairs, window=window...  25.1 us
    unnamed x7, local copies, waits for them, and re-layouts  2.66 us

profile of v9, /device:TPU:161, one launch (start us, length us, event | category | flops | bytes accessed | tf_op | source)
XLA Modules:
  0.0 28.5 jit_solution(2877446539624637068)
XLA Ops:
  0.6 25.1 %shard_map.67 = (f32[32,128]{1,0:T(8,128)}, f32[32,128]{1,0:T(8,128)}, f32[32,128]{1,0:T(8,128)}) custom-call(s32[32,512]{1,0:T(8,128)} %mask_ref.1, f32[32,128]{1,0:T(8,128)} %q_ref.1, bf16[3072,64]{1,0:T(8,128)(2,1)} %bitcast.1, f32[24]{0:T(128)} %w_smem.1), custom_call_target="tpu_custom_call" | custom-call | flops 5435817984 | bytes 720896 | tf_op jit(solution)/shard_map/pallas_call | solution.py:512
  25.8 0.0 copy-start.1
  25.8 1.3 %copy.10 = f32[32,128]{1,0:T(8,128)} copy(f32[32,128]{1,0:T(8,128)} %get-tuple-element.6) | data formatting | bytes 32768
  27.1 0.0 copy-done.1
  27.1 0.0 copy-start
  27.1 0.6 %copy.11 = f32[32,128]{1,0:T(8,128)} copy(f32[32,128]{1,0:T(8,128)S(1)} %copy-done.1) | data formatting | bytes 32768
  27.7 0.1 copy-done
  27.9 0.6 %copy.12 = f32[32,128]{1,0:T(8,128)} copy(f32[32,128]{1,0:T(8,128)S(1)} %copy-done) | data formatting | bytes 32768
Async XLA Ops:
  25.8 1.3 %copy-start.1 = (f32[32,128]{1,0:T(8,128)S(1)}, f32[32,128]{1,0:T(8,128)}, u32[]{:S(2)}) copy-start(f32[32,128]{1,0:T(8,128)} %get-tuple-element.7) | copy-start | bytes 49156
  27.1 0.7 %copy-start = (f32[32,128]{1,0:T(8,128)S(1)}, f32[32,128]{1,0:T(8,128)}, u32[]{:S(2)}) copy-start(f32[32,128]{1,0:T(8,128)} %get-tuple-element.8) | copy-start | bytes 49156

commit v10 on v9

v10 whole, which is shorter than its diff:
```python
import functools

import jax
import jax.numpy as jnp
from jax import lax
from jax.experimental import pallas as pl
from jax.experimental.pallas import tpu as pltpu
from jax.sharding import PartitionSpec as P

STEPS = 8


DIFFUSE_ACID = 0.2
DIFFUSE_BASE = 0.1
QUENCH_RATE = 0.5
EXPOSURE = 0.35

BLOCKS = 8
HALO = STEPS
TAP_GROUP = 8


def toeplitz_selector(ambit, window, width):
    tap_ids = lax.iota(jnp.int32, ambit)
    input_ids = lax.iota(jnp.int32, window)
    output_ids = lax.iota(jnp.int32, width)
    offsets = input_ids[None, None, :] - output_ids[None, :, None]
    selector = (offsets == tap_ids[:, None, None]).astype(jnp.bfloat16)
    return selector.reshape(ambit, width * window)


def spread_of(value):
    rows, lanes = value.shape
    up = pltpu.roll(value, 1, 0)
    down = pltpu.roll(value, rows - 1, 0)
    left = pltpu.roll(value, 1, 1)
    right = pltpu.roll(value, lanes - 1, 1)
    return up + down + left + right - 4.0 * value


MASK_FROM = ((-1, 0), (1, 0), (-2, 0), (2, 0))
QUENCH_FROM = ((-1, -1), (-1, 0), (-1, 1), (0, -1), (0, 1), (1, -1), (1, 0), (1, 1))


def fused_kernel(
    mask_ref, q_ref, k_ref, w_smem,
    o_ref,
    mask_slots, q_slots, send_sems, recv_sems, taps_ref, win_ref, acc_ref, red_ref, rows_ref,
    *, pairs, window, halo, width,
):
    tile = lax.axis_index("tile")
    kern = lax.axis_index("kern")
    tiles = lax.axis_size("tile")
    kerns = lax.axis_size("kern")
    local_rows, local_cols = q_ref.shape
    out_rows = local_rows + 2 * halo
    out_cols = local_cols + 2 * halo
    lanes = 2 * window
    ambit = k_ref.shape[1]
    groups = ambit // TAP_GROUP
    span = TAP_GROUP * window
    width_n = width * pairs

    def exists(dt, dq):
        return (tile + dt >= 0) & (tile + dt < tiles) & (kern + dq >= 0) & (kern + dq < kerns)

    def device(dt, dq):
        return {"tile": tile + dt, "kern": kern + dq}

    barrier = pltpu.get_barrier_semaphore()
    partners = sorted(set(MASK_FROM) | set(QUENCH_FROM))
    count = jnp.int32(0)
    for dt, dq in partners:
        here = exists(dt, dq)

        @pl.when(here)
        def _():
            pl.semaphore_signal(
                barrier, 1, device_id=device(dt, dq), device_id_type=pl.DeviceIdType.MESH
            )

        count = count + here.astype(jnp.int32)
    pl.semaphore_wait(barrier, count)

    def rows_for(source, dt, whole):
        height = source.shape[0]
        if dt == 0 or (abs(dt) == 1 and whole):
            return 0, height
        return (height - HALO, HALO) if dt < 0 else (0, HALO)

    plan = [(mask_ref, mask_slots, slot, offset, True) for slot, offset in enumerate(MASK_FROM)]
    plan += [(q_ref, q_slots, slot, offset, False) for slot, offset in enumerate(QUENCH_FROM)]
    copies = []
    for index, (source, slots, slot, (dt, dq), whole) in enumerate(plan):
        first, rows = rows_for(source, dt, whole)
        copy = pltpu.make_async_remote_copy(
            src_ref=source.at[pl.ds(first, rows)],
            dst_ref=slots.at[slot, pl.ds(first, rows)],
            send_sem=send_sems.at[index],
            recv_sem=recv_sems.at[index],
            device_id=device(-dt, -dq),
            device_id_type=pl.DeviceIdType.MESH,
        )

        @pl.when(exists(-dt, -dq))
        def _():
            copy.start()

        copies.append(copy)

    sel_lane = lax.broadcasted_iota(jnp.int32, (ambit, width * window), 1)
    sel_row = lax.broadcasted_iota(jnp.int32, (ambit, width * window), 0)
    selector = (sel_lane % window - sel_lane // window == sel_row).astype(jnp.bfloat16)

    rows_ref[...] = k_ref[...].astype(jnp.float32)

    def build(group, carry):
        kernel_rows = jnp.concatenate(
            [
                rows_ref[pl.ds(group * TAP_GROUP + j, pairs, stride=ambit), :]
                for j in range(TAP_GROUP)
            ],
            axis=0,
        ).astype(jnp.bfloat16)
        product = jnp.dot(
            kernel_rows, selector, preferred_element_type=jnp.float32
        ).astype(jnp.bfloat16)
        columns = [
            jnp.concatenate(
                [
                    product[j * pairs : (j + 1) * pairs, o * window : (o + 1) * window]
                    for o in range(width)
                ],
                axis=0,
            )
            for j in range(TAP_GROUP)
        ]
        taps_ref[:, pl.ds(pl.multiple_of(group * span, span), span)] = jnp.concatenate(
            columns, axis=1
        )
        return carry

    lax.fori_loop(0, groups, build, 0)

    def wait_for(kind):
        for copy, (source, slots, slot, (dt, dq), whole) in zip(copies, plan):
            if kind == "send":

                @pl.when(exists(-dt, -dq))
                def _():
                    copy.wait_send()

            elif (slots is mask_slots) == (kind == "mask"):

                @pl.when(exists(dt, dq))
                def _():
                    copy.wait_recv()

    wait_for("mask")

    def slot_rows(slots, slot, first, rows):
        dt, dq = (MASK_FROM if slots is mask_slots else QUENCH_FROM)[slot]
        value = slots[slot, pl.ds(first, rows), :]
        return jnp.where(exists(dt, dq), value, jnp.zeros_like(value))

    reach = HALO
    rows = jnp.concatenate(
        [
            slot_rows(mask_slots, 2, local_rows - reach, reach),
            slot_rows(mask_slots, 0, 0, local_rows),
            mask_ref[...],
            slot_rows(mask_slots, 1, 0, local_rows),
            slot_rows(mask_slots, 3, 0, reach),
        ],
        axis=0,
    ).astype(jnp.float32)
    total = rows.shape[1] + 128
    rows = jnp.concatenate([rows, jnp.zeros((rows.shape[0], 128), jnp.float32)], axis=1)
    lead = (win_ref.shape[0] // BLOCKS - out_rows) // 2 + halo
    for block in range(BLOCKS):
        start = kern * local_cols - lead + width * block
        part = pltpu.roll(rows, lax.rem(total - start, total), 1)[:, :window]
        win_ref[pl.ds(block, rows.shape[0], stride=BLOCKS), :] = part

    def band(left, middle, right):
        lane = lax.broadcasted_iota(jnp.int32, (middle.shape[0], lanes), 1)

        def widen(value):
            return jnp.concatenate(
                [value, jnp.zeros((value.shape[0], lanes - value.shape[1]), value.dtype)], axis=1
            )

        outer = lanes - (local_cols - halo)
        return jnp.where(
            lane < halo,
            pltpu.roll(widen(left), outer, 1),
            jnp.where(
                lane < halo + local_cols,
                pltpu.roll(widen(middle), halo, 1),
                jnp.where(lane < out_cols, pltpu.roll(widen(right), outer, 1), 0.0),
            ),
        )

    acc_ref[...] = jnp.zeros_like(acc_ref)

    def accumulate(group, carry):
        pieces = []
        for offset in range(TAP_GROUP):
            start = pl.multiple_of((group * TAP_GROUP + offset) * BLOCKS, BLOCKS)
            pieces.append(win_ref[pl.ds(start, out_rows * BLOCKS), :].astype(jnp.bfloat16))
        left = jnp.concatenate(pieces, axis=1)
        right = taps_ref[:, pl.ds(pl.multiple_of(group * span, span), span)]
        acc_ref[...] += lax.dot_general(
            left, right, (((1,), (1,)), ((), ())), preferred_element_type=jnp.float32
        )
        return carry

    lax.fori_loop(0, groups, accumulate, 0)

    wait_for("quench")
    wait_for("send")
    low = local_rows - halo
    base = jnp.concatenate(
        [
            band(*(slot_rows(q_slots, s, low, halo) for s in (0, 1, 2))),
            band(slot_rows(q_slots, 3, 0, local_rows), q_ref[...], slot_rows(q_slots, 4, 0, local_rows)),
            band(*(slot_rows(q_slots, s, 0, halo) for s in (5, 6, 7))),
        ],
        axis=0,
    )


    kernel_of_lane = lax.broadcasted_iota(jnp.int32, (1, width_n), 1) % pairs // 2
    lane_weights = jnp.zeros((1, width_n), jnp.float32)
    for k in range(pairs // 2):
        lane_weights = jnp.where(kernel_of_lane == k, w_smem[k], lane_weights)
    summer = (
        lax.broadcasted_iota(jnp.int32, (width_n, window), 0) // pairs
        == lax.broadcasted_iota(jnp.int32, (width_n, window), 1)
    ).astype(jnp.float32)
    field = acc_ref[...]
    weighted = field * field * lane_weights
    red_ref[...] = jnp.dot(
        weighted, summer, precision=lax.Precision.HIGHEST,
        preferred_element_type=jnp.float32,
    )
    intensity = jnp.zeros((out_rows, lanes), jnp.float32)
    for block in range(BLOCKS):
        part = red_ref[pl.ds(block, out_rows, stride=BLOCKS), :]
        part = jnp.concatenate([part, jnp.zeros_like(part)], axis=1)
        intensity = intensity + pltpu.roll(part, width * block, 1) if block else part
    r = tile * local_rows - halo + lax.broadcasted_iota(jnp.int32, (out_rows, lanes), 0)
    c = kern * local_cols - halo + lax.broadcasted_iota(jnp.int32, (out_rows, lanes), 1)
    keep = (r >= 0) & (r < tiles * local_rows) & (c >= 0) & (c < kerns * local_cols)
    keep = keep & (c < kern * local_cols - halo + out_cols)
    acid = jnp.where(keep, 1.0 - jnp.exp(-EXPOSURE * intensity), 0.0)
    for _ in range(STEPS):
        quenched = QUENCH_RATE * acid * base
        acid_next = acid + DIFFUSE_ACID * spread_of(acid) - quenched
        base_next = base + DIFFUSE_BASE * spread_of(base) - quenched
        acid = jnp.where(keep, acid_next, 0.0)
        base = jnp.where(keep, base_next, 0.0)
    for index, value in enumerate((intensity, acid, base)):
        o_ref[index] = pltpu.roll(value, lanes - halo, 1)[halo : halo + local_rows, :local_cols]


def on_device(mask, kernels, socs_weights, quencher):
    ambit = kernels.shape[2]
    half_ambit = ambit // 2
    kern_count = lax.axis_size("kern")
    kern_index = lax.axis_index("kern")
    tile_index = lax.axis_index("tile")
    local_rows = mask.shape[0]
    local_cols = quencher.shape[1]
    halo = HALO
    out_rows = local_rows + 2 * halo
    out_cols = local_cols + 2 * halo
    width = out_cols // BLOCKS
    window = 128
    lanes = 2 * window
    window_rows = out_rows + ambit

    pairs = kernels.shape[0] * kernels.shape[1]
    kernel_rows = kernels.reshape(pairs * ambit, ambit)

    vmem = pl.BlockSpec(memory_space=pltpu.VMEM)
    out = jax.ShapeDtypeStruct((3, local_rows, local_cols), jnp.float32)
    copies = len(MASK_FROM) + len(QUENCH_FROM)
    m_rows = out_rows * BLOCKS
    result = pl.pallas_call(
        functools.partial(fused_kernel, pairs=pairs, window=window, halo=halo, width=width),
        out_shape=out,
        in_specs=[vmem] * 3 + [pl.BlockSpec(memory_space=pltpu.SMEM)],
        out_specs=vmem,
        scratch_shapes=[
            pltpu.VMEM((len(MASK_FROM),) + mask.shape, mask.dtype),
            pltpu.VMEM((len(QUENCH_FROM),) + quencher.shape, quencher.dtype),
            pltpu.SemaphoreType.DMA((copies,)),
            pltpu.SemaphoreType.DMA((copies,)),
            pltpu.VMEM((width * pairs, ambit * window), jnp.bfloat16),
            pltpu.VMEM((window_rows * BLOCKS, window), jnp.float32),
            pltpu.VMEM((m_rows, width * pairs), jnp.float32),
            pltpu.VMEM((m_rows, window), jnp.float32),
            pltpu.VMEM((pairs * ambit, ambit), jnp.float32),
        ],
        compiler_params=pltpu.CompilerParams(
            collective_id=0, has_side_effects=True, vmem_limit_bytes=56 * 1024 * 1024
        ),
        cost_estimate=pl.CostEstimate(
            flops=2 * m_rows * ambit * window * width * pairs,
            transcendentals=0,
            bytes_accessed=kernel_rows.size * 2 + mask.size * 4 * 5,
        ),
    )(mask, quencher, kernel_rows, socs_weights)
    return result[0], result[1], result[2]


def solution(mesh):
    placed = (P("tile", None), P(), P(), P("tile", "kern"))
    return jax.shard_map(
        on_device,
        mesh=mesh,
        in_specs=placed,
        out_specs=(P("tile", "kern"), P("tile", "kern"), P("tile", "kern")),
        check_vma=False,
    )
```

time: 28.7 us -> 27.3 us (0.951)
  local copies, waits for them, and re-layouts: 2.66 us -> 1.37 us
    unnamed x7 -> x0, local copies, waits for them, and re-layouts: 2.66 us -> none
    squeeze x0 -> x1, local copies, waits for them, and re-layouts: none -> 1.37 us  [on_device(): return (result[0], result[1], result[2])]
where the time goes in v10:
time: 27.3 us; the launch traced here: 27.1 us
  Pallas kernels  25.1 us (92%)
  local copies, waits for them, and re-layouts  1.37 us (5%)
  between operations  0.64 us (2%)
    pallas_call x1, Pallas kernels, on_device(): pl.pallas_call(functools.partial(fused_kernel, pairs=pairs, window=window...  25.1 us
    squeeze x1, local copies, waits for them, and re-layouts, on_device(): return (result[0], result[1], result[2])  1.37 us

profile of v10, /device:TPU:161, one launch (start us, length us, event | category | flops | bytes accessed | tf_op | source)
XLA Modules:
  0.0 27.1 jit_solution(9231796490720636506)
XLA Ops:
  0.6 25.1 %shard_map.67 = f32[3,32,128]{2,1,0:T(8,128)} custom-call(s32[32,512]{1,0:T(8,128)} %mask_ref.1, f32[32,128]{1,0:T(8,128)} %q_ref.1, bf16[3072,64]{1,0:T(8,128)(2,1)} %bitcast.7, f32[24]{0:T(128)} %w_smem.1), custom_call_target="tpu_custom_call" | custom-call | flops 5435817984 | bytes 720896 | tf_op jit(solution)/shard_map/pallas_call | solution.py:290
  25.8 1.4 %slice_bitcast_fusion = (f32[32,128]{1,0:T(8,128)}, f32[32,128]{1,0:T(8,128)}, f32[32,128]{1,0:T(8,128)}) fusion(f32[3,32,128]{2,1,0:T(8,128)} %shard_map.67), kind=kLoop, calls=%fused_computation | loop fusion | bytes 98304 | tf_op jit(solution)/shard_map/squeeze | solution.py:315

commit v11 on v10

--- a/solution.py
+++ b/solution.py
@@ -80,34 +80,6 @@
             )
 
         count = count + here.astype(jnp.int32)
-    pl.semaphore_wait(barrier, count)
-
-    def rows_for(source, dt, whole):
-        height = source.shape[0]
-        if dt == 0 or (abs(dt) == 1 and whole):
-            return 0, height
-        return (height - HALO, HALO) if dt < 0 else (0, HALO)
-
-    plan = [(mask_ref, mask_slots, slot, offset, True) for slot, offset in enumerate(MASK_FROM)]
-    plan += [(q_ref, q_slots, slot, offset, False) for slot, offset in enumerate(QUENCH_FROM)]
-    copies = []
-    for index, (source, slots, slot, (dt, dq), whole) in enumerate(plan):
-        first, rows = rows_for(source, dt, whole)
-        copy = pltpu.make_async_remote_copy(
-            src_ref=source.at[pl.ds(first, rows)],
-            dst_ref=slots.at[slot, pl.ds(first, rows)],
-            send_sem=send_sems.at[index],
-            recv_sem=recv_sems.at[index],
-            device_id=device(-dt, -dq),
-            device_id_type=pl.DeviceIdType.MESH,
-        )
-
-        @pl.when(exists(-dt, -dq))
-        def _():
-            copy.start()
-
-        copies.append(copy)
-
     sel_lane = lax.broadcasted_iota(jnp.int32, (ambit, width * window), 1)
     sel_row = lax.broadcasted_iota(jnp.int32, (ambit, width * window), 0)
     selector = (sel_lane % window - sel_lane // window == sel_row).astype(jnp.bfloat16)
@@ -140,7 +112,36 @@
         )
         return carry
 
-    lax.fori_loop(0, groups, build, 0)
+    lax.fori_loop(0, groups // 2, build, 0)
+    pl.semaphore_wait(barrier, count)
+
+    def rows_for(source, dt, whole):
+        height = source.shape[0]
+        if dt == 0 or (abs(dt) == 1 and whole):
+            return 0, height
+        return (height - HALO, HALO) if dt < 0 else (0, HALO)
+
+    plan = [(mask_ref, mask_slots, slot, offset, True) for slot, offset in enumerate(MASK_FROM)]
+    plan += [(q_ref, q_slots, slot, offset, False) for slot, offset in enumerate(QUENCH_FROM)]
+    copies = []
+    for index, (source, slots, slot, (dt, dq), whole) in enumerate(plan):
+        first, rows = rows_for(source, dt, whole)
+        copy = pltpu.make_async_remote_copy(
+            src_ref=source.at[pl.ds(first, rows)],
+            dst_ref=slots.at[slot, pl.ds(first, rows)],
+            send_sem=send_sems.at[index],
+            recv_sem=recv_sems.at[index],
+            device_id=device(-dt, -dq),
+            device_id_type=pl.DeviceIdType.MESH,
+        )
+
+        @pl.when(exists(-dt, -dq))
+        def _():
+            copy.start()
+
+        copies.append(copy)
+
+    lax.fori_loop(groups // 2, groups, build, 0)
 
     def wait_for(kind):
         for copy, (source, slots, slot, (dt, dq), whole) in zip(copies, plan):
@@ -205,17 +206,17 @@
 
     def accumulate(group, carry):
         pieces = []
-        for offset in range(TAP_GROUP):
-            start = pl.multiple_of((group * TAP_GROUP + offset) * BLOCKS, BLOCKS)
+        for offset in range(32):
+            start = pl.multiple_of((group * 32 + offset) * BLOCKS, BLOCKS)
             pieces.append(win_ref[pl.ds(start, out_rows * BLOCKS), :].astype(jnp.bfloat16))
         left = jnp.concatenate(pieces, axis=1)
-        right = taps_ref[:, pl.ds(pl.multiple_of(group * span, span), span)]
+        right = taps_ref[:, pl.ds(pl.multiple_of(group * 32 * window, 32 * window), 32 * window)]
         acc_ref[...] += lax.dot_general(
             left, right, (((1,), (1,)), ((), ())), preferred_element_type=jnp.float32
         )
         return carry
 
-    lax.fori_loop(0, groups, accumulate, 0)
+    lax.fori_loop(0, ambit // 32, accumulate, 0)
 
     wait_for("quench")
     wait_for("send")

time: 27.3 us -> 25.7 us (0.941)
  the two profiles are of different devices: /device:TPU:161 before, /device:TPU:192 now
where the time goes in v11:
time: 25.7 us; the launch traced here: 25.5 us
  Pallas kernels  23.5 us (91%)
  local copies, waits for them, and re-layouts  1.37 us (5%)
  between operations  0.64 us (2%)
    pallas_call x1, Pallas kernels, on_device(): pl.pallas_call(functools.partial(fused_kernel, pairs=pairs, window=window...  23.5 us
    squeeze x1, local copies, waits for them, and re-layouts, on_device(): return (result[0], result[1], result[2])  1.37 us

profile of v11, /device:TPU:192, one launch (start us, length us, event | category | flops | bytes accessed | tf_op | source)
XLA Modules:
  0.0 25.5 jit_solution(3606839801660954137)
XLA Ops:
  0.6 23.5 %shard_map.67 = f32[3,32,128]{2,1,0:T(8,128)} custom-call(s32[32,512]{1,0:T(8,128)} %mask_ref.1, f32[32,128]{1,0:T(8,128)} %q_ref.1, bf16[3072,64]{1,0:T(8,128)(2,1)} %bitcast.7, f32[24]{0:T(128)} %w_smem.1), custom_call_target="tpu_custom_call" | custom-call | flops 5435817984 | bytes 720896 | tf_op jit(solution)/shard_map/pallas_call | solution.py:291
  24.1 1.4 %slice_bitcast_fusion = (f32[32,128]{1,0:T(8,128)}, f32[32,128]{1,0:T(8,128)}, f32[32,128]{1,0:T(8,128)}) fusion(f32[3,32,128]{2,1,0:T(8,128)} %shard_map.67), kind=kLoop, calls=%fused_computation | loop fusion | bytes 98304 | tf_op jit(solution)/shard_map/squeeze | solution.py:316

commit v12 on v11

--- a/solution.py
+++ b/solution.py
@@ -112,7 +112,7 @@
         )
         return carry
 
-    lax.fori_loop(0, groups // 2, build, 0)
+    lax.fori_loop(0, groups // 4, build, 0)
     pl.semaphore_wait(barrier, count)
 
     def rows_for(source, dt, whole):
@@ -141,7 +141,7 @@
 
         copies.append(copy)
 
-    lax.fori_loop(groups // 2, groups, build, 0)
+    lax.fori_loop(groups // 4, groups, build, 0)
 
     def wait_for(kind):
         for copy, (source, slots, slot, (dt, dq), whole) in zip(copies, plan):

time: 25.7 us -> 25 us (0.973)
  the two profiles are of different devices: /device:TPU:192 before, /device:TPU:120 now
where the time goes in v12:
time: 25 us; the launch traced here: 24.8 us
  Pallas kernels  22.8 us (91%)
  local copies, waits for them, and re-layouts  1.37 us (5%)
  between operations  0.64 us (3%)
    pallas_call x1, Pallas kernels, on_device(): pl.pallas_call(functools.partial(fused_kernel, pairs=pairs, window=window...  22.8 us
    squeeze x1, local copies, waits for them, and re-layouts, on_device(): return (result[0], result[1], result[2])  1.37 us

profile of v12, /device:TPU:120, one launch (start us, length us, event | category | flops | bytes accessed | tf_op | source)
XLA Modules:
  0.0 24.8 jit_solution(15429803680295491453)
XLA Ops:
  0.6 22.8 %shard_map.67 = f32[3,32,128]{2,1,0:T(8,128)} custom-call(s32[32,512]{1,0:T(8,128)} %mask_ref.1, f32[32,128]{1,0:T(8,128)} %q_ref.1, bf16[3072,64]{1,0:T(8,128)(2,1)} %bitcast.7, f32[24]{0:T(128)} %w_smem.1), custom_call_target="tpu_custom_call" | custom-call | flops 5435817984 | bytes 720896 | tf_op jit(solution)/shard_map/pallas_call | solution.py:291
  23.4 1.4 %slice_bitcast_fusion = (f32[32,128]{1,0:T(8,128)}, f32[32,128]{1,0:T(8,128)}, f32[32,128]{1,0:T(8,128)}) fusion(f32[3,32,128]{2,1,0:T(8,128)} %shard_map.67), kind=kLoop, calls=%fused_computation | loop fusion | bytes 98304 | tf_op jit(solution)/shard_map/squeeze | solution.py:316

commit v13 on v12

--- a/solution.py
+++ b/solution.py
@@ -15,7 +15,8 @@
 QUENCH_RATE = 0.5
 EXPOSURE = 0.35
 
-BLOCKS = 8
+BLOCKS = 9
+SHIFTS = 8
 HALO = STEPS
 TAP_GROUP = 8
 
@@ -46,6 +47,7 @@
     mask_ref, q_ref, k_ref, w_smem,
     o_ref,
     mask_slots, q_slots, send_sems, recv_sems, taps_ref, win_ref, acc_ref, red_ref, rows_ref,
+    shifted_ref,
     *, pairs, window, halo, width,
 ):
     tile = lax.axis_index("tile")
@@ -204,11 +206,19 @@
 
     acc_ref[...] = jnp.zeros_like(acc_ref)
 
+    height = win_ref.shape[0]
+    for shift in range(SHIFTS):
+        shifted_ref[shift, pl.ds(0, height - shift), :] = win_ref[pl.ds(shift, height - shift), :]
+
     def accumulate(group, carry):
         pieces = []
         for offset in range(32):
-            start = pl.multiple_of((group * 32 + offset) * BLOCKS, BLOCKS)
-            pieces.append(win_ref[pl.ds(start, out_rows * BLOCKS), :].astype(jnp.bfloat16))
+            start = pl.multiple_of(
+                (group * 32 + offset) * SHIFTS + (group * 32 + offset) // SHIFTS * SHIFTS, SHIFTS
+            )
+            pieces.append(
+                shifted_ref[offset % SHIFTS, pl.ds(start, out_rows * BLOCKS), :].astype(jnp.bfloat16)
+            )
         left = jnp.concatenate(pieces, axis=1)
         right = taps_ref[:, pl.ds(pl.multiple_of(group * 32 * window, 32 * window), 32 * window)]
         acc_ref[...] += lax.dot_general(
@@ -303,6 +313,7 @@
             pltpu.VMEM((m_rows, width * pairs), jnp.float32),
             pltpu.VMEM((m_rows, window), jnp.float32),
             pltpu.VMEM((pairs * ambit, ambit), jnp.float32),
+            pltpu.VMEM((SHIFTS, window_rows * BLOCKS, window), jnp.float32),
         ],
         compiler_params=pltpu.CompilerParams(
             collective_id=0, has_side_effects=True, vmem_limit_bytes=56 * 1024 * 1024

time: 25 us -> 24.2 us (0.968)
  Pallas kernels: 22.8 us -> 22.1 us
    pallas_call x1, Pallas kernels: 22.8 us -> 22.1 us  [on_device(): pl.pallas_call(functools.partial(fused_kernel, pairs=pairs, window=window...]
where the time goes in v13:
time: 24.2 us; the launch traced here: 24.1 us
  Pallas kernels  22.1 us (91%)
  local copies, waits for them, and re-layouts  1.37 us (6%)
  between operations  0.64 us (3%)
    pallas_call x1, Pallas kernels, on_device(): pl.pallas_call(functools.partial(fused_kernel, pairs=pairs, window=window...  22.1 us
    squeeze x1, local copies, waits for them, and re-layouts, on_device(): return (result[0], result[1], result[2])  1.37 us

profile of v13, /device:TPU:120, one launch (start us, length us, event | category | flops | bytes accessed | tf_op | source)
XLA Modules:
  0.0 24.1 jit_solution(8754205622389391657)
XLA Ops:
  0.6 22.1 %shard_map.67 = f32[3,32,128]{2,1,0:T(8,128)} custom-call(s32[32,512]{1,0:T(8,128)} %mask_ref.1, f32[32,128]{1,0:T(8,128)} %q_ref.1, bf16[3072,64]{1,0:T(8,128)(2,1)} %bitcast.7, f32[24]{0:T(128)} %w_smem.1), custom_call_target="tpu_custom_call" | custom-call | flops 5435817984 | bytes 720896 | tf_op jit(solution)/shard_map/pallas_call | solution.py:301
  22.7 1.4 %slice_bitcast_fusion = (f32[32,128]{1,0:T(8,128)}, f32[32,128]{1,0:T(8,128)}, f32[32,128]{1,0:T(8,128)}) fusion(f32[3,32,128]{2,1,0:T(8,128)} %shard_map.67), kind=kLoop, calls=%fused_computation | loop fusion | bytes 98304 | tf_op jit(solution)/shard_map/squeeze | solution.py:327

commit v14 on v13

--- a/solution.py
+++ b/solution.py
@@ -252,7 +252,7 @@
     field = acc_ref[...]
     weighted = field * field * lane_weights
     red_ref[...] = jnp.dot(
-        weighted, summer, precision=lax.Precision.HIGHEST,
+        weighted, summer, precision=lax.Precision.HIGH,
         preferred_element_type=jnp.float32,
     )
     intensity = jnp.zeros((out_rows, lanes), jnp.float32)

time: 24.2 us -> 23.7 us (0.979)
  Pallas kernels: 22.1 us -> 21.5 us
    pallas_call x1, Pallas kernels: 22.1 us -> 21.5 us  [on_device(): pl.pallas_call(functools.partial(fused_kernel, pairs=pairs, window=window...]
where the time goes in v14:
time: 23.7 us; the launch traced here: 23.5 us
  Pallas kernels  21.5 us (91%)
  local copies, waits for them, and re-layouts  1.37 us (6%)
  between operations  0.64 us (3%)
    pallas_call x1, Pallas kernels, on_device(): pl.pallas_call(functools.partial(fused_kernel, pairs=pairs, window=window...  21.5 us
    squeeze x1, local copies, waits for them, and re-layouts, on_device(): return (result[0], result[1], result[2])  1.37 us

profile of v14, /device:TPU:120, one launch (start us, length us, event | category | flops | bytes accessed | tf_op | source)
XLA Modules:
  0.0 23.5 jit_solution(14630534527133112613)
XLA Ops:
  0.6 21.5 %shard_map.67 = f32[3,32,128]{2,1,0:T(8,128)} custom-call(s32[32,512]{1,0:T(8,128)} %mask_ref.1, f32[32,128]{1,0:T(8,128)} %q_ref.1, bf16[3072,64]{1,0:T(8,128)(2,1)} %bitcast.7, f32[24]{0:T(128)} %w_smem.1), custom_call_target="tpu_custom_call" | custom-call | flops 5435817984 | bytes 720896 | tf_op jit(solution)/shard_map/pallas_call | solution.py:301
  22.1 1.4 %slice_bitcast_fusion = (f32[32,128]{1,0:T(8,128)}, f32[32,128]{1,0:T(8,128)}, f32[32,128]{1,0:T(8,128)}) fusion(f32[3,32,128]{2,1,0:T(8,128)} %shard_map.67), kind=kLoop, calls=%fused_computation | loop fusion | bytes 98304 | tf_op jit(solution)/shard_map/squeeze | solution.py:327

commit v15 on v14

--- a/solution.py
+++ b/solution.py
@@ -251,9 +251,11 @@
     ).astype(jnp.float32)
     field = acc_ref[...]
     weighted = field * field * lane_weights
-    red_ref[...] = jnp.dot(
-        weighted, summer, precision=lax.Precision.HIGH,
-        preferred_element_type=jnp.float32,
+    high = weighted.astype(jnp.bfloat16)
+    low = (weighted - high.astype(jnp.float32)).astype(jnp.bfloat16)
+    summer = summer.astype(jnp.bfloat16)
+    red_ref[...] = jnp.dot(high, summer, preferred_element_type=jnp.float32) + jnp.dot(
+        low, summer, preferred_element_type=jnp.float32
     )
     intensity = jnp.zeros((out_rows, lanes), jnp.float32)
     for block in range(BLOCKS):

time: 23.7 us -> 23.4 us (0.987)
  no operation moved by 1% of the time
where the time goes in v15:
time: 23.4 us; the launch traced here: 23.3 us
  Pallas kernels  21.3 us (91%)
  local copies, waits for them, and re-layouts  1.37 us (6%)
  between operations  0.64 us (3%)
    pallas_call x1, Pallas kernels, on_device(): pl.pallas_call(functools.partial(fused_kernel, pairs=pairs, window=window...  21.3 us
    squeeze x1, local copies, waits for them, and re-layouts, on_device(): return (result[0], result[1], result[2])  1.37 us

profile of v15, /device:TPU:120, one launch (start us, length us, event | category | flops | bytes accessed | tf_op | source)
XLA Modules:
  0.0 23.3 jit_solution(9973259513783152107)
XLA Ops:
  0.6 21.3 %shard_map.67 = f32[3,32,128]{2,1,0:T(8,128)} custom-call(s32[32,512]{1,0:T(8,128)} %mask_ref.1, f32[32,128]{1,0:T(8,128)} %q_ref.1, bf16[3072,64]{1,0:T(8,128)(2,1)} %bitcast.7, f32[24]{0:T(128)} %w_smem.1), custom_call_target="tpu_custom_call" | custom-call | flops 5435817984 | bytes 720896 | tf_op jit(solution)/shard_map/pallas_call | solution.py:303
  21.9 1.4 %slice_bitcast_fusion = (f32[32,128]{1,0:T(8,128)}, f32[32,128]{1,0:T(8,128)}, f32[32,128]{1,0:T(8,128)}) fusion(f32[3,32,128]{2,1,0:T(8,128)} %shard_map.67), kind=kLoop, calls=%fused_computation | loop fusion | bytes 98304 | tf_op jit(solution)/shard_map/squeeze | solution.py:329

commit v16 on v15

--- a/solution.py
+++ b/solution.py
@@ -183,7 +183,13 @@
     for block in range(BLOCKS):
         start = kern * local_cols - lead + width * block
         part = pltpu.roll(rows, lax.rem(total - start, total), 1)[:, :window]
-        win_ref[pl.ds(block, rows.shape[0], stride=BLOCKS), :] = part
+        for shift in range(SHIFTS):
+            if block >= shift:
+                shifted_ref[shift, pl.ds(block - shift, rows.shape[0], stride=BLOCKS), :] = part
+            else:
+                shifted_ref[
+                    shift, pl.ds(BLOCKS + block - shift, rows.shape[0] - 1, stride=BLOCKS), :
+                ] = part[1:]
 
     def band(left, middle, right):
         lane = lax.broadcasted_iota(jnp.int32, (middle.shape[0], lanes), 1)
@@ -204,11 +210,6 @@
             ),
         )
 
-    acc_ref[...] = jnp.zeros_like(acc_ref)
-
-    height = win_ref.shape[0]
-    for shift in range(SHIFTS):
-        shifted_ref[shift, pl.ds(0, height - shift), :] = win_ref[pl.ds(shift, height - shift), :]
 
     def accumulate(group, carry):
         pieces = []
@@ -221,12 +222,17 @@
             )
         left = jnp.concatenate(pieces, axis=1)
         right = taps_ref[:, pl.ds(pl.multiple_of(group * 32 * window, 32 * window), 32 * window)]
-        acc_ref[...] += lax.dot_general(
+        product = lax.dot_general(
             left, right, (((1,), (1,)), ((), ())), preferred_element_type=jnp.float32
         )
+        if group == 0:
+            acc_ref[...] = product
+        else:
+            acc_ref[...] += product
         return carry
 
-    lax.fori_loop(0, ambit // 32, accumulate, 0)
+    for group in range(ambit // 32):
+        accumulate(group, 0)
 
     wait_for("quench")
     wait_for("send")

time: 23.4 us -> 23.1 us (0.987)
  Pallas kernels: 21.3 us -> 21 us
    pallas_call x1, Pallas kernels: 21.3 us -> 21 us  [on_device(): pl.pallas_call(functools.partial(fused_kernel, pairs=pairs, window=window...]
where the time goes in v16:
time: 23.1 us; the launch traced here: 23 us
  Pallas kernels  21 us (91%)
  local copies, waits for them, and re-layouts  1.37 us (6%)
  between operations  0.64 us (3%)
    pallas_call x1, Pallas kernels, on_device(): pl.pallas_call(functools.partial(fused_kernel, pairs=pairs, window=window...  21 us
    squeeze x1, local copies, waits for them, and re-layouts, on_device(): return (result[0], result[1], result[2])  1.37 us

profile of v16, /device:TPU:120, one launch (start us, length us, event | category | flops | bytes accessed | tf_op | source)
XLA Modules:
  0.0 23.0 jit_solution(6578257487909763617)
XLA Ops:
  0.6 21.0 %shard_map.67 = f32[3,32,128]{2,1,0:T(8,128)} custom-call(s32[32,512]{1,0:T(8,128)} %mask_ref.1, f32[32,128]{1,0:T(8,128)} %q_ref.1, bf16[3072,64]{1,0:T(8,128)(2,1)} %bitcast.7, f32[24]{0:T(128)} %w_smem.1), custom_call_target="tpu_custom_call" | custom-call | flops 5435817984 | bytes 720896 | tf_op jit(solution)/shard_map/pallas_call | solution.py:309
  21.6 1.4 %slice_bitcast_fusion = (f32[32,128]{1,0:T(8,128)}, f32[32,128]{1,0:T(8,128)}, f32[32,128]{1,0:T(8,128)}) fusion(f32[3,32,128]{2,1,0:T(8,128)} %shard_map.67), kind=kLoop, calls=%fused_computation | loop fusion | bytes 98304 | tf_op jit(solution)/shard_map/squeeze | solution.py:335
